TPU v7x, 128 devices: a whole 4x4x4 slice. The times are simulated.
128 devices in a mesh: wide: 16 (over y, z), narrow: 8 (over x, core).
Axes of the slice: x: 4, y: 4, z: 4, core: 2. Of those that a mesh axis runs over, the one named last changes fastest.
Arguments:
- adjoint: float32 [3, 512, 256, 256], P(None, 'wide', 'narrow'), may hold values from -6 to 6
- velocity: float32 [3, 512, 256, 256], P(None, 'wide', 'narrow'), may hold values from -6 to 6
- deriv_x: float32 [256, 256], replicated, as said below
- deriv_y: float32 [256, 256], replicated, as said below
- deriv_z: float32 [512, 512], replicated, as said below
- rotor_blocks: int32 [96, 64], replicated, may hold values from 0 to 262143, as said below
- turbine_owner: int32 [96], replicated, may hold values from 0 to 127, as said below
- disk_weight: float32 [96, 64, 128], replicated, may hold values from 0.1 to 1
- thrust: float32 [96], replicated, may hold values from 0.5 to 2
Outputs:
- updated_adjoint: float32 [3, 512, 256, 256], P(None, 'wide', 'narrow')
- turbine_grad: float32 [256, 2], P(('wide', 'narrow'))
Inputs may be any that keep to these rules, and one draw needn't show every extreme that they name: `deriv_x`: entries vanish where the row's block of 64 and the column's block differ by more than one. `deriv_y`: entries vanish where the row's block of 32 and the column's block differ by more than one. `deriv_z`: entries vanish where the row's block of 16 and the column's block differ by more than one. `rotor_blocks`: block id b = (z * 256 + y) * 2 + x block. A rotor's row lists 64 // 2 consecutive z planes times 2 consecutive y lines, all at one x block, z major. `turbine_owner`: devices are numbered wide major over wide and narrow. No device owns more than 2 turbines, and one owns exactly 2.
All inputs are finite; a program needn't handle non-finite values.
Results may differ from a plain program's by a relative error of at most 0.00014.
Values sent between devices are 32-bit elements; how exact they have to be, the bound alone decides.
No kernel may reach another device: no remote copies, remote signals or barrier semaphores. Data moves between devices by JAX's collectives and lax.ppermute only.
A program may use at most 192 MiB of HBM per device.

v0:
```python
import math

import jax
import jax.numpy as jnp
from jax import lax
from jax.sharding import PartitionSpec as P

NY = 256


def directional(adjoint, velocity, adj_deriv, vel_deriv, direction):
    advect = velocity[direction][None] * adj_deriv
    stretch = -jnp.sum(adjoint * vel_deriv, axis=0)
    select = (jnp.arange(3) == direction).astype(jnp.float32)[:, None, None, None]
    return advect + select * stretch[None]


def turbine_terms(adjoint, velocity, rotor_blocks, disk_weight, thrust):
    shard_z = adjoint.shape[1]
    shard_y = adjoint.shape[2]
    x_blocks = adjoint.shape[3] // 128
    line_id = rotor_blocks // x_blocks
    block_x = rotor_blocks % x_blocks
    row_y = line_id % NY
    row_z = line_id // NY
    first_z = lax.axis_index("wide") * shard_z
    first_y = lax.axis_index("narrow") * shard_y
    is_local = (
        (row_z >= first_z)
        & (row_z < first_z + shard_z)
        & (row_y >= first_y)
        & (row_y < first_y + shard_y)
    )
    row_index = jnp.where(
        is_local, ((row_z - first_z) * shard_y + row_y - first_y) * x_blocks + block_x, 0
    )
    ax_rows = adjoint[0].reshape(-1, 128)[row_index]
    ay_rows = adjoint[1].reshape(-1, 128)[row_index]
    ux_rows = velocity[0].reshape(-1, 128)[row_index]
    weight = jnp.where(is_local[:, :, None], disk_weight, 0.0)
    thrust_drive = ux_rows * jnp.abs(ux_rows)
    scale = 1.0 / math.sqrt(128.0 * rotor_blocks.shape[1])
    grad_thrust = jnp.sum(weight * ax_rows * thrust_drive, axis=(1, 2)) * scale
    grad_side = jnp.sum(weight * ay_rows * thrust_drive, axis=(1, 2)) * scale
    partial_value = jnp.stack([grad_thrust, grad_side], axis=1)
    weighted = (weight * thrust[:, None, None]).reshape(-1, 128)
    source = jnp.zeros((shard_z * shard_y * x_blocks, 128), jnp.float32)
    source = source.at[row_index.reshape(-1)].add(weighted).reshape(adjoint.shape[1:])
    return (partial_value, source)


def on_device(
    adjoint, velocity, deriv_x, deriv_y, deriv_z, rotor_blocks, turbine_owner, disk_weight, thrust
):
    highest = lax.Precision.HIGHEST
    adj_dx = jnp.einsum("czyk,xk->czyx", adjoint, deriv_x, precision=highest)
    vel_dx = jnp.einsum("czyk,xk->czyx", velocity, deriv_x, precision=highest)
    part_x = directional(adjoint, velocity, adj_dx, vel_dx, 0)
    rows_adj, rows_vel = (
        lax.all_to_all(adjoint, "narrow", split_axis=3, concat_axis=2, tiled=True),
        lax.all_to_all(velocity, "narrow", split_axis=3, concat_axis=2, tiled=True),
    )
    adj_dy = jnp.einsum("czkx,yk->czyx", rows_adj, deriv_y, precision=highest)
    vel_dy = jnp.einsum("czkx,yk->czyx", rows_vel, deriv_y, precision=highest)
    part_y = directional(rows_adj, rows_vel, adj_dy, vel_dy, 1)
    returned_rows = lax.all_to_all(part_y, "narrow", split_axis=2, concat_axis=3, tiled=True)
    cols_adj, cols_vel = (
        lax.all_to_all(adjoint, "wide", split_axis=3, concat_axis=1, tiled=True),
        lax.all_to_all(velocity, "wide", split_axis=3, concat_axis=1, tiled=True),
    )
    col_shape = cols_adj.shape
    flat_adj = cols_adj.reshape(3, col_shape[1], -1)
    flat_vel = cols_vel.reshape(3, col_shape[1], -1)
    adj_dz = jnp.einsum("ckm,zk->czm", flat_adj, deriv_z, precision=highest).reshape(col_shape)
    vel_dz = jnp.einsum("ckm,zk->czm", flat_vel, deriv_z, precision=highest).reshape(col_shape)
    part_z = directional(cols_adj, cols_vel, adj_dz, vel_dz, 2)
    vertical_term = lax.all_to_all(part_z, "wide", split_axis=1, concat_axis=3, tiled=True)
    partial_value, source = turbine_terms(adjoint, velocity, rotor_blocks, disk_weight, thrust)
    forcing = source * jnp.abs(velocity[0]) * adjoint[0]
    select = (jnp.arange(3) == 0).astype(jnp.float32)[:, None, None, None]
    tendency = part_x + returned_rows + vertical_term - select * forcing[None]
    updated = adjoint + 0.2 * tendency
    turbines = turbine_owner.shape[0]
    devices = lax.axis_size("wide") * lax.axis_size("narrow")
    slot_count = (turbines - 2) // devices + 2
    positions = jnp.arange(turbines)
    shared = turbine_owner[:, None] == turbine_owner[None, :]
    earlier = positions[:, None] > positions[None, :]
    slot_rank = jnp.sum((shared & earlier).astype(jnp.int32), axis=1)
    target_slot = turbine_owner * slot_count + slot_rank
    onehot = (jnp.arange(devices * slot_count)[:, None] == target_slot[None, :]).astype(jnp.float32)
    owner_term = jnp.dot(
        onehot, partial_value, precision=highest, preferred_element_type=jnp.float32
    )
    owner_share = lax.psum_scatter(owner_term, ("wide", "narrow"), scatter_dimension=0, tiled=True)
    return (updated, owner_share)


def solution(mesh):
    return jax.shard_map(
        on_device,
        mesh=mesh,
        in_specs=(
            P(None, "wide", "narrow", None),
            P(None, "wide", "narrow", None),
            P(),
            P(),
            P(),
            P(),
            P(),
            P(),
            P(),
        ),
        out_specs=(P(None, "wide", "narrow", None), P(("wide", "narrow"), None)),
        check_vma=False,
    )
```

profile of v0, /device:TPU:2, one launch (start us, length us, event | category | flops | bytes accessed | tf_op | source)
XLA Modules:
  0.0 851.3 jit_solution(10227270723661208699)
XLA Ops:
  0.6 11.5 %copy.128 = f32[3,32,32,256]{2,1,0,3:T(8,128)} copy(f32[3,32,32,256]{3,2,1,0:T(8,128)} %param.9) | data formatting | bytes 6291456 | tf_op args[0]
  12.2 10.6 %reshape.169 = f32[8,1,98304]{2,1,0:T(1,128)} reshape(f32[256,3,32,32]{3,2,1,0:T(8,128)} %bitcast.125) | data formatting | bytes 6291456
  22.8 4.8 all-to-all-start.1
  27.6 11.5 %copy.126 = f32[3,32,32,256]{2,1,0,3:T(8,128)} copy(f32[3,32,32,256]{3,2,1,0:T(8,128)} %param.10) | data formatting | bytes 6291456 | tf_op args[1]
  39.1 10.6 %reshape.171 = f32[8,1,98304]{2,1,0:T(1,128)} reshape(f32[256,3,32,32]{3,2,1,0:T(8,128)} %bitcast.127) | data formatting | bytes 6291456
  49.8 14.9 %all-to-all-done.1 = f32[8,1,98304]{2,1,0:T(1,128)} async-done(((f32[8,1,98304]{2,1,0:T(1,128)}), f32[8,1,98304]{2,1,0:T(1,128)}, u32[]{:S(2)}, u32[]{:S(2)}) %all-to-all-start.1) | async-done | bytes 3145760 | tf_op jit(solution)/shard_map/all_to_all | solution.py:60
  64.7 5.8 all-to-all-start
  70.6 14.2 %reshape.165 = f32[16,1,49152]{2,1,0:T(1,128)} reshape(f32[256,3,32,32]{3,2,1,0:T(8,128)} %bitcast.128) | data formatting | bytes 6291456
  84.7 23.0 %all-to-all-done = f32[8,1,98304]{2,1,0:T(1,128)} async-done(((f32[8,1,98304]{2,1,0:T(1,128)}), f32[8,1,98304]{2,1,0:T(1,128)}, u32[]{:S(2)}, u32[]{:S(2)}) %all-to-all-start) | async-done | bytes 3145760 | tf_op jit(solution)/shard_map/all_to_all | solution.py:61
  107.7 8.2 all-to-all-start.3
  115.8 14.1 %reshape.163 = f32[16,1,49152]{2,1,0:T(1,128)} reshape(f32[256,3,32,32]{3,2,1,0:T(8,128)} %bitcast.126) | data formatting | bytes 6291456
  130.0 28.7 %all-to-all-done.3 = f32[16,1,49152]{2,1,0:T(1,128)} async-done(((f32[16,1,49152]{2,1,0:T(1,128)}), f32[16,1,49152]{2,1,0:T(1,128)}, u32[]{:S(2)}, u32[]{:S(2)}) %all-to-all-start.3) | async-done | bytes 3145760 | tf_op jit(solution)/shard_map/all_to_all | solution.py:69
  158.7 6.0 all-to-all-start.4
  171.9 20.9 %gather_fusion = f32[6144,128]{1,0:T(8,128)} fusion(f32[2048,128]{1,0:T(8,128)S(1)} %reshape_squeeze.9, s32[6144]{0:T(1024)S(1)} %broadcast_clamp_fusion), kind=kCustom, calls=%fused_computation | custom fusion | bytes 6316032 | tf_op jit(solution)/shard_map/gather | solution.py:37
  192.8 20.9 %gather_fusion.1 = f32[6144,128]{1,0:T(8,128)} fusion(f32[2048,128]{1,0:T(8,128)S(1)} %reshape_squeeze.10, s32[6144]{0:T(1024)S(1)} %broadcast_clamp_fusion), kind=kCustom, calls=%fused_computation.1 | custom fusion | bytes 6316032 | tf_op jit(solution)/shard_map/gather | solution.py:39
  215.0 20.9 %gather_fusion.2 = f32[6144,128]{1,0:T(8,128)} fusion(f32[2048,128]{1,0:T(8,128)S(1)} %reshape_squeeze.11, s32[6144]{0:T(1024)S(1)} %broadcast_clamp_fusion), kind=kCustom, calls=%fused_computation.2 | custom fusion | bytes 6316032 | tf_op jit(solution)/shard_map/gather | solution.py:38
  236.8 9.1 %multiply_reduce_fusion.2 = (f32[96]{0:T(128)}, f32[96]{0:T(128)}, f32[96,64,128]{2,1,0:T(8,128)}) fusion(f32[96,64,128]{2,1,0:T(8,128)} %bitcast.143, f32[96,64,128]{2,1,0:T(8,128)} %bitcast.144, f32[96,64,128]{2,1,0:T(8,128)} %param.16, pred[96,64]{1,0:T(8,128)(4,1)S(1)} %copy.150, f32[96,64,128]{2,1,0:T(8,128)} %bitcast.145, f32[96]{0:T(128)S(1)} %copy-done.11), kind=kLoop, calls=%fused_computation.15 | loop fusion | flops 7864128 | bytes 15735936 | tf_op jit(solution)/shard_map/reduce_sum | solution.py:43
  246.5 11.7 %reduce.5 = f32[8,98304]{1,0:T(8,128)} reduce(f32[8,1,98304]{2,1,0:T(1,128)} %all-to-all-done, f32[]{:T(128)} %broadcast.137), dimensions={1}, to_apply=%all_to_all.74.reduce_sub_computation | reduce | bytes 6291460 | tf_op jit(solution)/shard_map/all_to_all | solution.py:61
  258.2 10.8 %reshape.172 = f32[256,3,32,32]{3,2,1,0:T(8,128)} reshape(f32[8,98304]{1,0:T(8,128)} %reduce.5) | data formatting | bytes 6291456
  269.1 16.4 %copy.168 = f32[3,32,32,8,32]{2,3,4,1,0:T(8,128)} copy(f32[3,32,32,8,32]{2,1,0,4,3:T(8,128)} %bitcast.132) | data formatting | bytes 6291456 | tf_op jit(solution)/shard_map/all_to_all | solution.py:61
  285.5 9.7 %all_to_all.81 = f32[3,32,256,32]{2,3,1,0:T(8,128)} reshape(f32[3,32,8,32,32]{3,2,4,1,0:T(8,128)} %bitcast.129) | data formatting | bytes 6291456 | tf_op jit(solution)/shard_map/all_to_all | solution.py:61
  295.3 4.6 slice.31
  299.9 11.8 %reduce.4 = f32[8,98304]{1,0:T(8,128)} reduce(f32[8,1,98304]{2,1,0:T(1,128)} %all-to-all-done.1, f32[]{:T(128)} %broadcast.137), dimensions={1}, to_apply=%all_to_all.77.reduce_sub_computation | reduce | bytes 6291460 | tf_op jit(solution)/shard_map/all_to_all | solution.py:60
  311.7 10.9 %reshape.170 = f32[256,3,32,32]{3,2,1,0:T(8,128)} reshape(f32[8,98304]{1,0:T(8,128)} %reduce.4) | data formatting | bytes 6291456
  322.6 16.3 %copy.167 = f32[3,32,32,8,32]{2,3,4,1,0:T(8,128)} copy(f32[3,32,32,8,32]{2,1,0,4,3:T(8,128)} %bitcast.133) | data formatting | bytes 6291456 | tf_op jit(solution)/shard_map/all_to_all | solution.py:60
  338.9 9.6 %all_to_all.80 = f32[3,32,256,32]{2,3,1,0:T(8,128)} reshape(f32[3,32,8,32,32]{3,2,4,1,0:T(8,128)} %bitcast.134) | data formatting | bytes 6291456 | tf_op jit(solution)/shard_map/all_to_all | solution.py:60
  348.5 5.7 fusion
  354.2 3.5 mul.186
  357.8 6.3 fusion.1
  364.1 11.4 %copy.130 = f32[3,32,256,32]{3,1,0,2:T(8,128)} copy(f32[3,32,256,32]{2,3,1,0:T(8,128)} %fusion.1) | data formatting | bytes 6291456 | tf_op jit(solution)/shard_map/add | solution.py:15
  375.5 10.6 %reshape.173 = f32[8,1,98304]{2,1,0:T(1,128)} reshape(f32[256,3,32,32]{3,2,1,0:T(8,128)} %bitcast.139) | data formatting | bytes 6291456
  386.1 11.8 %reduce.2 = f32[16,49152]{1,0:T(8,128)} reduce(f32[16,1,49152]{2,1,0:T(1,128)} %all-to-all-done.3, f32[]{:T(128)} %broadcast.137), dimensions={1}, to_apply=%all_to_all.86.reduce_sub_computation | reduce | bytes 6291460 | tf_op jit(solution)/shard_map/all_to_all | solution.py:69
  397.9 12.5 %reshape.166 = f32[256,3,32,32]{3,2,1,0:T(8,128)} reshape(f32[16,49152]{1,0:T(8,128)} %reduce.2) | data formatting | bytes 6291456
  410.5 16.4 %copy.133 = f32[3,32,32,256]{2,3,1,0:T(8,128)} copy(f32[3,32,32,256]{2,1,0,3:T(8,128)} %bitcast.123) | data formatting | bytes 6291456 | tf_op jit(solution)/shard_map/all_to_all | solution.py:69
  426.9 14.4 %copy.140 = f32[3,16,32,32,16]{2,1,4,3,0:T(8,128)} copy(f32[3,16,32,32,16]{3,2,0,4,1:T(8,128)} %bitcast.124) | data formatting | bytes 6291456 | tf_op jit(solution)/shard_map/all_to_all | solution.py:69
  441.3 10.0 %reshape.115 = f32[3,512,512]{1,2,0:T(8,128)} reshape(f32[3,16,32,32,16]{2,1,4,3,0:T(8,128)} %copy.140) | data formatting | bytes 6291456 | tf_op jit(solution)/shard_map/reshape | solution.py:73
  451.3 5.8 all-to-all-start.2
  457.1 8.0 convolution_bitcast_fusion
  465.1 3.6 copy.142
  468.6 8.5 %reshape.116 = f32[3,16,32,32,16]{2,1,4,3,0:T(8,128)} reshape(f32[3,512,512]{1,2,0:T(8,128)} %copy.142) | data formatting | bytes 6291456 | tf_op jit(solution)/shard_map/reshape | solution.py:75
  477.2 17.5 %copy.143 = f32[3,16,32,32,16]{3,4,1,2,0:T(8,128)} copy(f32[3,16,32,32,16]{2,1,4,3,0:T(8,128)} %reshape.116) | data formatting | bytes 6291456 | tf_op jit(solution)/shard_map/reshape | solution.py:75
  494.7 11.8 %reduce.1 = f32[16,49152]{1,0:T(8,128)} reduce(f32[16,1,49152]{2,1,0:T(1,128)} %all-to-all-done.4, f32[]{:T(128)} %broadcast.137), dimensions={1}, to_apply=%all_to_all.89.reduce_sub_computation | reduce | bytes 6291460 | tf_op jit(solution)/shard_map/all_to_all | solution.py:68
  506.5 12.3 %reshape.164 = f32[256,3,32,32]{3,2,1,0:T(8,128)} reshape(f32[16,49152]{1,0:T(8,128)} %reduce.1) | data formatting | bytes 6291456
  518.8 16.3 %copy.137 = f32[3,32,32,256]{2,3,1,0:T(8,128)} copy(f32[3,32,32,256]{2,1,0,3:T(8,128)} %bitcast.121) | data formatting | bytes 6291456 | tf_op jit(solution)/shard_map/all_to_all | solution.py:68
  535.1 9.7 %multiply_reduce_fusion = f32[16,32,32,16]{2,3,0,1:T(8,128)S(1)} fusion(f32[3,16,32,32,16]{3,4,1,2,0:T(8,128)} %bitcast.131, f32[3,16,32,32,16]{3,4,1,2,0:T(8,128)} %copy.143), kind=kLoop, calls=%fused_computation.8 | loop fusion | flops 1310720 | bytes 7340032 | tf_op jit(solution)/shard_map/reduce_sum | solution.py:13
  547.6 14.4 %copy.138 = f32[3,16,32,32,16]{2,1,4,3,0:T(8,128)} copy(f32[3,16,32,32,16]{3,2,0,4,1:T(8,128)} %bitcast.122) | data formatting | bytes 6291456 | tf_op jit(solution)/shard_map/all_to_all | solution.py:68
  562.0 9.9 %reshape.113 = f32[3,512,512]{1,2,0:T(8,128)} reshape(f32[3,16,32,32,16]{2,1,4,3,0:T(8,128)} %copy.138) | data formatting | bytes 6291456 | tf_op jit(solution)/shard_map/reshape | solution.py:72
  572.0 8.4 fusion.3
  580.4 10.3 %copy.139 = f32[3,512,32,16]{2,3,0,1:T(8,128)} copy(f32[3,512,32,16]{1,3,2,0:T(8,128)} %bitcast.146) | data formatting | bytes 6291456 | tf_op jit(solution)/shard_map/reshape | solution.py:74
  598.0 7.1 fusion.27
  605.0 14.1 %reshape.167 = f32[16,1,49152]{2,1,0:T(1,128)} reshape(f32[512,3,16,32]{3,2,1,0:T(8,128)} %fusion.27) | data formatting | bytes 6291456
  619.1 7.3 all-to-all-start.5
  626.5 43.4 %scatter_custom_fusion = f32[2048,128]{1,0:T(8,128)S(1)} fusion(s32[6144]{0:T(1024)S(1)} %bitcast.148, f32[6144,128]{1,0:T(8,128)} %bitcast.147, f32[]{:T(128)} %constant.62.clone.1), kind=kCustom, calls=%fused_computation.24 | custom fusion | flops 786432 | bytes 1049088 | tf_op jit(solution)/shard_map/scatter-add | solution.py:48
  671.2 5.7 multiply_reduce_fusion.3
  677.4 66.5 %all-reduce = f32[256,2]{1,0:T(8,128)} all-reduce(f32[256,2]{1,0:T(8,128)S(1)} %fusion.11), channel_id=2, replica_groups=mesh['wide'=16,'narrow'=8] {'wide','narrow'}, use_global_device_ids=true, to_apply=%region_7.8.clone | all-reduce | flops 512 | bytes 4096
  748.1 11.7 %reduce.6 = f32[8,98304]{1,0:T(8,128)} reduce(f32[8,1,98304]{2,1,0:T(1,128)} %all-to-all-done.2, f32[]{:T(128)} %broadcast.137), dimensions={1}, to_apply=%all_to_all.82.reduce_sub_computation | reduce | bytes 6291460 | tf_op jit(solution)/shard_map/all_to_all | solution.py:66
  759.8 10.8 %reshape.174 = f32[256,3,32,32]{3,2,1,0:T(8,128)} reshape(f32[8,98304]{1,0:T(8,128)} %reduce.6) | data formatting | bytes 6291456
  770.5 16.3 %copy.166 = f32[3,32,8,32,32]{4,2,3,1,0:T(8,128)} copy(f32[3,32,8,32,32]{4,1,0,3,2:T(8,128)} %bitcast.135) | data formatting | bytes 6291456 | tf_op jit(solution)/shard_map/all_to_all | solution.py:66
  786.9 9.8 %all_to_all.85 = f32[3,32,32,256]{3,2,1,0:T(8,128)} reshape(f32[3,32,32,8,32]{4,3,2,1,0:T(8,128)} %bitcast.136) | data formatting | bytes 6291456 | tf_op jit(solution)/shard_map/all_to_all | solution.py:66
  796.7 11.8 %reduce.3 = f32[16,49152]{1,0:T(8,128)} reduce(f32[16,1,49152]{2,1,0:T(1,128)} %all-to-all-done.5, f32[]{:T(128)} %broadcast.137), dimensions={1}, to_apply=%all_to_all.92.reduce_sub_computation | reduce | bytes 6291460 | tf_op jit(solution)/shard_map/all_to_all | solution.py:77
  808.6 12.3 %reshape.168 = f32[512,3,16,32]{3,2,1,0:T(8,128)} reshape(f32[16,49152]{1,0:T(8,128)} %reduce.3) | data formatting | bytes 6291456
  820.8 11.0 %copy.147 = f32[3,32,32,16,16]{2,4,3,1,0:T(8,128)} copy(f32[3,32,32,16,16]{2,4,0,1,3:T(8,128)} %bitcast.137) | data formatting | bytes 6291456 | tf_op jit(solution)/shard_map/all_to_all | solution.py:77
  831.8 9.2 %copy.148 = f32[3,32,32,256]{3,2,1,0:T(8,128)} copy(f32[3,32,32,256]{2,3,1,0:T(8,128)} %bitcast.138) | data formatting | bytes 6291456 | tf_op jit(solution)/shard_map/all_to_all | solution.py:77
  840.9 9.9 %multiply_add_fusion.1 = f32[3,32,32,256]{3,2,1,0:T(8,128)} fusion(f32[3,32,32,256]{3,2,1,0:T(8,128)} %param.9, f32[3,32,32,256]{3,2,1,0:T(8,128)} %copy.148, f32[3,32,32,256]{3,2,1,0:T(8,128)} %all_to_all.85, f32[32,32,256]{2,1,0:T(8,128)} %multiply_bitcast_fusion, f32[32,32,256]{2,1,0:T(8,128)S(1)} %neg.24, f32[3]{0:T(128)S(1)} %compare_convert_fusion.2, ...), kind=kOutput, calls=%fused_computation.16 | convolution fusion | flops 2422996992 | bytes 15990796 | tf_op jit(solution)/shard_map/czyk,xk->czyx/dot_general | solution.py:56
  (59 shorter events, 26.0 us)
Async XLA Ops:
  0.6 456.4 %copy-start = (f32[512,512]{1,0:T(8,128)S(1)}, f32[512,512]{1,0:T(8,128)}, u32[]{:S(2)}) copy-start(f32[512,512]{1,0:T(8,128)} %param.13) | copy-start | bytes 3145732
  22.8 41.9 %all-to-all-start.1 = ((f32[8,1,98304]{2,1,0:T(1,128)}), f32[8,1,98304]{2,1,0:T(1,128)}, u32[]{:S(2)}, u32[]{:S(2)}) async-start(f32[8,1,98304]{2,1,0:T(1,128)} %reshape.169), calls=%async_computation.1 | async-start | bytes 6291456 | tf_op jit(solution)/shard_map/all_to_all | solution.py:60
  64.7 42.9 %all-to-all-start = ((f32[8,1,98304]{2,1,0:T(1,128)}), f32[8,1,98304]{2,1,0:T(1,128)}, u32[]{:S(2)}, u32[]{:S(2)}) async-start(f32[8,1,98304]{2,1,0:T(1,128)} %reshape.171), calls=%async_computation | async-start | bytes 6291456 | tf_op jit(solution)/shard_map/all_to_all | solution.py:61
  107.7 51.0 %all-to-all-start.3 = ((f32[16,1,49152]{2,1,0:T(1,128)}), f32[16,1,49152]{2,1,0:T(1,128)}, u32[]{:S(2)}, u32[]{:S(2)}) async-start(f32[16,1,49152]{2,1,0:T(1,128)} %reshape.165), calls=%async_computation.3 | async-start | bytes 6291456 | tf_op jit(solution)/shard_map/all_to_all | solution.py:69
  130.0 34.7 %copy-start.8 = (s32[96,64]{0,1:T(8,128)S(1)}, s32[96,64]{0,1:T(8,128)}, u32[]{:S(2)}) copy-start(s32[96,64]{0,1:T(8,128)} %param.14) | copy-start | bytes 73732
  158.7 292.6 %all-to-all-start.4 = ((f32[16,1,49152]{2,1,0:T(1,128)}), f32[16,1,49152]{2,1,0:T(1,128)}, u32[]{:S(2)}, u32[]{:S(2)}) async-start(f32[16,1,49152]{2,1,0:T(1,128)} %reshape.163), calls=%async_computation.4 | async-start | bytes 6291456 | tf_op jit(solution)/shard_map/all_to_all | solution.py:68
  215.0 21.8 %copy-start.11 = (f32[96]{0:T(128)S(1)}, f32[96]{0:T(128)}, u32[]{:S(2)}) copy-start(f32[96]{0:T(128)} %param.17) | copy-start | bytes 1156
  338.9 9.6 %copy-start.5 = (f32[256,256]{1,0:T(8,128)S(1)}, f32[256,256]{1,0:T(8,128)}, u32[]{:S(2)}) copy-start(f32[256,256]{1,0:T(8,128)} %param.12) | copy-start | bytes 786436
  451.3 167.9 %all-to-all-start.2 = ((f32[8,1,98304]{2,1,0:T(1,128)}), f32[8,1,98304]{2,1,0:T(1,128)}, u32[]{:S(2)}, u32[]{:S(2)}) async-start(f32[8,1,98304]{2,1,0:T(1,128)} %reshape.173), calls=%async_computation.2 | async-start | bytes 6291456 | tf_op jit(solution)/shard_map/all_to_all | solution.py:66
  590.7 5.8 copy-start.1
  593.4 4.6 copy-start.2
  619.1 7.4 copy-start.7
  619.1 177.6 %all-to-all-start.5 = ((f32[16,1,49152]{2,1,0:T(1,128)}), f32[16,1,49152]{2,1,0:T(1,128)}, u32[]{:S(2)}, u32[]{:S(2)}) async-start(f32[16,1,49152]{2,1,0:T(1,128)} %reshape.167), calls=%async_computation.5 | async-start | bytes 6291456 | tf_op jit(solution)/shard_map/all_to_all | solution.py:77
  626.5 44.7 %copy-start.6 = (f32[256,256]{1,0:T(8,128)S(1)}, f32[256,256]{1,0:T(8,128)}, u32[]{:S(2)}) copy-start(f32[256,256]{1,0:T(8,128)} %param.11) | copy-start | bytes 786436
  671.2 5.8 copy-start.12
  671.2 6.0 copy-start.9
  671.2 6.0 copy-start.10
  676.9 68.3 %copy-start.4 = (f32[1,32,32,256]{3,2,1,0:T(8,128)S(1)}, f32[1,32,32,256]{3,2,1,0:T(8,128)}, u32[]{:S(2)}) copy-start(f32[1,32,32,256]{3,2,1,0:T(8,128)} %reshape.119) | copy-start | bytes 3145732
  831.8 9.2 %copy-start.3 = (f32[32,32,256]{2,1,0:T(8,128)S(1)}, f32[32,32,256]{2,1,0:T(8,128)}, u32[]{:S(2)}) copy-start(f32[32,32,256]{2,1,0:T(8,128)} %get-tuple-element.11) | copy-start | bytes 3145732
where the time goes:
time: 863 us; the launch traced here: 851 us
  local copies, waits for them, and re-layouts  491 us (57%)
  other arithmetic  144 us (17%)
  waiting for transfers between devices  66.6 us (8%)
  blocking collectives  66.5 us (8%)
  matrix products  44.1 us (5%)
  starting transfers between devices  37.9 us (4%)
    unnamed x41, local copies, waits for them, and re-layouts  172 us
    unnamed x1, blocking collectives  66.5 us
    scatter-add x1, other arithmetic, turbine_terms(): source.at[row_index.reshape(-1)].add(weighted).reshape(adjoint.shape[1:])  43.4 us
    all_to_all x3, local copies, waits for them, and re-layouts, on_device(): lax.all_to_all(adjoint, 'wide', split_axis=3, concat_axis=1, tiled=True)  31.3 us
    all_to_all x2, local copies, waits for them, and re-layouts, on_device(): lax.all_to_all(velocity, 'wide', split_axis=3, concat_axis=1, tiled=True)  30.8 us
    all_to_all x1, waiting for transfers between devices, on_device(): lax.all_to_all(velocity, 'wide', split_axis=3, concat_axis=1, tiled=True)  28.7 us
    all_to_all x2, local copies, waits for them, and re-layouts, on_device(): lax.all_to_all(part_y, 'narrow', split_axis=2, concat_axis=3, tiled=True)  26.2 us
    all_to_all x2, local copies, waits for them, and re-layouts, on_device(): lax.all_to_all(velocity, 'narrow', split_axis=3, concat_axis=2, tiled=True)  26.2 us
  transfers between devices with their start and end apart: 6, of which 3 were waited for; matrix products, arithmetic and copies ran while one was open for 67% of the time, Pallas kernels for 0%

commit v1 on v0

v1 whole, which is shorter than its diff:
```python
import math

import jax
import jax.numpy as jnp
from jax import lax
from jax.experimental import pallas as pl
from jax.experimental.pallas import tpu as pltpu
from jax.sharding import PartitionSpec as P

F32 = jnp.float32
BF16 = jnp.bfloat16
NX = 256
NY = 256
SZ = 32
SY = 32
HZ = 16
TURB = 96
STEP = 0.2
VMEM = pl.BlockSpec(memory_space=pltpu.VMEM)
SMEM = pl.BlockSpec(memory_space=pltpu.SMEM)
COST = pl.CostEstimate(flops=1, transcendentals=0, bytes_accessed=1)
PARAMS = pltpu.CompilerParams(vmem_limit_bytes=56 << 20)

DX, YL, YU, YD, ZL, ZH = 0, 1, 2, 3, 4, 5


def split(v):
    hi = v.astype(BF16)
    lo = (v - hi.astype(F32)).astype(BF16)
    return hi, lo


def dot(a, b):
    return lax.dot_general(a, b, (((1,), (0,)), ((), ())), preferred_element_type=F32)


def mix(k_hi, k_lo, v):
    hi, lo = split(v)
    return dot(k_hi, hi) + (dot(k_hi, lo) + dot(k_lo, hi))


def iota(axis):
    return lax.broadcasted_iota(jnp.int32, (256, 256), axis)


def prep_kernel(dx_ref, dy_ref, dz_ref, mats_ref):
    wide, narrow = lax.axis_index("wide"), lax.axis_index("narrow")
    row, col = iota(0), iota(1)
    hi, lo = split(dx_ref[...].T)
    mats_ref[2 * DX] = hi
    mats_ref[2 * DX + 1] = lo
    rows = split(dy_ref[pl.ds(pl.multiple_of(narrow * SY, SY), SY), :])
    spread = (lax.broadcasted_iota(jnp.int32, (256, SY), 0) % SY == lax.broadcasted_iota(jnp.int32, (256, SY), 1)).astype(BF16)
    same = row // SY == col // SY
    for at, shift in ((YL, 0), (YU, -1), (YD, 1)):
        chosen = (row == (narrow + shift) * SY + col % SY).astype(BF16)
        for half in range(2):
            wider = dot(dot(spread, rows[half]).astype(BF16), chosen)
            mats_ref[2 * at + half] = jnp.where(same, wider, 0.0).astype(BF16)
    rows = split(dz_ref[pl.ds(pl.multiple_of(wide * SZ, SZ), SZ), :])
    spread = (lax.broadcasted_iota(jnp.int32, (256, SZ), 0) // 8 == lax.broadcasted_iota(jnp.int32, (256, SZ), 1)).astype(BF16)
    same = row % 8 == col % 8
    source = lax.broadcasted_iota(jnp.int32, (512, 256), 0)
    plane = lax.broadcasted_iota(jnp.int32, (512, 256), 1) // 8
    halo = jnp.where(plane < HZ, plane - HZ, plane - HZ + SZ)
    for at, offset in ((ZL, plane), (ZH, halo)):
        chosen = (source == wide * SZ + offset).astype(BF16)
        for half in range(2):
            wider = dot(dot(spread, rows[half]).astype(BF16), chosen)
            mats_ref[2 * at + half] = jnp.where(same, wider, 0.0).astype(BF16)


def prep(deriv_x, deriv_y, deriv_z):
    return pl.pallas_call(
        prep_kernel,
        in_specs=[VMEM] * 3,
        out_specs=VMEM,
        out_shape=jax.ShapeDtypeStruct((12, 256, 256), BF16),
        compiler_params=PARAMS,
        cost_estimate=COST,
        name="prep",
    )(deriv_x, deriv_y, deriv_z)


def turbine_kernel(block_ref, thrust_ref, owner_ref, ax_ref, ay_ref, ux_ref, weight_ref, force_ref, grad_ref, ax, ay, ux, total, padded, g0, g1):
    wide, narrow = lax.axis_index("wide"), lax.axis_index("narrow")
    cells = SZ * SY
    for half in range(2):
        lanes = pl.ds(128 * half, 128)
        rows = pl.ds(cells * half, cells)
        ax[rows, :] = ax_ref[0, :, :, lanes].reshape(cells, 128)
        ay[rows, :] = ay_ref[0, :, :, lanes].reshape(cells, 128)
        ux[rows, :] = ux_ref[0, :, :, lanes].reshape(cells, 128)
    total[...] = jnp.zeros_like(total)
    padded[...] = jnp.zeros_like(padded)
    g0[...] = jnp.zeros_like(g0)
    g1[...] = jnp.zeros_like(g1)

    def turbine(t, _):
        block = block_ref[0, t]
        start_z = block // (2 * NY) - wide * SZ
        start_y = (block // 2) % NY - narrow * SY
        half = block % 2
        near = (start_z > -SZ) & (start_z < SZ) & (start_y > -2) & (start_y < SY)

        @pl.when(near)
        def _():
            padded[pl.ds(64, 64), :] = weight_ref[t]
            for line in range(2):
                y = start_y + line

                @pl.when((y >= 0) & (y < SY))
                def _():
                    w = padded[pl.ds(64 - 2 * start_z + line, SZ, stride=2), :]
                    rows = pl.ds(half * cells + y, SZ, stride=SY)
                    a, b, u = ax[rows, :], ay[rows, :], ux[rows, :]
                    size = jnp.abs(u)
                    drive = w * (u * size)
                    g0[pl.ds(t, 1), :] += jnp.sum(drive * a, axis=0, keepdims=True)
                    g1[pl.ds(t, 1), :] += jnp.sum(drive * b, axis=0, keepdims=True)
                    total[rows, :] += (thrust_ref[t] * w) * (size * a)

        return 0

    lax.fori_loop(0, TURB, turbine, 0)
    for half in range(2):
        force_ref[:, :, pl.ds(128 * half, 128)] = total[pl.ds(cells * half, cells), :].reshape(SZ, SY, 128)
    ones = jnp.ones((8, 128), F32)
    lanes_sum = lambda g: lax.dot_general(
        ones, g[...], (((1,), (1,)), ((), ())), precision=lax.Precision.HIGHEST, preferred_element_type=F32
    )
    row, col = lax.broadcasted_iota(jnp.int32, (128, 128), 0), lax.broadcasted_iota(jnp.int32, (128, 128), 1)
    owner = owner_ref[0:1, :]
    owner_col = jnp.sum(jnp.where(row == col, owner, 0), axis=1, keepdims=True)
    rank = jnp.sum(((owner_col == owner) & (row < col)).astype(jnp.int32), axis=0, keepdims=True)
    value = jnp.where(row % 2 == 0, lanes_sum(g0)[0:1], lanes_sum(g1)[0:1]) * (1.0 / math.sqrt(128.0 * 64.0))
    value = jnp.where((row < 4) & (rank == row // 2), value, 0.0)
    grad_ref[...] = lax.dot_general(
        (owner == row).astype(F32), value, (((1,), (1,)), ((), ())), precision=lax.Precision.HIGHEST, preferred_element_type=F32
    )


def turbines(rotor_blocks, thrust, owner, adjoint, velocity, weight):
    cells = SZ * SY
    part = lambda c: pl.BlockSpec((1, SZ, SY, NX), lambda i: (c, 0, 0, 0))
    whole = lambda *shape: pl.BlockSpec(shape, lambda i: (0,) * len(shape))
    return pl.pallas_call(
        turbine_kernel,
        grid=(1,),
        in_specs=[SMEM, SMEM, whole(8, 128), part(0), part(1), part(0), whole(TURB, 64, 128)],
        out_specs=[whole(SZ, SY, NX), whole(128, 128)],
        out_shape=[jax.ShapeDtypeStruct((SZ, SY, NX), F32), jax.ShapeDtypeStruct((128, 128), F32)],
        scratch_shapes=[pltpu.VMEM((2 * cells, 128), F32)] * 4 + [pltpu.VMEM((192, 128), F32)] + [pltpu.VMEM((128, 128), F32)] * 2,
        compiler_params=PARAMS,
        cost_estimate=COST,
        name="turbines",
    )(rotor_blocks, thrust, owner, adjoint, adjoint, velocity, weight)


def local_kernel(adj_ref, vel_ref, force_ref, mats_ref, out_ref):
    def lines(yb, _):
        at = pl.ds(pl.multiple_of(yb * 8, 8), 8)
        field = lambda ref, c: ref[c, :, at, :].reshape(256, 256)
        x_hi, x_lo, z_hi, z_lo = mats_ref[2 * DX], mats_ref[2 * DX + 1], mats_ref[2 * ZL], mats_ref[2 * ZL + 1]

        def both(v):
            hi, lo = split(v)
            return (
                dot(hi, x_hi) + (dot(lo, x_hi) + dot(hi, x_lo)),
                dot(z_hi, hi) + (dot(z_hi, lo) + dot(z_lo, hi)),
            )

        stretch_x = jnp.zeros((256, 256), F32)
        stretch_z = jnp.zeros((256, 256), F32)
        for c in range(3):
            dx, dz = both(field(vel_ref, c))
            a = field(adj_ref, c)
            stretch_x += a * dx
            stretch_z += a * dz
        for c in range(3):
            a = field(adj_ref, c)
            dx, dz = both(a)
            tend = field(vel_ref, 0) * dx + field(vel_ref, 2) * dz
            if c == 0:
                tend -= stretch_x + force_ref[:, at, :].reshape(256, 256)
            if c == 2:
                tend -= stretch_z
            out_ref[c, :, at, :] = (a + STEP * tend).reshape(SZ, 8, NX)
        return 0

    lax.fori_loop(0, SY // 8, lines, 0)

    def planes(zg, _):
        at = pl.ds(pl.multiple_of(zg * 8, 8), 8)
        field = lambda ref, c: ref[c, at, :, :].reshape(256, 256)
        y_hi, y_lo = mats_ref[2 * YL], mats_ref[2 * YL + 1]
        stretch = jnp.zeros((256, 256), F32)
        for c in range(3):
            stretch += field(adj_ref, c) * mix(y_hi, y_lo, field(vel_ref, c))
        for c in range(3):
            tend = field(vel_ref, 1) * mix(y_hi, y_lo, field(adj_ref, c))
            if c == 1:
                tend -= stretch
            out_ref[c, at, :, :] = (field(out_ref, c) + STEP * tend).reshape(8, SY, NX)
        return 0

    lax.fori_loop(0, SZ // 8, planes, 0)


def local(adjoint, velocity, force, mats):
    return pl.pallas_call(
        local_kernel,
        in_specs=[VMEM] * 4,
        out_specs=VMEM,
        out_shape=jax.ShapeDtypeStruct(adjoint.shape, F32),
        compiler_params=PARAMS,
        cost_estimate=COST,
        name="local",
    )(adjoint, velocity, force, mats)


def field(ref, c):
    return ref[c].reshape(256, 256)


def adj_kernel(vel_ref, up_ref, down_ref, k_ref, old_ref, out_ref):
    for c in range(3):
        deriv = pair(up_ref, down_ref, c, k_ref)
        out_ref[c] = (field(old_ref, c) + STEP * (field(vel_ref, 0) * deriv)).reshape(out_ref.shape[1:])


def vel_kernel(adj_ref, up_ref, down_ref, k_ref, old_ref, out_ref):
    stretch = jnp.zeros((256, 256), F32)
    for c in range(3):
        stretch += field(adj_ref, c) * pair(up_ref, down_ref, c, k_ref)
    out_ref[0] = (field(old_ref, 0) - STEP * stretch).reshape(out_ref.shape[1:])


def pair(up_ref, down_ref, c, k_ref):
    if k_ref.shape[0] == 2:
        return mix(k_ref[0], k_ref[1], jnp.concatenate([up_ref[c].reshape(128, 256), down_ref[c].reshape(128, 256)], axis=0))
    return mix(k_ref[0], k_ref[1], field(up_ref, c)) + mix(k_ref[2], k_ref[3], field(down_ref, c))


def halo(axis, kind, other, up, down, mats, old):
    at = {"y": 1, "z": 2}[axis]
    n_other, at_other, n_old, at_old = (1, at, 3, 0) if kind == "adj" else (3, 0, 1, at)
    if axis == "y":
        block = lambda n, c: pl.BlockSpec((n, 8, SY, NX), lambda i: (c, i, 0, 0))
        side, mat = block(3, 0), pl.BlockSpec((4, 256, 256), lambda i: (YU // 2, 0, 0))
    else:
        block = lambda n, c: pl.BlockSpec((n, SZ, 8, NX), lambda i: (c, 0, i, 0))
        side, mat = pl.BlockSpec((3, HZ, 8, NX), lambda i: (0, 0, i, 0)), pl.BlockSpec((2, 256, 256), lambda i: (ZH, 0, 0))
    return pl.pallas_call(
        adj_kernel if kind == "adj" else vel_kernel,
        grid=(4,),
        in_specs=[block(n_other, at_other), side, side, mat, block(n_old, at_old)],
        out_specs=block(n_old, at_old),
        out_shape=jax.ShapeDtypeStruct(old.shape, F32),
        input_output_aliases={4: 0},
        compiler_params=PARAMS,
        cost_estimate=COST,
        name=axis + "_" + kind,
    )(other, up, down, mats, old)


def on_device(adjoint, velocity, deriv_x, deriv_y, deriv_z, rotor_blocks, turbine_owner, disk_weight, thrust):
    n_wide, n_narrow = lax.axis_size("wide"), lax.axis_size("narrow")
    up = lambda v, axis, n: lax.ppermute(v, axis, [(i, i + 1) for i in range(n - 1)])
    down = lambda v, axis, n: lax.ppermute(v, axis, [(i + 1, i) for i in range(n - 1)])
    def exchange(v):
        return (
            up(v, "narrow", n_narrow),
            down(v, "narrow", n_narrow),
            up(v[:, HZ:], "wide", n_wide),
            down(v[:, :HZ], "wide", n_wide),
        )

    sides = exchange(adjoint)
    owner = jnp.broadcast_to(jnp.pad(turbine_owner, (0, 128 - TURB), constant_values=-1)[None], (8, 128))
    mats = prep(deriv_x, deriv_y, deriv_z)
    force, grad = turbines(rotor_blocks.T, thrust, owner, adjoint, velocity, disk_weight)
    grad = lax.all_to_all(grad.reshape(n_wide, n_narrow, 128), "wide", split_axis=0, concat_axis=0, tiled=True)
    out = local(adjoint, velocity, force, mats)
    out, grad, velocity, *sides = lax.optimization_barrier((out, grad, velocity, *sides))

    vel_sides = exchange(velocity)
    grad = jnp.sum(grad, axis=0)
    grad = lax.all_to_all(grad.reshape(n_narrow, 1, 128), "narrow", split_axis=0, concat_axis=0, tiled=True)
    out = halo("y", "adj", velocity, sides[0], sides[1], mats, out)
    out = halo("z", "adj", velocity, sides[2], sides[3], mats, out)
    out, grad, *sides = lax.optimization_barrier((out, grad, *vel_sides))

    share = jnp.sum(grad, axis=(0, 1))[:4].reshape(2, 2)
    out = halo("y", "vel", adjoint, sides[0], sides[1], mats, out)
    out = halo("z", "vel", adjoint, sides[2], sides[3], mats, out)
    return out, share


def solution(mesh):
    field = P(None, "wide", "narrow", None)
    return jax.shard_map(
        on_device,
        mesh=mesh,
        in_specs=(field, field) + (P(),) * 7,
        out_specs=(field, P(("wide", "narrow"), None)),
        check_vma=False,
    )
```

time: 863 us -> 124 us (0.14)
  the two profiles are of different devices: /device:TPU:2 before, /device:TPU:11 now
where the time goes in v1:
time: 124 us; the launch traced here: 123 us
  Pallas kernels  52.7 us (42%)
  starting transfers between devices  38.4 us (31%)
  waiting for transfers between devices  23.7 us (19%)
  local copies, waits for them, and re-layouts  7.21 us (6%)
    pallas_call x4, Pallas kernels, halo(): pl.pallas_call(adj_kernel if kind == 'adj' else vel_kernel, grid=(4,), in...  26.4 us
    ppermute x4, starting transfers between devices, on_device(): lax.ppermute(v, axis, [(i + 1, i) for i in range(n - 1)])  15.4 us
    pallas_call x1, Pallas kernels, local(): pl.pallas_call(local_kernel, in_specs=[VMEM] * 4, out_specs=VMEM, out_sha...  14.6 us
    ppermute x4, starting transfers between devices, on_device(): lax.ppermute(v, axis, [(i, i + 1) for i in range(n - 1)])  9.88 us
    pallas_call x1, Pallas kernels, turbines(): pl.pallas_call(turbine_kernel, grid=(1,), in_specs=[SMEM, SMEM, whole(8,...  8.13 us
    all_to_all x1, starting transfers between devices, on_device(): lax.all_to_all(grad.reshape(n_wide, n_narrow, 128), 'wide', split_axis=0,...  7.61 us
    all_to_all x1, waiting for transfers between devices, on_device(): lax.all_to_all(grad.reshape(n_narrow, 1, 128), 'narrow', split_axis=0, co...  6.86 us
    ppermute x4, waiting for transfers between devices, on_device(): lax.ppermute(v, axis, [(i, i + 1) for i in range(n - 1)])  6.23 us
  transfers between devices with their start and end apart: 10, of which 4 were waited for; matrix products, arithmetic and copies ran while one was open for 6% of the time, Pallas kernels for 32%

profile of v1, /device:TPU:11, one launch (start us, length us, event | category | flops | bytes accessed | tf_op | source)
XLA Modules:
  0.0 123.4 jit_solution(14057403909793680341)
XLA Ops:
  0.6 0.0 copy-start.1
  0.6 2.6 %collective-permute-start.1 = (f32[3,32,32,256]{3,2,1,0:T(8,128)}, f32[3,32,32,256]{3,2,1,0:T(8,128)}, u32[]{:S(2)}, u32[]{:S(2)}) collective-permute-start(f32[3,32,32,256]{3,2,1,0:T(8,128)} %adj_ref.5), channel_id=1, source_target_pairs={{1,0},{2,1},{3,2},{4,3},{5,4},{6,5},{7,6},{9,8},{10,9},{11,10},{12... | collective-permute-start | bytes 9437192 | tf_op jit(solution)/shard_map/ppermute | solution.py:270
  3.2 3.0 %collective-permute-start = (f32[3,32,32,256]{3,2,1,0:T(8,128)}, f32[3,32,32,256]{3,2,1,0:T(8,128)}, u32[]{:S(2)}, u32[]{:S(2)}) collective-permute-start(f32[3,32,32,256]{3,2,1,0:T(8,128)} %adj_ref.5), channel_id=1, source_target_pairs={{0,1},{1,2},{2,3},{3,4},{4,5},{5,6},{6,7},{8,9},{9,10},{10,11},{11... | collective-permute-start | bytes 9437192 | tf_op jit(solution)/shard_map/ppermute | solution.py:269
  6.3 4.0 %fusion.1 = (f32[3,16,32,256]{3,2,1,0:T(8,128)}, f32[3,16,32,256]{3,2,1,0:T(8,128)}) fusion(f32[3,32,32,256]{3,2,1,0:T(8,128)} %adj_ref.5), kind=kLoop, calls=%fused_computation.1 | loop fusion | bytes 6291456 | tf_op jit(solution)/shard_map/slice | solution.py:276
  10.3 5.5 %collective-permute-start.3 = (f32[3,16,32,256]{3,2,1,0:T(8,128)}, f32[3,16,32,256]{3,2,1,0:T(8,128)}, u32[]{:S(2)}, u32[]{:S(2)}) collective-permute-start(f32[3,16,32,256]{3,2,1,0:T(8,128)} %get-tuple-element.34), channel_id=1, source_target_pairs={{8,0},{16,8},{24,16},{32,24},{40,32},{48,40},{56,48},{64,56},{72,6... | collective-permute-start | bytes 4718600 | tf_op jit(solution)/shard_map/ppermute | solution.py:270
  15.8 1.9 %collective-permute-start.2 = (f32[3,16,32,256]{3,2,1,0:T(8,128)}, f32[3,16,32,256]{3,2,1,0:T(8,128)}, u32[]{:S(2)}, u32[]{:S(2)}) collective-permute-start(f32[3,16,32,256]{3,2,1,0:T(8,128)} %get-tuple-element.35), channel_id=1, source_target_pairs={{0,8},{8,16},{16,24},{24,32},{32,40},{40,48},{48,56},{56,64},{64,7... | collective-permute-start | bytes 4718600 | tf_op jit(solution)/shard_map/ppermute | solution.py:269
  17.8 0.0 copy-done.1
  17.8 0.6 broadcast_in_dim.2.owner_ref
  18.4 8.1 %turbines.1 = (f32[32,32,256]{2,1,0:T(8,128)}, f32[128,128]{1,0:T(8,128)}) custom-call(s32[64,96]{1,0:T(8,128)} %bitcast.5, f32[96]{0:T(128)} %thrust_ref.1, s32[8,128]{1,0:T(8,128)} %broadcast_in_dim.2.owner_ref, f32[3,32,32,256]{3,2,1,0:T(8,128)} %adj_ref.5, f32[3,32,32,256]{3,2,1,0:T(8,128)} %adj_ref.5, f32[3,32,32,256]{3,2,1,0:T(8,128)} %vel_ref.3, ...), custom_call_target="tpu_custom_call" | custom-call | flops 1 | bytes 1 | tf_op jit(solution)/shard_map/turbines/pallas_call | solution.py:147
  26.5 7.6 %all-to-all-start = ((f32[16,8,128]{2,1,0:T(8,128)}), f32[16,8,128]{2,1,0:T(8,128)S(1)}, u32[]{:S(2)}, u32[]{:S(2)}) async-start(f32[16,8,128]{2,1,0:T(8,128)} %bitcast.4), calls=%async_computation | async-start | bytes 131072 | tf_op jit(solution)/shard_map/all_to_all | solution.py:283
  34.1 3.6 %prep.1.mats_ref.k_ref = bf16[12,256,256]{2,1,0:T(8,128)(2,1)} custom-call(f32[256,256]{1,0:T(8,128)} %dx_ref.1, f32[256,256]{1,0:T(8,128)} %dy_ref.1, f32[512,512]{1,0:T(8,128)} %dz_ref.1), custom_call_target="tpu_custom_call" | custom-call | flops 1 | bytes 1 | tf_op jit(solution)/shard_map/prep/pallas_call | solution.py:74
  37.8 0.0 copy-start
  37.8 14.6 %local.1.old_ref = f32[3,32,32,256]{3,2,1,0:T(8,128)} custom-call(f32[3,32,32,256]{3,2,1,0:T(8,128)} %adj_ref.5, f32[3,32,32,256]{3,2,1,0:T(8,128)} %vel_ref.3, f32[32,32,256]{2,1,0:T(8,128)} %get-tuple-element.17.force_ref, bf16[12,256,256]{2,1,0:T(8,128)(2,1)} %prep.1.mats_ref.k_ref), custom_call_target="tpu_custom_call" | custom-call | flops 1 | bytes 1 | tf_op jit(solution)/shard_map/local/pallas_call | solution.py:211
  52.4 4.9 %all-to-all-done = f32[16,8,128]{2,1,0:T(8,128)S(1)} async-done(((f32[16,8,128]{2,1,0:T(8,128)}), f32[16,8,128]{2,1,0:T(8,128)S(1)}, u32[]{:S(2)}, u32[]{:S(2)}) %all-to-all-start) | async-done | bytes 65568 | tf_op jit(solution)/shard_map/all_to_all | solution.py:283
  57.3 0.0 collective-permute-done.3.down_ref
  57.3 0.0 collective-permute-done.2.up_ref
  57.3 0.0 collective-permute-done.1.down_ref
  57.3 0.0 collective-permute-done.up_ref
  57.3 0.0 copy-done
  57.3 2.5 %collective-permute-start.5 = (f32[3,32,32,256]{3,2,1,0:T(8,128)S(1)}, f32[3,32,32,256]{3,2,1,0:T(8,128)}, u32[]{:S(2)}, u32[]{:S(2)}) collective-permute-start(f32[3,32,32,256]{3,2,1,0:T(8,128)S(1)} %copy-done), channel_id=1, source_target_pairs={{1,0},{2,1},{3,2},{4,3},{5,4},{6,5},{7,6},{9,8},{10,9},{11,10},{12... | collective-permute-start | bytes 9437192 | tf_op jit(solution)/shard_map/ppermute | solution.py:270
  59.9 3.0 %collective-permute-start.4 = (f32[3,32,32,256]{3,2,1,0:T(8,128)S(1)}, f32[3,32,32,256]{3,2,1,0:T(8,128)}, u32[]{:S(2)}, u32[]{:S(2)}) collective-permute-start(f32[3,32,32,256]{3,2,1,0:T(8,128)S(1)} %copy-done), channel_id=1, source_target_pairs={{0,1},{1,2},{2,3},{3,4},{4,5},{5,6},{6,7},{8,9},{9,10},{10,11},{11... | collective-permute-start | bytes 9437192 | tf_op jit(solution)/shard_map/ppermute | solution.py:269
  62.9 1.9 %fusion = (f32[3,16,32,256]{3,2,1,0:T(8,128)}, f32[3,16,32,256]{3,2,1,0:T(8,128)}) fusion(f32[3,32,32,256]{3,2,1,0:T(8,128)S(1)} %copy-done), kind=kLoop, calls=%fused_computation | loop fusion | bytes 6291456 | tf_op jit(solution)/shard_map/slice | solution.py:276
  64.8 4.7 %collective-permute-start.7 = (f32[3,16,32,256]{3,2,1,0:T(8,128)}, f32[3,16,32,256]{3,2,1,0:T(8,128)}, u32[]{:S(2)}, u32[]{:S(2)}) collective-permute-start(f32[3,16,32,256]{3,2,1,0:T(8,128)} %get-tuple-element.32), channel_id=1, source_target_pairs={{8,0},{16,8},{24,16},{32,24},{40,32},{48,40},{56,48},{64,56},{72,6... | collective-permute-start | bytes 4718600 | tf_op jit(solution)/shard_map/ppermute | solution.py:270
  69.5 1.9 %collective-permute-start.6 = (f32[3,16,32,256]{3,2,1,0:T(8,128)}, f32[3,16,32,256]{3,2,1,0:T(8,128)}, u32[]{:S(2)}, u32[]{:S(2)}) collective-permute-start(f32[3,16,32,256]{3,2,1,0:T(8,128)} %get-tuple-element.33), channel_id=1, source_target_pairs={{0,8},{8,16},{16,24},{24,32},{32,40},{40,48},{48,56},{56,64},{64,7... | collective-permute-start | bytes 4718600 | tf_op jit(solution)/shard_map/ppermute | solution.py:269
  71.5 0.6 reduce_sum.18
  72.1 5.5 %all-to-all-start.1 = ((f32[8,1,128]{2,1,0:T(1,128)}), f32[8,1,128]{2,1,0:T(1,128)S(1)}, u32[]{:S(2)}, u32[]{:S(2)}) async-start(f32[8,1,128]{2,1,0:T(1,128)} %bitcast.2), calls=%async_computation.1 | async-start | bytes 8192 | tf_op jit(solution)/shard_map/all_to_all | solution.py:289
  77.6 7.5 %y_adj.1.old_ref = f32[3,32,32,256]{3,2,1,0:T(8,128)} custom-call(f32[3,32,32,256]{3,2,1,0:T(8,128)} %vel_ref.3, f32[3,32,32,256]{3,2,1,0:T(8,128)} %collective-permute-done.up_ref, f32[3,32,32,256]{3,2,1,0:T(8,128)} %collective-permute-done.1.down_ref, bf16[12,256,256]{2,1,0:T(8,128)(2,1)} %prep.1.mats_ref.k_ref, ...), custom_call_target="tpu_custom_call", output_to_operand_aliasing={{}: (4, {})} | custom-call | flops 1 | bytes 1 | tf_op jit(solution)/shard_map/y_adj/pallas_call | solution.py:254
  85.1 6.2 %z_adj.1.old_ref = f32[3,32,32,256]{3,2,1,0:T(8,128)} custom-call(f32[3,32,32,256]{3,2,1,0:T(8,128)} %vel_ref.3, f32[3,16,32,256]{3,2,1,0:T(8,128)} %collective-permute-done.2.up_ref, f32[3,16,32,256]{3,2,1,0:T(8,128)} %collective-permute-done.3.down_ref, bf16[12,256,256]{2,1,0:T(8,128)(2,1)} %prep.1.mats_ref.k_ref, ...), custom_call_target="tpu_custom_call", output_to_operand_aliasing={{}: (4, {})} | custom-call | flops 1 | bytes 1 | tf_op jit(solution)/shard_map/z_adj/pallas_call | solution.py:254
  91.3 6.9 %all-to-all-done.1 = f32[8,1,128]{2,1,0:T(1,128)S(1)} async-done(((f32[8,1,128]{2,1,0:T(1,128)}), f32[8,1,128]{2,1,0:T(1,128)S(1)}, u32[]{:S(2)}, u32[]{:S(2)}) %all-to-all-start.1) | async-done | bytes 4128 | tf_op jit(solution)/shard_map/all_to_all | solution.py:289
  98.2 5.7 %collective-permute-done.7.down_ref = f32[3,16,32,256]{3,2,1,0:T(8,128)} collective-permute-done((f32[3,16,32,256]{3,2,1,0:T(8,128)}, f32[3,16,32,256]{3,2,1,0:T(8,128)}, u32[]{:S(2)}, u32[]{:S(2)}) %collective-permute-start.7) | collective-permute-done | bytes 1572896 | tf_op jit(solution)/shard_map/ppermute | solution.py:270
  103.9 6.2 %collective-permute-done.6.up_ref = f32[3,16,32,256]{3,2,1,0:T(8,128)} collective-permute-done((f32[3,16,32,256]{3,2,1,0:T(8,128)}, f32[3,16,32,256]{3,2,1,0:T(8,128)}, u32[]{:S(2)}, u32[]{:S(2)}) %collective-permute-start.6) | collective-permute-done | bytes 1572896 | tf_op jit(solution)/shard_map/ppermute | solution.py:269
  110.1 0.0 collective-permute-done.5.down_ref
  110.1 0.0 collective-permute-done.4.up_ref
  110.2 0.6 reshape.24
  110.8 7.0 %y_vel.1.old_ref = f32[3,32,32,256]{3,2,1,0:T(8,128)} custom-call(f32[3,32,32,256]{3,2,1,0:T(8,128)} %adj_ref.5, f32[3,32,32,256]{3,2,1,0:T(8,128)} %collective-permute-done.4.up_ref, f32[3,32,32,256]{3,2,1,0:T(8,128)} %collective-permute-done.5.down_ref, bf16[12,256,256]{2,1,0:T(8,128)(2,1)} %prep.1.mats_ref.k_ref, ...), custom_call_target="tpu_custom_call", output_to_operand_aliasing={{}: (4, {})} | custom-call | flops 1 | bytes 1 | tf_op jit(solution)/shard_map/y_vel/pallas_call | solution.py:254
  117.8 5.6 %z_vel.1 = f32[3,32,32,256]{3,2,1,0:T(8,128)} custom-call(f32[3,32,32,256]{3,2,1,0:T(8,128)} %adj_ref.5, f32[3,16,32,256]{3,2,1,0:T(8,128)} %collective-permute-done.6.up_ref, f32[3,16,32,256]{3,2,1,0:T(8,128)} %collective-permute-done.7.down_ref, bf16[12,256,256]{2,1,0:T(8,128)(2,1)} %prep.1.mats_ref.k_ref, ...), custom_call_target="tpu_custom_call", output_to_operand_aliasing={{}: (4, {})} | custom-call | flops 1 | bytes 1 | tf_op jit(solution)/shard_map/z_vel/pallas_call | solution.py:254
  (2 shorter events, 0.0 us)
Async XLA Ops:
  0.6 17.1 %copy-start.1 = (s32[96]{0:T(128)S(1)}, s32[96]{0:T(128)}, u32[]{:S(2)}) copy-start(s32[96]{0:T(128)} %param.15) | copy-start | bytes 1156
  0.6 56.6 %collective-permute-start.1 = (f32[3,32,32,256]{3,2,1,0:T(8,128)}, f32[3,32,32,256]{3,2,1,0:T(8,128)}, u32[]{:S(2)}, u32[]{:S(2)}) collective-permute-start(f32[3,32,32,256]{3,2,1,0:T(8,128)} %adj_ref.5), channel_id=1, source_target_pairs={{1,0},{2,1},{3,2},{4,3},{5,4},{6,5},{7,6},{9,8},{10,9},{11,10},{12... | collective-permute-start | bytes 9437192 | tf_op jit(solution)/shard_map/ppermute | solution.py:270
  3.2 54.0 %collective-permute-start = (f32[3,32,32,256]{3,2,1,0:T(8,128)}, f32[3,32,32,256]{3,2,1,0:T(8,128)}, u32[]{:S(2)}, u32[]{:S(2)}) collective-permute-start(f32[3,32,32,256]{3,2,1,0:T(8,128)} %adj_ref.5), channel_id=1, source_target_pairs={{0,1},{1,2},{2,3},{3,4},{4,5},{5,6},{6,7},{8,9},{9,10},{10,11},{11... | collective-permute-start | bytes 9437192 | tf_op jit(solution)/shard_map/ppermute | solution.py:269
  10.3 47.0 %collective-permute-start.3 = (f32[3,16,32,256]{3,2,1,0:T(8,128)}, f32[3,16,32,256]{3,2,1,0:T(8,128)}, u32[]{:S(2)}, u32[]{:S(2)}) collective-permute-start(f32[3,16,32,256]{3,2,1,0:T(8,128)} %get-tuple-element.34), channel_id=1, source_target_pairs={{8,0},{16,8},{24,16},{32,24},{40,32},{48,40},{56,48},{64,56},{72,6... | collective-permute-start | bytes 4718600 | tf_op jit(solution)/shard_map/ppermute | solution.py:270
  15.8 41.4 %collective-permute-start.2 = (f32[3,16,32,256]{3,2,1,0:T(8,128)}, f32[3,16,32,256]{3,2,1,0:T(8,128)}, u32[]{:S(2)}, u32[]{:S(2)}) collective-permute-start(f32[3,16,32,256]{3,2,1,0:T(8,128)} %get-tuple-element.35), channel_id=1, source_target_pairs={{0,8},{8,16},{16,24},{24,32},{32,40},{40,48},{48,56},{56,64},{64,7... | collective-permute-start | bytes 4718600 | tf_op jit(solution)/shard_map/ppermute | solution.py:269
  26.5 30.7 %all-to-all-start = ((f32[16,8,128]{2,1,0:T(8,128)}), f32[16,8,128]{2,1,0:T(8,128)S(1)}, u32[]{:S(2)}, u32[]{:S(2)}) async-start(f32[16,8,128]{2,1,0:T(8,128)} %bitcast.4), calls=%async_computation | async-start | bytes 131072 | tf_op jit(solution)/shard_map/all_to_all | solution.py:283
  37.8 19.5 %copy-start = (f32[3,32,32,256]{3,2,1,0:T(8,128)S(1)}, f32[3,32,32,256]{3,2,1,0:T(8,128)}, u32[]{:S(2)}) copy-start(f32[3,32,32,256]{3,2,1,0:T(8,128)} %vel_ref.3) | copy-start | bytes 9437188
  57.3 52.8 %collective-permute-start.5 = (f32[3,32,32,256]{3,2,1,0:T(8,128)S(1)}, f32[3,32,32,256]{3,2,1,0:T(8,128)}, u32[]{:S(2)}, u32[]{:S(2)}) collective-permute-start(f32[3,32,32,256]{3,2,1,0:T(8,128)S(1)} %copy-done), channel_id=1, source_target_pairs={{1,0},{2,1},{3,2},{4,3},{5,4},{6,5},{7,6},{9,8},{10,9},{11,10},{12... | collective-permute-start | bytes 9437192 | tf_op jit(solution)/shard_map/ppermute | solution.py:270
  59.9 50.3 %collective-permute-start.4 = (f32[3,32,32,256]{3,2,1,0:T(8,128)S(1)}, f32[3,32,32,256]{3,2,1,0:T(8,128)}, u32[]{:S(2)}, u32[]{:S(2)}) collective-permute-start(f32[3,32,32,256]{3,2,1,0:T(8,128)S(1)} %copy-done), channel_id=1, source_target_pairs={{0,1},{1,2},{2,3},{3,4},{4,5},{5,6},{6,7},{8,9},{9,10},{10,11},{11... | collective-permute-start | bytes 9437192 | tf_op jit(solution)/shard_map/ppermute | solution.py:269
  64.8 39.1 %collective-permute-start.7 = (f32[3,16,32,256]{3,2,1,0:T(8,128)}, f32[3,16,32,256]{3,2,1,0:T(8,128)}, u32[]{:S(2)}, u32[]{:S(2)}) collective-permute-start(f32[3,16,32,256]{3,2,1,0:T(8,128)} %get-tuple-element.32), channel_id=1, source_target_pairs={{8,0},{16,8},{24,16},{32,24},{40,32},{48,40},{56,48},{64,56},{72,6... | collective-permute-start | bytes 4718600 | tf_op jit(solution)/shard_map/ppermute | solution.py:270
  69.5 40.6 %collective-permute-start.6 = (f32[3,16,32,256]{3,2,1,0:T(8,128)}, f32[3,16,32,256]{3,2,1,0:T(8,128)}, u32[]{:S(2)}, u32[]{:S(2)}) collective-permute-start(f32[3,16,32,256]{3,2,1,0:T(8,128)} %get-tuple-element.33), channel_id=1, source_target_pairs={{0,8},{8,16},{16,24},{24,32},{32,40},{40,48},{48,56},{56,64},{64,7... | collective-permute-start | bytes 4718600 | tf_op jit(solution)/shard_map/ppermute | solution.py:269
  72.1 26.1 %all-to-all-start.1 = ((f32[8,1,128]{2,1,0:T(1,128)}), f32[8,1,128]{2,1,0:T(1,128)S(1)}, u32[]{:S(2)}, u32[]{:S(2)}) async-start(f32[8,1,128]{2,1,0:T(1,128)} %bitcast.2), calls=%async_computation.1 | async-start | bytes 8192 | tf_op jit(solution)/shard_map/all_to_all | solution.py:289

commit v2 on v1

v2 whole, which is shorter than its diff:
```python
import math

import jax
import jax.numpy as jnp
from jax import lax
from jax.experimental import pallas as pl
from jax.experimental.pallas import tpu as pltpu
from jax.sharding import PartitionSpec as P

F32 = jnp.float32
BF16 = jnp.bfloat16
NX = 256
NY = 256
SZ = 32
SY = 32
HZ = 16
TURB = 96
STEP = 0.2
VMEM = pl.BlockSpec(memory_space=pltpu.VMEM)
SMEM = pl.BlockSpec(memory_space=pltpu.SMEM)
HBM = pl.BlockSpec(memory_space=pltpu.HBM)
COST = pl.CostEstimate(flops=1, transcendentals=0, bytes_accessed=1)


def resident(v):
    return pltpu.with_memory_space_constraint(v, pltpu.VMEM)


def call(kernel, operands, outs, name, limit=12, **kw):
    return pl.pallas_call(
        kernel,
        out_shape=outs,
        compiler_params=pltpu.CompilerParams(vmem_limit_bytes=limit << 20),
        cost_estimate=COST,
        name=name,
        **kw,
    )(*operands)


def split(v):
    hi = v.astype(BF16)
    lo = (v - hi.astype(F32)).astype(BF16)
    return hi, lo


def dot(a, b):
    return lax.dot_general(a, b, (((1,), (0,)), ((), ())), preferred_element_type=F32)


def mix(k_hi, k_lo, v):
    hi, lo = split(v)
    return dot(k_hi, hi) + (dot(k_hi, lo) + dot(k_lo, hi))


def iota(axis):
    return lax.broadcasted_iota(jnp.int32, (256, 256), axis)


def prep_kernel(dx_ref, dy_ref, dz_ref, x_ref, z_ref, side_ref, far_ref, near_ref):
    wide, narrow = lax.axis_index("wide"), lax.axis_index("narrow")
    row, col = iota(0), iota(1)
    x_ref[0], x_ref[1] = split(dx_ref[...].T)

    def expand(rows, spread, chosen, same):
        return [jnp.where(same, dot(dot(spread, half).astype(BF16), chosen), 0.0).astype(BF16) for half in rows]

    rows = split(dy_ref[pl.ds(pl.multiple_of(narrow * SY, SY), SY), :])
    spread = (lax.broadcasted_iota(jnp.int32, (256, SY), 0) % SY == lax.broadcasted_iota(jnp.int32, (256, SY), 1)).astype(BF16)
    odd = narrow % 2
    other = narrow + 2 * odd - 1
    partner = narrow + 1 - 2 * odd
    chosen = (row == other * SY + col % SY).astype(BF16)
    far_ref[0], far_ref[1] = expand(rows, spread, chosen, row // SY == col // SY)
    chosen = (row == jnp.where((col // SY) % 2 == 0, narrow, partner) * SY + col % SY).astype(BF16)
    near_ref[0], near_ref[1] = expand(rows, spread[:128], chosen, row[:128] // SY == col[:128] // (2 * SY))
    rows = split(dz_ref[pl.ds(pl.multiple_of(wide * SZ, SZ), SZ), :])
    spread = (lax.broadcasted_iota(jnp.int32, (256, SZ), 0) // 8 == lax.broadcasted_iota(jnp.int32, (256, SZ), 1)).astype(BF16)
    source = lax.broadcasted_iota(jnp.int32, (512, 256), 0)
    plane = lax.broadcasted_iota(jnp.int32, (512, 256), 1) // 8
    halo = jnp.where(plane < HZ, plane - HZ, plane - HZ + SZ)
    for out_ref, offset in ((z_ref, plane), (side_ref, halo)):
        chosen = (source == wide * SZ + offset).astype(BF16)
        out_ref[0], out_ref[1] = expand(rows, spread, chosen, row % 8 == col % 8)


def prep(deriv_x, deriv_y, deriv_z):
    outs = [pltpu.VMEM((2, rows, 256), BF16) for rows in (256, 256, 256, 256, 128)]
    return call(prep_kernel, (deriv_x, deriv_y, deriv_z), outs, "prep", in_specs=[VMEM] * 3, out_specs=[VMEM] * 5)


def turbine_kernel(block_ref, thrust_ref, owner_ref, adj_ref, vel_ref, weight_ref, force_ref, grad_ref, ax, ay, ux, total, padded, g0, g1):
    wide, narrow = lax.axis_index("wide"), lax.axis_index("narrow")
    cells = SZ * SY
    for half in range(2):
        lanes = pl.ds(128 * half, 128)
        rows = pl.ds(cells * half, cells)
        ax[rows, :] = adj_ref[0, :, :, lanes].reshape(cells, 128)
        ay[rows, :] = adj_ref[1, :, :, lanes].reshape(cells, 128)
        ux[rows, :] = vel_ref[0, :, :, lanes].reshape(cells, 128)
    total[...] = jnp.zeros_like(total)
    padded[...] = jnp.zeros_like(padded)
    g0[...] = jnp.zeros_like(g0)
    g1[...] = jnp.zeros_like(g1)

    def turbine(t, _):
        block = block_ref[0, t]
        start_z = block // (2 * NY) - wide * SZ
        start_y = (block // 2) % NY - narrow * SY
        half = block % 2
        near = (start_z > -SZ) & (start_z < SZ) & (start_y > -2) & (start_y < SY)

        @pl.when(near)
        def _():
            padded[pl.ds(64, 64), :] = weight_ref[t]
            for line in range(2):
                y = start_y + line

                @pl.when((y >= 0) & (y < SY))
                def _():
                    w = padded[pl.ds(64 - 2 * start_z + line, SZ, stride=2), :]
                    rows = pl.ds(half * cells + y, SZ, stride=SY)
                    a, b, u = ax[rows, :], ay[rows, :], ux[rows, :]
                    size = jnp.abs(u)
                    drive = w * (u * size)
                    g0[pl.ds(t, 1), :] += jnp.sum(drive * a, axis=0, keepdims=True)
                    g1[pl.ds(t, 1), :] += jnp.sum(drive * b, axis=0, keepdims=True)
                    total[rows, :] += (thrust_ref[t] * w) * (size * a)

        return 0

    lax.fori_loop(0, TURB, turbine, 0)
    for half in range(2):
        force_ref[:, :, pl.ds(128 * half, 128)] = total[pl.ds(cells * half, cells), :].reshape(SZ, SY, 128)
    ones = jnp.ones((8, 128), F32)
    lanes_sum = lambda g: lax.dot_general(
        ones, g[...], (((1,), (1,)), ((), ())), precision=lax.Precision.HIGHEST, preferred_element_type=F32
    )
    row, col = lax.broadcasted_iota(jnp.int32, (128, 128), 0), lax.broadcasted_iota(jnp.int32, (128, 128), 1)
    owner = owner_ref[0:1, :]
    owner_col = jnp.sum(jnp.where(row == col, owner, 0), axis=1, keepdims=True)
    rank = jnp.sum(((owner_col == owner) & (row < col)).astype(jnp.int32), axis=0, keepdims=True)
    value = jnp.where(row % 2 == 0, lanes_sum(g0)[0:1], lanes_sum(g1)[0:1]) * (1.0 / math.sqrt(128.0 * 64.0))
    value = jnp.where((row < 4) & (rank == row // 2), value, 0.0)
    grad_ref[...] = lax.dot_general(
        (owner == row).astype(F32), value, (((1,), (1,)), ((), ())), precision=lax.Precision.HIGHEST, preferred_element_type=F32
    )


def turbines(blocks, thrust, owner, adjoint, velocity, weight):
    scratch = [pltpu.VMEM((2 * SZ * SY, 128), F32)] * 4 + [pltpu.VMEM((192, 128), F32)] + [pltpu.VMEM((128, 128), F32)] * 2
    outs = [pltpu.VMEM((SZ, SY, NX), F32), jax.ShapeDtypeStruct((128, 128), F32)]
    operands = (blocks, thrust, owner, adjoint, velocity, weight)
    return call(turbine_kernel, operands, outs, "turbines", 16, in_specs=[SMEM] * 2 + [VMEM] * 4, out_specs=[VMEM] * 2, scratch_shapes=scratch)


def copy_of(source, target, sem):
    return pltpu.make_async_copy(source, target, sem)


def chip_lines(one, two, c, at):
    return jnp.stack([one[c, at, :, :], two[c, at, :, :]], axis=1).reshape(256, 256)


def xz_kernel(adj_ref, vel_ref, force_ref, x_ref, z_ref, out_ref, tend, sems):
    stores = []
    for yb in range(SY // 8):
        at = pl.ds(yb * 8, 8)
        field = lambda ref, c: ref[c, :, at, :].reshape(256, 256)
        x_hi, x_lo, z_hi, z_lo = x_ref[0], x_ref[1], z_ref[0], z_ref[1]

        def both(v):
            hi, lo = split(v)
            return (
                dot(hi, x_hi) + (dot(lo, x_hi) + dot(hi, x_lo)),
                dot(z_hi, hi) + (dot(z_hi, lo) + dot(z_lo, hi)),
            )

        stretch_x = jnp.zeros((256, 256), F32)
        stretch_z = jnp.zeros((256, 256), F32)
        for c in range(3):
            dx, dz = both(field(vel_ref, c))
            a = field(adj_ref, c)
            stretch_x += a * dx
            stretch_z += a * dz
        for c in range(3):
            a = field(adj_ref, c)
            dx, dz = both(a)
            total = field(vel_ref, 0) * dx + field(vel_ref, 2) * dz
            if c == 0:
                total -= stretch_x + force_ref[:, at, :].reshape(256, 256)
            if c == 2:
                total -= stretch_z
            tend[c, :, at, :] = (a + STEP * total).reshape(SZ, 8, NX)
        stores.append(copy_of(tend.at[:, :, at], out_ref.at[:, :, at], sems.at[yb]))
        stores[-1].start()
    for copy in stores:
        copy.wait()


def side_lines(up_ref, down_ref, c, at):
    return jnp.concatenate([up_ref[c, :, at, :].reshape(128, 256), down_ref[c, :, at, :].reshape(128, 256)], axis=0)


def adj_kernel(vel_ref, far_ref, up_ref, down_ref, y_ref, z_ref, old_ref, out_ref):
    def planes(g, _):
        at = pl.ds(pl.multiple_of(g * 8, 8), 8)
        field = lambda ref, c: ref[c, at, :, :].reshape(256, 256)
        for c in range(3):
            total = field(vel_ref, 1) * mix(y_ref[0], y_ref[1], field(far_ref, c))
            out_ref[c, at, :, :] = (field(old_ref, c) + STEP * total).reshape(8, SY, NX)
        return 0

    def lines(yb, _):
        at = pl.ds(pl.multiple_of(yb * 8, 8), 8)
        field = lambda ref, c: ref[c, :, at, :].reshape(256, 256)
        for c in range(3):
            total = field(vel_ref, 2) * mix(z_ref[0], z_ref[1], side_lines(up_ref, down_ref, c, at))
            out_ref[c, :, at, :] = (field(out_ref, c) + STEP * total).reshape(SZ, 8, NX)
        return 0

    lax.fori_loop(0, SZ // 8, planes, 0)
    lax.fori_loop(0, SY // 8, lines, 0)


def near_kernel(adj_ref, vel_ref, adj2_ref, vel2_ref, k_ref, old_ref, done_ref, rest_ref, stage, sem):
    def planes(g, _):
        at = pl.ds(pl.multiple_of(g * 4, 4), 4)
        field = lambda ref, c: ref[c, at, :, :].reshape(128, 256)
        both = jnp.concatenate([k_ref[0], k_ref[1]], axis=0)

        def deriv(one, two, c):
            hi, lo = split(chip_lines(one, two, c, at))
            most = dot(both, hi)
            return most[:128] + (most[128:] + dot(k_ref[0], lo))

        stretch = jnp.zeros((128, 256), F32)
        for c in range(3):
            stretch += field(adj_ref, c) * deriv(vel_ref, vel2_ref, c)
        for c in range(3):
            total = field(vel_ref, 1) * deriv(adj_ref, adj2_ref, c)
            if c == 1:
                total -= stretch
            total = (field(old_ref, c) + STEP * total).reshape(4, SY, NX)
            if c == 0:
                stage[at, :, :] = total
            else:
                rest_ref[c - 1, at, :, :] = total
        return 0

    lax.fori_loop(0, SZ // 4, planes, 0)
    store = copy_of(stage, done_ref.at[0], sem)
    store.start()
    store.wait()


def vel_kernel(adj_ref, far_ref, up_ref, down_ref, y_ref, z_ref, rest_ref, done_ref, out_ref, token_ref, stage, sems):
    del done_ref
    token_ref[...] = jnp.zeros_like(token_ref)
    stores = []
    for g in range(SZ // 8):
        at = pl.ds(8 * g, 8)
        field = lambda ref, c: ref[c, at, :, :].reshape(256, 256)
        stretch = jnp.zeros((256, 256), F32)
        for c in range(3):
            stretch += field(adj_ref, c) * mix(y_ref[0], y_ref[1], field(far_ref, c))
        stage[0, at, :, :] = (field(rest_ref, 0) - STEP * stretch).reshape(8, SY, NX)
        stores.append(copy_of(stage.at[0, at], out_ref.at[1, at], sems.at[0, g]))
        stores[-1].start()
    for yb in range(SY // 8):
        at = pl.ds(8 * yb, 8)
        field = lambda ref, c: ref[c, :, at, :].reshape(256, 256)
        stretch = jnp.zeros((256, 256), F32)
        for c in range(3):
            stretch += field(adj_ref, c) * mix(z_ref[0], z_ref[1], side_lines(up_ref, down_ref, c, at))
        stage[1, :, at, :] = (field(rest_ref, 1) - STEP * stretch).reshape(SZ, 8, NX)
        stores.append(copy_of(stage.at[1, :, at], out_ref.at[2, :, at], sems.at[1, yb]))
        stores[-1].start()
    for copy in stores:
        copy.wait()


def share_kernel(terms_ref, done_ref, out_ref):
    del done_ref
    total = jnp.sum(terms_ref[...].reshape(128, 128), axis=0, keepdims=True)
    out_ref[0:1, :] = total[:, 0:2]
    out_ref[1:2, :] = total[:, 2:4]


def on_device(adjoint, velocity, deriv_x, deriv_y, deriv_z, rotor_blocks, turbine_owner, disk_weight, thrust):
    n_wide, n_narrow = lax.axis_size("wide"), lax.axis_size("narrow")
    up = [(i, i + 1) for i in range(n_wide - 1)]
    down = [(i + 1, i) for i in range(n_wide - 1)]
    chip = [(i, i ^ 1) for i in range(n_narrow)]
    across = [pair for i in range(1, n_narrow - 1, 2) for pair in ((i, i + 1), (i + 1, i))]
    barrier = lax.optimization_barrier
    shape = jax.ShapeDtypeStruct(adjoint.shape, F32)
    field = pltpu.VMEM(adjoint.shape, F32)
    dma = pltpu.SemaphoreType.DMA

    def exchange(v, upper, lower):
        return lax.ppermute(v, "narrow", across), lax.ppermute(upper, "wide", up), lax.ppermute(lower, "wide", down)

    first, upper, lower = barrier((adjoint, adjoint[:, HZ:], adjoint[:, :HZ]))
    sides = exchange(first, upper, lower)
    adj, vel = resident(adjoint), resident(velocity)
    owner = jnp.broadcast_to(jnp.pad(turbine_owner, (0, 128 - TURB), constant_values=-1)[None], (8, 128))
    force, grad = turbines(rotor_blocks.T, thrust, owner, adj, vel, resident(disk_weight))
    grad = lax.all_to_all(grad.reshape(n_wide * n_narrow, 1, 128), ("wide", "narrow"), split_axis=0, concat_axis=0, tiled=True)
    m_x, m_z, m_side, m_far, m_near = prep(deriv_x, deriv_y, deriv_z)
    out = call(
        xz_kernel, (adj, vel, force, m_x, m_z), shape, "xz", 16, in_specs=[VMEM] * 5, out_specs=HBM, scratch_shapes=[field, dma((4,))]
    )
    out, grad, adjoint, velocity, upper, lower, *sides = barrier(
        (out, grad, adjoint, velocity, velocity[:, HZ:], velocity[:, :HZ], *sides)
    )

    vel_sides = exchange(velocity, upper, lower)
    near = [resident(lax.ppermute(v, "narrow", chip)) for v in (adjoint, velocity)]
    adj, vel = resident(adjoint), resident(velocity)
    operands = (vel, *[resident(v) for v in sides], m_far, m_side, resident(out))
    out = call(adj_kernel, operands, field, "halo_adj", in_specs=[VMEM] * 7, out_specs=VMEM)
    out, rest = call(
        near_kernel,
        (adj, vel, *near, m_near, out),
        [shape, pltpu.VMEM((2, SZ, SY, NX), F32)],
        "near",
        in_specs=[VMEM] * 6,
        out_specs=[HBM, VMEM],
        scratch_shapes=[pltpu.VMEM((SZ, SY, NX), F32), dma(())],
    )
    out, token = call(
        vel_kernel,
        (adj, *[resident(v) for v in vel_sides], m_far, m_side, rest, out),
        [shape, jax.ShapeDtypeStruct((8, 128), F32)],
        "halo_vel",
        in_specs=[VMEM] * 7 + [HBM],
        out_specs=[HBM, VMEM],
        input_output_aliases={7: 0},
        scratch_shapes=[pltpu.VMEM((2, SZ, SY, NX), F32), dma((2, 4))],
    )
    share = call(share_kernel, (grad, token), jax.ShapeDtypeStruct((2, 2), F32), "share", in_specs=[VMEM] * 2, out_specs=VMEM)
    return out, share


def solution(mesh):
    field = P(None, "wide", "narrow", None)
    return jax.shard_map(
        on_device,
        mesh=mesh,
        in_specs=(field, field) + (P(),) * 7,
        out_specs=(field, P(("wide", "narrow"), None)),
        check_vma=False,
    )
```

time: 124 us -> 107 us (0.86)
  the two profiles are of different devices: /device:TPU:11 before, /device:TPU:2 now
where the time goes in v2:
time: 107 us; the launch traced here: 105 us
  Pallas kernels  35.1 us (33%)
  starting transfers between devices  27.6 us (26%)
  waiting for transfers between devices  27 us (25%)
  local copies, waits for them, and re-layouts  13.9 us (13%)
    pallas_call x7, Pallas kernels, call(): pl.pallas_call(kernel, out_shape=outs, compiler_params=pltpu.CompilerPara...  35.1 us
    ppermute x2, waiting for transfers between devices, exchange(): lax.ppermute(upper, 'wide', up)  16.6 us
    all_to_all x1, starting transfers between devices, on_device(): lax.all_to_all(grad.reshape(n_wide * n_narrow, 1, 128), ('wide', 'narrow'...  11.4 us
    ppermute x2, starting transfers between devices, exchange(): lax.ppermute(upper, 'wide', up)  8.53 us
    unnamed x34, local copies, waits for them, and re-layouts  7.64 us
    all_to_all x1, waiting for transfers between devices, on_device(): lax.all_to_all(grad.reshape(n_wide * n_narrow, 1, 128), ('wide', 'narrow'...  5.83 us
    ppermute x2, waiting for transfers between devices, exchange(): lax.ppermute(lower, 'wide', down)  4.57 us
    ppermute x2, starting transfers between devices, exchange(): lax.ppermute(v, 'narrow', across)  4.27 us
  transfers between devices with their start and end apart: 9, of which 3 were waited for; matrix products, arithmetic and copies ran while one was open for 2% of the time, Pallas kernels for 28%

profile of v2, /device:TPU:2, one launch (start us, length us, event | category | flops | bytes accessed | tf_op | source)
XLA Modules:
  0.0 104.6 jit_solution(3939112213497620007)
XLA Ops:
  0.6 0.0 copy-start.16
  0.6 0.0 copy-start
  0.7 0.0 copy-start.15
  0.7 0.0 copy-start.3
  0.7 4.2 %fusion = (f32[3,16,32,256]{3,2,1,0:T(8,128)}, f32[3,16,32,256]{3,2,1,0:T(8,128)}) fusion(f32[3,32,32,256]{3,2,1,0:T(8,128)} %adj_ref.5), kind=kLoop, calls=%fused_computation | loop fusion | bytes 6291456 | tf_op jit(solution)/shard_map/slice | solution.py:303
  4.8 1.9 %collective-permute-start = (f32[3,32,32,256]{3,2,1,0:T(8,128)}, f32[3,32,32,256]{3,2,1,0:T(8,128)}, u32[]{:S(2)}, u32[]{:S(2)}) collective-permute-start(f32[3,32,32,256]{3,2,1,0:T(8,128)} %adj_ref.5), channel_id=1, source_target_pairs={{1,2},{2,1},{3,4},{4,3},{5,6},{6,5},{9,10},{10,9},{11,12},{12,11},... | collective-permute-start | bytes 9437192 | tf_op jit(solution)/shard_map/ppermute | solution.py:301
  6.7 5.0 %collective-permute-start.1 = (f32[3,16,32,256]{3,2,1,0:T(8,128)}, f32[3,16,32,256]{3,2,1,0:T(8,128)}, u32[]{:S(2)}, u32[]{:S(2)}) collective-permute-start(f32[3,16,32,256]{3,2,1,0:T(8,128)} %get-tuple-element.30), channel_id=1, source_target_pairs={{0,8},{8,16},{16,24},{24,32},{32,40},{40,48},{48,56},{56,64},{64,7... | collective-permute-start | bytes 4718600 | tf_op jit(solution)/shard_map/ppermute | solution.py:301
  11.7 1.3 %collective-permute-start.2 = (f32[3,16,32,256]{3,2,1,0:T(8,128)}, f32[3,16,32,256]{3,2,1,0:T(8,128)}, u32[]{:S(2)}, u32[]{:S(2)}) collective-permute-start(f32[3,16,32,256]{3,2,1,0:T(8,128)} %get-tuple-element.31), channel_id=1, source_target_pairs={{8,0},{16,8},{24,16},{32,24},{40,32},{48,40},{56,48},{64,56},{72,6... | collective-permute-start | bytes 4718600 | tf_op jit(solution)/shard_map/ppermute | solution.py:301
  13.0 0.0 copy-done.16
  13.1 0.0 copy-done
  13.1 0.0 copy-done.15
  13.1 0.0 copy-done.3
  13.1 0.0 copy-start.14
  13.1 0.7 copy-done.14
  13.9 6.2 %turbines.1 = (f32[32,32,256]{2,1,0:T(8,128)S(1)}, f32[128,128]{1,0:T(8,128)}) custom-call(s32[64,96]{1,0:T(8,128)S(1)} %bitcast.2, f32[96]{0:T(128)S(1)} %copy-done.15, s32[8,128]{1,0:T(8,128)S(1)} %broadcast_in_dim.2.owner_ref, f32[3,32,32,256]{3,2,1,0:T(8,128)} %adj_ref.5, f32[3,32,32,256]{3,2,1,0:T(8,128)S(1)} %copy-done, f32[96,64,128]{2,1,0:T(8,128)S(1)} %copy-done.3), custom_call_target="tpu_custom_call" | custom-call | flops 1 | bytes 1 | tf_op jit(solution)/shard_map/turbines/pallas_call | solution.py:30
  20.0 0.0 copy-start.8
  20.0 1.0 copy-done.8
  21.0 11.4 %all-to-all-start = ((f32[128,1,128]{2,1,0:T(1,128)}), f32[128,1,128]{2,1,0:T(1,128)S(1)}, u32[]{:S(2)}, u32[]{:S(2)}) async-start(f32[128,1,128]{2,1,0:T(1,128)} %bitcast.1), calls=%async_computation | async-start | bytes 131072 | tf_op jit(solution)/shard_map/all_to_all | solution.py:308
  32.5 0.0 copy-start.7
  32.5 0.0 copy-start.10
  32.5 0.0 copy-start.11
  32.5 0.0 copy-start.9
  32.5 2.1 %fusion.1 = (f32[3,16,32,256]{3,2,1,0:T(8,128)}, f32[3,16,32,256]{3,2,1,0:T(8,128)}) fusion(f32[3,32,32,256]{3,2,1,0:T(8,128)S(1)} %copy-done), kind=kLoop, calls=%fused_computation.1 | loop fusion | bytes 6291456 | tf_op jit(solution)/shard_map/slice | solution.py:314
  34.6 0.0 copy-done.7
  34.6 0.0 copy-done.10
  34.6 0.0 copy-done.11
  34.6 1.0 prep.1
  35.6 0.0 copy-start.4
  35.6 0.7 copy-done.4
  36.3 0.0 copy-start.12
  36.3 0.7 copy-done.12
  37.0 0.0 copy-done.9
  37.0 8.1 %xz.1.old_ref = f32[3,32,32,256]{3,2,1,0:T(8,128)S(1)} custom-call(f32[3,32,32,256]{3,2,1,0:T(8,128)} %adj_ref.5, f32[3,32,32,256]{3,2,1,0:T(8,128)S(1)} %copy-done, f32[32,32,256]{2,1,0:T(8,128)S(1)} %copy-done.9, bf16[2,256,256]{2,1,0:T(8,128)(2,1)S(1)} %get-tuple-element.26.x_ref, bf16[2,256,256]{2,1,0:T(8,128)(2,1)S(1)} %get-tuple-element.27.z_ref), custom_call_target="tpu_custom_call" | custom-call | flops 1 | bytes 1 | tf_op jit(solution)/shard_map/xz/pallas_call | solution.py:30
  45.1 0.0 copy-start.1
  45.1 1.7 %copy-done.1 = f32[3,32,32,256]{3,2,1,0:T(8,128)} copy-done((f32[3,32,32,256]{3,2,1,0:T(8,128)}, f32[3,32,32,256]{3,2,1,0:T(8,128)S(1)}, u32[]{:S(2)}) %copy-start.1) | copy-done | bytes 3145752
  46.8 5.8 %all-to-all-done.terms_ref = f32[128,1,128]{2,1,0:T(1,128)S(1)} async-done(((f32[128,1,128]{2,1,0:T(1,128)}), f32[128,1,128]{2,1,0:T(1,128)S(1)}, u32[]{:S(2)}, u32[]{:S(2)}) %all-to-all-start) | async-done | bytes 65568 | tf_op jit(solution)/shard_map/all_to_all | solution.py:308
  52.6 0.0 collective-permute-done.1.up_ref
  52.6 0.0 collective-permute-done.2.down_ref
  52.6 0.0 collective-permute-done.far_ref
  52.6 0.1 collective-permute-start.6
  52.7 0.5 collective-permute-start.7
  53.2 2.4 %collective-permute-start.3 = (f32[3,32,32,256]{3,2,1,0:T(8,128)S(1)}, f32[3,32,32,256]{3,2,1,0:T(8,128)S(1)}, u32[]{:S(2)}, u32[]{:S(2)}) collective-permute-start(f32[3,32,32,256]{3,2,1,0:T(8,128)S(1)} %copy-done), channel_id=1, source_target_pairs={{1,2},{2,1},{3,4},{4,3},{5,6},{6,5},{9,10},{10,9},{11,12},{12,11},... | collective-permute-start | bytes 9437192 | tf_op jit(solution)/shard_map/ppermute | solution.py:301
  55.6 3.5 %collective-permute-start.4 = (f32[3,16,32,256]{3,2,1,0:T(8,128)}, f32[3,16,32,256]{3,2,1,0:T(8,128)S(1)}, u32[]{:S(2)}, u32[]{:S(2)}) collective-permute-start(f32[3,16,32,256]{3,2,1,0:T(8,128)} %get-tuple-element.34), channel_id=1, source_target_pairs={{0,8},{8,16},{16,24},{24,32},{32,40},{40,48},{48,56},{56,64},{64,7... | collective-permute-start | bytes 4718600 | tf_op jit(solution)/shard_map/ppermute | solution.py:301
  59.1 1.5 %collective-permute-start.5 = (f32[3,16,32,256]{3,2,1,0:T(8,128)}, f32[3,16,32,256]{3,2,1,0:T(8,128)S(1)}, u32[]{:S(2)}, u32[]{:S(2)}) collective-permute-start(f32[3,16,32,256]{3,2,1,0:T(8,128)} %get-tuple-element.35), channel_id=1, source_target_pairs={{8,0},{16,8},{24,16},{32,24},{40,32},{48,40},{56,48},{64,56},{72,6... | collective-permute-start | bytes 4718600 | tf_op jit(solution)/shard_map/ppermute | solution.py:301
  60.6 0.0 copy-start.2
  60.6 1.9 %copy-done.2 = f32[3,32,32,256]{3,2,1,0:T(8,128)S(1)} copy-done((f32[3,32,32,256]{3,2,1,0:T(8,128)S(1)}, f32[3,32,32,256]{3,2,1,0:T(8,128)}, u32[]{:S(2)}) %copy-start.2) | copy-done | bytes 3145752
  62.5 0.0 copy-start.5
  62.5 0.9 copy-done.5
  63.4 0.0 copy-start.13
  63.4 6.8 %halo_adj.1.old_ref = f32[3,32,32,256]{3,2,1,0:T(8,128)S(1)} custom-call(f32[3,32,32,256]{3,2,1,0:T(8,128)S(1)} %copy-done, f32[3,32,32,256]{3,2,1,0:T(8,128)} %collective-permute-done.far_ref, f32[3,16,32,256]{3,2,1,0:T(8,128)} %collective-permute-done.1.up_ref, f32[3,16,32,256]{3,2,1,0:T(8,128)} %collective-permute-done.2.down_ref, ...), custom_call_target="tpu_custom_call" | custom-call | flops 1 | bytes 1 | tf_op jit(solution)/shard_map/halo_adj/pallas_call | solution.py:30
  70.3 0.0 collective-permute-done.6.adj2_ref
  70.3 0.0 collective-permute-done.7.vel2_ref
  70.3 0.0 copy-done.13
  70.3 0.0 copy-start.6
  70.3 6.9 %near.1 = (f32[3,32,32,256]{3,2,1,0:T(8,128)}, f32[2,32,32,256]{3,2,1,0:T(8,128)S(1)}) custom-call(f32[3,32,32,256]{3,2,1,0:T(8,128)} %adj_ref.5, f32[3,32,32,256]{3,2,1,0:T(8,128)S(1)} %copy-done, f32[3,32,32,256]{3,2,1,0:T(8,128)S(1)} %collective-permute-done.6.adj2_ref, f32[3,32,32,256]{3,2,1,0:T(8,128)S(1)} %collective-permute-done.7.vel2_ref, ...), custom_call_target="tpu_custom_call" | custom-call | flops 1 | bytes 1 | tf_op jit(solution)/shard_map/near/pallas_call | solution.py:30
  77.3 16.6 %collective-permute-done.4.up_ref = f32[3,16,32,256]{3,2,1,0:T(8,128)S(1)} collective-permute-done((f32[3,16,32,256]{3,2,1,0:T(8,128)}, f32[3,16,32,256]{3,2,1,0:T(8,128)S(1)}, u32[]{:S(2)}, u32[]{:S(2)}) %collective-permute-start.4) | collective-permute-done | bytes 1572896 | tf_op jit(solution)/shard_map/ppermute | solution.py:301
  93.9 4.6 %collective-permute-done.5.down_ref = f32[3,16,32,256]{3,2,1,0:T(8,128)S(1)} collective-permute-done((f32[3,16,32,256]{3,2,1,0:T(8,128)}, f32[3,16,32,256]{3,2,1,0:T(8,128)S(1)}, u32[]{:S(2)}, u32[]{:S(2)}) %collective-permute-start.5) | collective-permute-done | bytes 1572896 | tf_op jit(solution)/shard_map/ppermute | solution.py:301
  98.4 0.0 collective-permute-done.3.far_ref
  98.4 0.0 copy-done.6
  98.4 5.4 %halo_vel.1 = (f32[3,32,32,256]{3,2,1,0:T(8,128)}, f32[8,128]{1,0:T(8,128)S(1)}) custom-call(f32[3,32,32,256]{3,2,1,0:T(8,128)} %adj_ref.5, f32[3,32,32,256]{3,2,1,0:T(8,128)S(1)} %collective-permute-done.3.far_ref, f32[3,16,32,256]{3,2,1,0:T(8,128)S(1)} %collective-permute-done.4.up_ref, ...), custom_call_target="tpu_custom_call", output_to_operand_aliasing={{0}: (7, {})} | custom-call | flops 1 | bytes 1 | tf_op jit(solution)/shard_map/halo_vel/pallas_call | solution.py:30
  103.9 0.7 share.1
  (2 shorter events, 0.0 us)
Async XLA Ops:
  0.6 12.4 %copy-start.16 = (s32[96]{0:T(128)S(1)}, s32[96]{0:T(128)}, u32[]{:S(2)}) copy-start(s32[96]{0:T(128)} %param.15) | copy-start | bytes 1156
  0.6 12.4 %copy-start = (f32[3,32,32,256]{3,2,1,0:T(8,128)S(1)}, f32[3,32,32,256]{3,2,1,0:T(8,128)}, u32[]{:S(2)}) copy-start(f32[3,32,32,256]{3,2,1,0:T(8,128)} %vel_ref.5) | copy-start | bytes 9437188
  0.7 12.4 %copy-start.15 = (f32[96]{0:T(128)S(1)}, f32[96]{0:T(128)}, u32[]{:S(2)}) copy-start(f32[96]{0:T(128)} %thrust_ref.1) | copy-start | bytes 1156
  0.7 12.4 %copy-start.3 = (f32[96,64,128]{2,1,0:T(8,128)S(1)}, f32[96,64,128]{2,1,0:T(8,128)}, u32[]{:S(2)}) copy-start(f32[96,64,128]{2,1,0:T(8,128)} %weight_ref.1) | copy-start | bytes 9437188
  4.8 47.8 %collective-permute-start = (f32[3,32,32,256]{3,2,1,0:T(8,128)}, f32[3,32,32,256]{3,2,1,0:T(8,128)}, u32[]{:S(2)}, u32[]{:S(2)}) collective-permute-start(f32[3,32,32,256]{3,2,1,0:T(8,128)} %adj_ref.5), channel_id=1, source_target_pairs={{1,2},{2,1},{3,4},{4,3},{5,6},{6,5},{9,10},{10,9},{11,12},{12,11},... | collective-permute-start | bytes 9437192 | tf_op jit(solution)/shard_map/ppermute | solution.py:301
  6.7 45.9 %collective-permute-start.1 = (f32[3,16,32,256]{3,2,1,0:T(8,128)}, f32[3,16,32,256]{3,2,1,0:T(8,128)}, u32[]{:S(2)}, u32[]{:S(2)}) collective-permute-start(f32[3,16,32,256]{3,2,1,0:T(8,128)} %get-tuple-element.30), channel_id=1, source_target_pairs={{0,8},{8,16},{16,24},{24,32},{32,40},{40,48},{48,56},{56,64},{64,7... | collective-permute-start | bytes 4718600 | tf_op jit(solution)/shard_map/ppermute | solution.py:301
  11.7 40.9 %collective-permute-start.2 = (f32[3,16,32,256]{3,2,1,0:T(8,128)}, f32[3,16,32,256]{3,2,1,0:T(8,128)}, u32[]{:S(2)}, u32[]{:S(2)}) collective-permute-start(f32[3,16,32,256]{3,2,1,0:T(8,128)} %get-tuple-element.31), channel_id=1, source_target_pairs={{8,0},{16,8},{24,16},{32,24},{40,32},{48,40},{56,48},{64,56},{72,6... | collective-permute-start | bytes 4718600 | tf_op jit(solution)/shard_map/ppermute | solution.py:301
  13.1 0.8 copy-start.14
  20.0 1.0 copy-start.8
  21.0 31.6 %all-to-all-start = ((f32[128,1,128]{2,1,0:T(1,128)}), f32[128,1,128]{2,1,0:T(1,128)S(1)}, u32[]{:S(2)}, u32[]{:S(2)}) async-start(f32[128,1,128]{2,1,0:T(1,128)} %bitcast.1), calls=%async_computation | async-start | bytes 131072 | tf_op jit(solution)/shard_map/all_to_all | solution.py:308
  32.5 2.2 %copy-start.7 = (f32[512,512]{1,0:T(8,128)S(1)}, f32[512,512]{1,0:T(8,128)}, u32[]{:S(2)}) copy-start(f32[512,512]{1,0:T(8,128)} %dz_ref.1) | copy-start | bytes 3145732
  32.5 2.1 %copy-start.10 = (f32[256,256]{1,0:T(8,128)S(1)}, f32[256,256]{1,0:T(8,128)}, u32[]{:S(2)}) copy-start(f32[256,256]{1,0:T(8,128)} %dx_ref.1) | copy-start | bytes 786436
  32.5 2.1 %copy-start.11 = (f32[256,256]{1,0:T(8,128)S(1)}, f32[256,256]{1,0:T(8,128)}, u32[]{:S(2)}) copy-start(f32[256,256]{1,0:T(8,128)} %dy_ref.1) | copy-start | bytes 786436
  32.5 4.5 %copy-start.9 = (f32[32,32,256]{2,1,0:T(8,128)S(1)}, f32[32,32,256]{2,1,0:T(8,128)}, u32[]{:S(2)}) copy-start(f32[32,32,256]{2,1,0:T(8,128)} %copy-done.8) | copy-start | bytes 3145732
  35.6 0.7 copy-start.4
  36.3 0.7 copy-start.12
  45.1 1.7 %copy-start.1 = (f32[3,32,32,256]{3,2,1,0:T(8,128)}, f32[3,32,32,256]{3,2,1,0:T(8,128)S(1)}, u32[]{:S(2)}) copy-start(f32[3,32,32,256]{3,2,1,0:T(8,128)S(1)} %xz.1.old_ref) | copy-start | bytes 9437188
  52.6 17.7 %collective-permute-start.6 = (f32[3,32,32,256]{3,2,1,0:T(8,128)}, f32[3,32,32,256]{3,2,1,0:T(8,128)S(1)}, u32[]{:S(2)}, u32[]{:S(2)}) collective-permute-start(f32[3,32,32,256]{3,2,1,0:T(8,128)} %adj_ref.5), channel_id=1, source_target_pairs={{0,1},{1,0},{2,3},{3,2},{4,5},{5,4},{6,7},{7,6},{8,9},{9,8},{10,11... | collective-permute-start | bytes 9437192 | tf_op jit(solution)/shard_map/ppermute | solution.py:318
  52.7 17.6 %collective-permute-start.7 = (f32[3,32,32,256]{3,2,1,0:T(8,128)S(1)}, f32[3,32,32,256]{3,2,1,0:T(8,128)S(1)}, u32[]{:S(2)}, u32[]{:S(2)}) collective-permute-start(f32[3,32,32,256]{3,2,1,0:T(8,128)S(1)} %copy-done), channel_id=1, source_target_pairs={{0,1},{1,0},{2,3},{3,2},{4,5},{5,4},{6,7},{7,6},{8,9},{9,8},{10,11... | collective-permute-start | bytes 9437192 | tf_op jit(solution)/shard_map/ppermute | solution.py:318
  53.2 45.2 %collective-permute-start.3 = (f32[3,32,32,256]{3,2,1,0:T(8,128)S(1)}, f32[3,32,32,256]{3,2,1,0:T(8,128)S(1)}, u32[]{:S(2)}, u32[]{:S(2)}) collective-permute-start(f32[3,32,32,256]{3,2,1,0:T(8,128)S(1)} %copy-done), channel_id=1, source_target_pairs={{1,2},{2,1},{3,4},{4,3},{5,6},{6,5},{9,10},{10,9},{11,12},{12,11},... | collective-permute-start | bytes 9437192 | tf_op jit(solution)/shard_map/ppermute | solution.py:301
  55.6 38.3 %collective-permute-start.4 = (f32[3,16,32,256]{3,2,1,0:T(8,128)}, f32[3,16,32,256]{3,2,1,0:T(8,128)S(1)}, u32[]{:S(2)}, u32[]{:S(2)}) collective-permute-start(f32[3,16,32,256]{3,2,1,0:T(8,128)} %get-tuple-element.34), channel_id=1, source_target_pairs={{0,8},{8,16},{16,24},{24,32},{32,40},{40,48},{48,56},{56,64},{64,7... | collective-permute-start | bytes 4718600 | tf_op jit(solution)/shard_map/ppermute | solution.py:301
  59.1 39.3 %collective-permute-start.5 = (f32[3,16,32,256]{3,2,1,0:T(8,128)}, f32[3,16,32,256]{3,2,1,0:T(8,128)S(1)}, u32[]{:S(2)}, u32[]{:S(2)}) collective-permute-start(f32[3,16,32,256]{3,2,1,0:T(8,128)} %get-tuple-element.35), channel_id=1, source_target_pairs={{8,0},{16,8},{24,16},{32,24},{40,32},{48,40},{56,48},{64,56},{72,6... | collective-permute-start | bytes 4718600 | tf_op jit(solution)/shard_map/ppermute | solution.py:301
  60.6 1.9 %copy-start.2 = (f32[3,32,32,256]{3,2,1,0:T(8,128)S(1)}, f32[3,32,32,256]{3,2,1,0:T(8,128)}, u32[]{:S(2)}) copy-start(f32[3,32,32,256]{3,2,1,0:T(8,128)} %copy-done.1) | copy-start | bytes 9437188
  62.5 0.9 copy-start.5
  63.4 6.8 %copy-start.13 = (bf16[2,128,256]{2,1,0:T(8,128)(2,1)S(1)}, bf16[2,128,256]{2,1,0:T(8,128)(2,1)}, u32[]{:S(2)}) copy-start(bf16[2,128,256]{2,1,0:T(8,128)(2,1)} %copy-done.12) | copy-start | bytes 393220
  70.3 28.1 %copy-start.6 = (bf16[2,256,256]{2,1,0:T(8,128)(2,1)S(1)}, bf16[2,256,256]{2,1,0:T(8,128)(2,1)}, u32[]{:S(2)}) copy-start(bf16[2,256,256]{2,1,0:T(8,128)(2,1)} %copy-done.4) | copy-start | bytes 786436

commit v3 on v2

--- a/solution.py
+++ b/solution.py
@@ -18,7 +18,7 @@
 STEP = 0.2
 VMEM = pl.BlockSpec(memory_space=pltpu.VMEM)
 SMEM = pl.BlockSpec(memory_space=pltpu.SMEM)
-HBM = pl.BlockSpec(memory_space=pltpu.HBM)
+HBM = pl.BlockSpec(memory_space=pl.ANY)
 COST = pl.CostEstimate(flops=1, transcendentals=0, bytes_accessed=1)
 
 
@@ -56,7 +56,8 @@
     return lax.broadcasted_iota(jnp.int32, (256, 256), axis)
 
 
-def prep_kernel(dx_ref, dy_ref, dz_ref, x_ref, z_ref, side_ref, far_ref, near_ref):
+def prep_kernel(dx_ref, dy_ref, dz_ref, x_ref, z_ref, side_ref, far_ref, near_ref, token_ref):
+    token_ref[...] = jnp.zeros_like(token_ref)
     wide, narrow = lax.axis_index("wide"), lax.axis_index("narrow")
     row, col = iota(0), iota(1)
     x_ref[0], x_ref[1] = split(dx_ref[...].T)
@@ -85,7 +86,8 @@
 
 def prep(deriv_x, deriv_y, deriv_z):
     outs = [pltpu.VMEM((2, rows, 256), BF16) for rows in (256, 256, 256, 256, 128)]
-    return call(prep_kernel, (deriv_x, deriv_y, deriv_z), outs, "prep", in_specs=[VMEM] * 3, out_specs=[VMEM] * 5)
+    outs.append(jax.ShapeDtypeStruct((8, 128), F32))
+    return call(prep_kernel, (deriv_x, deriv_y, deriv_z), outs, "prep", in_specs=[VMEM] * 3, out_specs=[VMEM] * 6)
 
 
 def turbine_kernel(block_ref, thrust_ref, owner_ref, adj_ref, vel_ref, weight_ref, force_ref, grad_ref, ax, ay, ux, total, padded, g0, g1):
@@ -161,7 +163,8 @@
     return jnp.stack([one[c, at, :, :], two[c, at, :, :]], axis=1).reshape(256, 256)
 
 
-def xz_kernel(adj_ref, vel_ref, force_ref, x_ref, z_ref, out_ref, tend, sems):
+def xz_kernel(token_ref, adj_ref, vel_ref, force_ref, x_ref, z_ref, out_ref, next_ref, tend, sems):
+    next_ref[...] = token_ref[...]
     stores = []
     for yb in range(SY // 8):
         at = pl.ds(yb * 8, 8)
@@ -222,7 +225,9 @@
     lax.fori_loop(0, SY // 8, lines, 0)
 
 
-def near_kernel(adj_ref, vel_ref, adj2_ref, vel2_ref, k_ref, old_ref, done_ref, rest_ref, stage, sem):
+def near_kernel(before_ref, adj_ref, vel_ref, adj2_ref, vel2_ref, k_ref, old_ref, done_ref, rest_ref, token_ref, stage, sem):
+    token_ref[...] = before_ref[...]
+
     def planes(g, _):
         at = pl.ds(pl.multiple_of(g * 4, 4), 4)
         field = lambda ref, c: ref[c, at, :, :].reshape(128, 256)
@@ -253,27 +258,35 @@
     store.wait()
 
 
-def vel_kernel(adj_ref, far_ref, up_ref, down_ref, y_ref, z_ref, rest_ref, done_ref, out_ref, token_ref, stage, sems):
-    del done_ref
-    token_ref[...] = jnp.zeros_like(token_ref)
+def far_kernel(token_ref, adj_ref, far_ref, k_ref, rest_ref, done_ref, out_ref, last_ref, stage, sems):
+    del token_ref, done_ref
     stores = []
     for g in range(SZ // 8):
         at = pl.ds(8 * g, 8)
         field = lambda ref, c: ref[c, at, :, :].reshape(256, 256)
         stretch = jnp.zeros((256, 256), F32)
         for c in range(3):
-            stretch += field(adj_ref, c) * mix(y_ref[0], y_ref[1], field(far_ref, c))
-        stage[0, at, :, :] = (field(rest_ref, 0) - STEP * stretch).reshape(8, SY, NX)
-        stores.append(copy_of(stage.at[0, at], out_ref.at[1, at], sems.at[0, g]))
+            stretch += field(adj_ref, c) * mix(k_ref[0], k_ref[1], field(far_ref, c))
+        stage[at, :, :] = (field(rest_ref, 0) - STEP * stretch).reshape(8, SY, NX)
+        stores.append(copy_of(stage.at[at], out_ref.at[1, at], sems.at[g]))
         stores[-1].start()
+    last_ref[...] = rest_ref[1]
+    for copy in stores:
+        copy.wait()
+
+
+def z_kernel(adj_ref, up_ref, down_ref, k_ref, last_ref, done_ref, out_ref, token_ref, stage, sems):
+    del done_ref
+    token_ref[...] = jnp.zeros_like(token_ref)
+    stores = []
     for yb in range(SY // 8):
         at = pl.ds(8 * yb, 8)
         field = lambda ref, c: ref[c, :, at, :].reshape(256, 256)
         stretch = jnp.zeros((256, 256), F32)
         for c in range(3):
-            stretch += field(adj_ref, c) * mix(z_ref[0], z_ref[1], side_lines(up_ref, down_ref, c, at))
-        stage[1, :, at, :] = (field(rest_ref, 1) - STEP * stretch).reshape(SZ, 8, NX)
-        stores.append(copy_of(stage.at[1, :, at], out_ref.at[2, :, at], sems.at[1, yb]))
+            stretch += field(adj_ref, c) * mix(k_ref[0], k_ref[1], side_lines(up_ref, down_ref, c, at))
+        stage[:, at, :] = (last_ref[:, at, :].reshape(256, 256) - STEP * stretch).reshape(SZ, 8, NX)
+        stores.append(copy_of(stage.at[:, at], out_ref.at[2, :, at], sems.at[yb]))
         stores[-1].start()
     for copy in stores:
         copy.wait()
@@ -297,46 +310,70 @@
     field = pltpu.VMEM(adjoint.shape, F32)
     dma = pltpu.SemaphoreType.DMA
 
-    def exchange(v, upper, lower):
-        return lax.ppermute(v, "narrow", across), lax.ppermute(upper, "wide", up), lax.ppermute(lower, "wide", down)
+    small = jax.ShapeDtypeStruct((8, 128), F32)
+    far = lambda v: lax.ppermute(v, "narrow", across)
+    sides = lambda upper, lower: [lax.ppermute(upper, "wide", up), lax.ppermute(lower, "wide", down)]
 
     first, upper, lower = barrier((adjoint, adjoint[:, HZ:], adjoint[:, :HZ]))
-    sides = exchange(first, upper, lower)
+    adj_sides = sides(upper, lower)
+    adj_far = far(first)
+    near = [lax.ppermute(v, "narrow", chip) for v in (first, velocity)]
     adj, vel = resident(adjoint), resident(velocity)
     owner = jnp.broadcast_to(jnp.pad(turbine_owner, (0, 128 - TURB), constant_values=-1)[None], (8, 128))
     force, grad = turbines(rotor_blocks.T, thrust, owner, adj, vel, resident(disk_weight))
+    deriv_y, grad, *near = barrier((deriv_y, grad, *near))
+    m_x, m_z, m_side, m_far, m_near, token = prep(deriv_x, deriv_y, deriv_z)
     grad = lax.all_to_all(grad.reshape(n_wide * n_narrow, 1, 128), ("wide", "narrow"), split_axis=0, concat_axis=0, tiled=True)
-    m_x, m_z, m_side, m_far, m_near = prep(deriv_x, deriv_y, deriv_z)
-    out = call(
-        xz_kernel, (adj, vel, force, m_x, m_z), shape, "xz", 16, in_specs=[VMEM] * 5, out_specs=HBM, scratch_shapes=[field, dma((4,))]
-    )
-    out, grad, adjoint, velocity, upper, lower, *sides = barrier(
-        (out, grad, adjoint, velocity, velocity[:, HZ:], velocity[:, :HZ], *sides)
-    )
-
-    vel_sides = exchange(velocity, upper, lower)
-    near = [resident(lax.ppermute(v, "narrow", chip)) for v in (adjoint, velocity)]
-    adj, vel = resident(adjoint), resident(velocity)
-    operands = (vel, *[resident(v) for v in sides], m_far, m_side, resident(out))
-    out = call(adj_kernel, operands, field, "halo_adj", in_specs=[VMEM] * 7, out_specs=VMEM)
-    out, rest = call(
-        near_kernel,
-        (adj, vel, *near, m_near, out),
-        [shape, pltpu.VMEM((2, SZ, SY, NX), F32)],
-        "near",
+    out, token = call(
+        xz_kernel,
+        (token, adj, vel, force, m_x, m_z),
+        [shape, small],
+        "xz",
+        16,
         in_specs=[VMEM] * 6,
         out_specs=[HBM, VMEM],
+        scratch_shapes=[field, dma((4,))],
+    )
+    token, gated = barrier((token, velocity))
+    vel_far = far(gated)
+    out, upper, lower, adj_far, *adj_sides = barrier(
+        (out, velocity[:, HZ:], velocity[:, :HZ], adj_far, *adj_sides)
+    )
+
+    vel_sides = sides(upper, lower)
+    adj, vel = resident(adjoint), resident(velocity)
+    operands = (vel, *[resident(v) for v in (adj_far, *adj_sides)], m_far, m_side, resident(out))
+    out = call(adj_kernel, operands, field, "halo_adj", in_specs=[VMEM] * 7, out_specs=VMEM)
+    out, rest, token = call(
+        near_kernel,
+        (token, adj, vel, *[resident(v) for v in near], m_near, out),
+        [shape, pltpu.VMEM((2, SZ, SY, NX), F32), small],
+        "near",
+        in_specs=[VMEM] * 7,
+        out_specs=[HBM, VMEM, VMEM],
         scratch_shapes=[pltpu.VMEM((SZ, SY, NX), F32), dma(())],
     )
+    token, vel_far = barrier((token, vel_far))
+    plane = pltpu.VMEM((SZ, SY, NX), F32)
+    out, last = call(
+        far_kernel,
+        (token, adj, resident(vel_far), m_far, rest, out),
+        [shape, plane],
+        "far_vel",
+        in_specs=[VMEM] * 5 + [HBM],
+        out_specs=[HBM, VMEM],
+        input_output_aliases={5: 0},
+        scratch_shapes=[plane, dma((4,))],
+    )
     out, token = call(
-        vel_kernel,
-        (adj, *[resident(v) for v in vel_sides], m_far, m_side, rest, out),
-        [shape, jax.ShapeDtypeStruct((8, 128), F32)],
-        "halo_vel",
-        in_specs=[VMEM] * 7 + [HBM],
+        z_kernel,
+        (adj, *[resident(v) for v in vel_sides], m_side, last, out),
+        [shape, small],
+        "z_vel",
+        in_specs=[VMEM] * 5 + [HBM],
         out_specs=[HBM, VMEM],
-        input_output_aliases={7: 0},
-        scratch_shapes=[pltpu.VMEM((2, SZ, SY, NX), F32), dma((2, 4))],
+        input_output_aliases={5: 0},
+        scratch_shapes=[plane, dma((4,))],
     )
     share = call(share_kernel, (grad, token), jax.ShapeDtypeStruct((2, 2), F32), "share", in_specs=[VMEM] * 2, out_specs=VMEM)
     return out, share

time: 107 us -> 101 us (0.944); the launches traced: 105 us -> 101 us
  waiting for transfers between devices: 27 us -> 9.57 us
  local copies, waits for them, and re-layouts: 13.9 us -> 25.5 us
  Pallas kernels: 35.1 us -> 37.3 us
    ppermute x8, waiting for transfers between devices: 21.2 us -> 9.56 us  [the longest x2 6.34 us: on_device(): lax.ppermute(lower, 'wide', down)]
    unnamed x34 -> x50, local copies, waits for them, and re-layouts: 7.64 us -> 19.2 us
    all_to_all x1, waiting for transfers between devices: 5.83 us -> 0.01 us  [on_device(): lax.all_to_all(grad.reshape(n_wide * n_narrow, 1, 128), ('wide', 'narrow'...]
    pallas_call x7 -> x8, Pallas kernels: 35.1 us -> 37.3 us  [call(): pl.pallas_call(kernel, out_shape=outs, compiler_params=pltpu.CompilerPara...]
    slice x1, local copies, waits for them, and re-layouts: 4.16 us -> 2.28 us  [on_device(): first, upper, lower = barrier((adjoint, adjoint[:, HZ:], adjoint[:, :HZ]))]
    slice x1, local copies, waits for them, and re-layouts: 2.1 us -> 3.94 us  [on_device(): velocity[:, :HZ]]
    all_to_all x1, starting transfers between devices: 11.4 us -> 10.3 us  [on_device(): lax.all_to_all(grad.reshape(n_wide * n_narrow, 1, 128), ('wide', 'narrow'...]
    ppermute x8, starting transfers between devices: 16.1 us -> 17.2 us  [the longest x2 8.97 us: on_device(): lax.ppermute(upper, 'wide', up)]
  transfers between devices with their start and end apart: 9 -> 9, of which waited for: 3 -> 3; matrix products, arithmetic and copies ran while one was open for 2% -> 4% of each run, Pallas kernels for 28% -> 36%
where the time goes in v3:
time: 101 us
  Pallas kernels  37.3 us (37%)
  starting transfers between devices  27.6 us (27%)
  local copies, waits for them, and re-layouts  25.5 us (25%)
  waiting for transfers between devices  9.57 us (9%)
    pallas_call x8, Pallas kernels, call(): pl.pallas_call(kernel, out_shape=outs, compiler_params=pltpu.CompilerPara...  37.3 us
    unnamed x50, local copies, waits for them, and re-layouts  19.2 us
    all_to_all x1, starting transfers between devices, on_device(): lax.all_to_all(grad.reshape(n_wide * n_narrow, 1, 128), ('wide', 'narrow'...  10.3 us
    ppermute x2, starting transfers between devices, on_device(): lax.ppermute(upper, 'wide', up)  8.97 us
    ppermute x2, waiting for transfers between devices, on_device(): lax.ppermute(lower, 'wide', down)  6.34 us
    ppermute x2, starting transfers between devices, on_device(): far = lambda v: lax.ppermute(v, 'narrow', across)  5.18 us
    slice x1, local copies, waits for them, and re-layouts, on_device(): velocity[:, :HZ]  3.94 us
    ppermute x2, waiting for transfers between devices, on_device(): lax.ppermute(upper, 'wide', up)  3.21 us
  transfers between devices with their start and end apart: 9, of which 3 were waited for; matrix products, arithmetic and copies ran while one was open for 4% of the time, Pallas kernels for 36%

profile of v3, /device:TPU:2, one launch (start us, length us, event | category | flops | bytes accessed | tf_op | source)
XLA Modules:
  0.0 100.8 jit_solution(13826715502756901562)
XLA Ops:
  0.6 0.0 copy-start
  0.6 0.0 copy-start.24
  0.7 0.0 copy-start.23
  0.7 0.0 copy-start.1
  0.7 2.3 %fusion.1 = (f32[3,16,32,256]{3,2,1,0:T(8,128)S(1)}, f32[3,16,32,256]{3,2,1,0:T(8,128)S(1)}) fusion(f32[3,32,32,256]{3,2,1,0:T(8,128)} %adj_ref.9), kind=kLoop, calls=%fused_computation.1 | loop fusion | bytes 6291456 | tf_op jit(solution)/shard_map/slice | solution.py:317
  3.0 0.5 copy-done
  3.5 0.0 collective-permute-start
  3.5 0.5 collective-permute-start.1
  4.0 2.0 %collective-permute-start.2 = (f32[3,32,32,256]{3,2,1,0:T(8,128)S(1)}, f32[3,32,32,256]{3,2,1,0:T(8,128)S(1)}, u32[]{:S(2)}, u32[]{:S(2)}) collective-permute-start(f32[3,32,32,256]{3,2,1,0:T(8,128)S(1)} %copy-done), channel_id=1, source_target_pairs={{1,2},{2,1},{3,4},{4,3},{5,6},{6,5},{9,10},{10,9},{11,12},{12,11},... | collective-permute-start | bytes 9437192 | tf_op jit(solution)/shard_map/ppermute | solution.py:314
  5.9 4.0 %collective-permute-start.3 = (f32[3,16,32,256]{3,2,1,0:T(8,128)S(1)}, f32[3,16,32,256]{3,2,1,0:T(8,128)S(1)}, u32[]{:S(2)}, u32[]{:S(2)}) collective-permute-start(f32[3,16,32,256]{3,2,1,0:T(8,128)S(1)} %get-tuple-element.44), channel_id=1, source_target_pairs={{0,8},{8,16},{16,24},{24,32},{32,40},{40,48},{48,56},{56,64},{64,7... | collective-permute-start | bytes 4718600 | tf_op jit(solution)/shard_map/ppermute | solution.py:315
  10.0 1.3 %collective-permute-start.4 = (f32[3,16,32,256]{3,2,1,0:T(8,128)S(1)}, f32[3,16,32,256]{3,2,1,0:T(8,128)S(1)}, u32[]{:S(2)}, u32[]{:S(2)}) collective-permute-start(f32[3,16,32,256]{3,2,1,0:T(8,128)S(1)} %get-tuple-element.45), channel_id=1, source_target_pairs={{8,0},{16,8},{24,16},{32,24},{40,32},{48,40},{56,48},{64,56},{72,6... | collective-permute-start | bytes 4718600 | tf_op jit(solution)/shard_map/ppermute | solution.py:315
  11.3 0.0 copy-done.24
  11.3 0.0 copy-done.23
  11.3 0.0 copy-done.1
  11.3 0.0 copy-start.22
  11.3 0.7 copy-done.22
  12.1 0.0 copy-start.17
  12.1 0.0 copy-start.18
  12.1 6.3 %turbines.1 = (f32[32,32,256]{2,1,0:T(8,128)S(1)}, f32[128,128]{1,0:T(8,128)}) custom-call(s32[64,96]{1,0:T(8,128)S(1)} %bitcast.2, f32[96]{0:T(128)S(1)} %copy-done.23, s32[8,128]{1,0:T(8,128)S(1)} %broadcast_in_dim.2.owner_ref, f32[3,32,32,256]{3,2,1,0:T(8,128)S(1)} %copy-done, f32[3,32,32,256]{3,2,1,0:T(8,128)} %vel_ref.7, f32[96,64,128]{2,1,0:T(8,128)S(1)} %copy-done.1), custom_call_target="tpu_custom_call" | custom-call | flops 1 | bytes 1 | tf_op jit(solution)/shard_map/turbines/pallas_call | solution.py:30
  18.4 0.0 collective-permute-done.adj2_ref
  18.4 1.7 %copy-done.2 = f32[3,32,32,256]{3,2,1,0:T(8,128)} copy-done((f32[3,32,32,256]{3,2,1,0:T(8,128)}, f32[3,32,32,256]{3,2,1,0:T(8,128)S(1)}, u32[]{:S(2)}) %copy-start.2) | copy-done | bytes 3145752
  20.0 0.0 collective-permute-done.1.vel2_ref
  20.0 1.6 %copy-done.4 = f32[3,32,32,256]{3,2,1,0:T(8,128)} copy-done((f32[3,32,32,256]{3,2,1,0:T(8,128)}, f32[3,32,32,256]{3,2,1,0:T(8,128)S(1)}, u32[]{:S(2)}) %copy-start.4) | copy-done | bytes 3145752
  21.7 0.0 copy-done.17
  21.7 0.0 copy-done.18
  21.7 0.0 copy-done.19
  21.7 1.0 prep.1
  22.7 0.0 copy-start.14
  22.7 0.7 copy-done.14
  23.4 0.6 copy-done.20
  24.0 8.1 %xz.1 = (f32[3,32,32,256]{3,2,1,0:T(8,128)S(1)}, f32[8,128]{1,0:T(8,128)S(1)}) custom-call(f32[8,128]{1,0:T(8,128)S(1)} %get-tuple-element.39.token_ref, f32[3,32,32,256]{3,2,1,0:T(8,128)S(1)} %copy-done, f32[3,32,32,256]{3,2,1,0:T(8,128)} %vel_ref.7, f32[32,32,256]{2,1,0:T(8,128)S(1)} %get-tuple-element.40.force_ref, ...), custom_call_target="tpu_custom_call" | custom-call | flops 1 | bytes 1 | tf_op jit(solution)/shard_map/xz/pallas_call | solution.py:30
  32.1 0.0 copy-start.8
  32.1 1.7 %copy-done.8 = f32[3,32,32,256]{3,2,1,0:T(8,128)} copy-done((f32[3,32,32,256]{3,2,1,0:T(8,128)}, f32[3,32,32,256]{3,2,1,0:T(8,128)S(1)}, u32[]{:S(2)}) %copy-start.8) | copy-done | bytes 3145752
  33.8 3.2 %collective-permute-start.7 = (f32[3,32,32,256]{3,2,1,0:T(8,128)}, f32[3,32,32,256]{3,2,1,0:T(8,128)}, u32[]{:S(2)}, u32[]{:S(2)}) collective-permute-start(f32[3,32,32,256]{3,2,1,0:T(8,128)} %vel_ref.7), channel_id=1, source_target_pairs={{1,2},{2,1},{3,4},{4,3},{5,6},{6,5},{9,10},{10,9},{11,12},{12,11},... | collective-permute-start | bytes 9437192 | tf_op jit(solution)/shard_map/ppermute | solution.py:314
  37.1 3.9 %fusion = (f32[3,16,32,256]{3,2,1,0:T(8,128)}, f32[3,16,32,256]{3,2,1,0:T(8,128)}) fusion(f32[3,32,32,256]{3,2,1,0:T(8,128)} %vel_ref.7), kind=kLoop, calls=%fused_computation | loop fusion | bytes 6291456 | tf_op jit(solution)/shard_map/slice | solution.py:340
  41.0 3.2 %collective-permute-done.3.up_ref = f32[3,16,32,256]{3,2,1,0:T(8,128)S(1)} collective-permute-done((f32[3,16,32,256]{3,2,1,0:T(8,128)S(1)}, f32[3,16,32,256]{3,2,1,0:T(8,128)S(1)}, u32[]{:S(2)}, u32[]{:S(2)}) %collective-permute-start.3) | collective-permute-done | bytes 1572896 | tf_op jit(solution)/shard_map/ppermute | solution.py:315
  44.2 1.2 %copy-done.10 = f32[3,16,32,256]{3,2,1,0:T(8,128)} copy-done((f32[3,16,32,256]{3,2,1,0:T(8,128)}, f32[3,16,32,256]{3,2,1,0:T(8,128)S(1)}, u32[]{:S(2)}) %copy-start.10) | copy-done | bytes 1572888
  45.4 3.4 %collective-permute-done.4.down_ref = f32[3,16,32,256]{3,2,1,0:T(8,128)S(1)} collective-permute-done((f32[3,16,32,256]{3,2,1,0:T(8,128)S(1)}, f32[3,16,32,256]{3,2,1,0:T(8,128)S(1)}, u32[]{:S(2)}, u32[]{:S(2)}) %collective-permute-start.4) | collective-permute-done | bytes 1572896 | tf_op jit(solution)/shard_map/ppermute | solution.py:315
  48.8 1.2 %copy-done.12 = f32[3,16,32,256]{3,2,1,0:T(8,128)} copy-done((f32[3,16,32,256]{3,2,1,0:T(8,128)}, f32[3,16,32,256]{3,2,1,0:T(8,128)S(1)}, u32[]{:S(2)}) %copy-start.12) | copy-done | bytes 1572888
  50.0 0.0 collective-permute-done.2.far_ref
  50.0 1.7 %copy-done.6 = f32[3,32,32,256]{3,2,1,0:T(8,128)} copy-done((f32[3,32,32,256]{3,2,1,0:T(8,128)}, f32[3,32,32,256]{3,2,1,0:T(8,128)S(1)}, u32[]{:S(2)}) %copy-start.6) | copy-done | bytes 3145752
  51.7 5.0 %collective-permute-start.5 = (f32[3,16,32,256]{3,2,1,0:T(8,128)}, f32[3,16,32,256]{3,2,1,0:T(8,128)}, u32[]{:S(2)}, u32[]{:S(2)}) collective-permute-start(f32[3,16,32,256]{3,2,1,0:T(8,128)} %get-tuple-element.46), channel_id=1, source_target_pairs={{0,8},{8,16},{16,24},{24,32},{32,40},{40,48},{48,56},{56,64},{64,7... | collective-permute-start | bytes 4718600 | tf_op jit(solution)/shard_map/ppermute | solution.py:315
  56.7 1.3 %collective-permute-start.6 = (f32[3,16,32,256]{3,2,1,0:T(8,128)}, f32[3,16,32,256]{3,2,1,0:T(8,128)}, u32[]{:S(2)}, u32[]{:S(2)}) collective-permute-start(f32[3,16,32,256]{3,2,1,0:T(8,128)} %get-tuple-element.47), channel_id=1, source_target_pairs={{8,0},{16,8},{24,16},{32,24},{40,32},{48,40},{56,48},{64,56},{72,6... | collective-permute-start | bytes 4718600 | tf_op jit(solution)/shard_map/ppermute | solution.py:315
  58.0 10.3 %all-to-all-start = ((f32[128,1,128]{2,1,0:T(1,128)}), f32[128,1,128]{2,1,0:T(1,128)S(1)}, u32[]{:S(2)}, u32[]{:S(2)}) async-start(f32[128,1,128]{2,1,0:T(1,128)} %bitcast.1), calls=%async_computation | async-start | bytes 131072 | tf_op jit(solution)/shard_map/all_to_all | solution.py:326
  68.3 0.0 copy-start.7
  68.3 1.9 %copy-done.7 = f32[3,32,32,256]{3,2,1,0:T(8,128)S(1)} copy-done((f32[3,32,32,256]{3,2,1,0:T(8,128)S(1)}, f32[3,32,32,256]{3,2,1,0:T(8,128)}, u32[]{:S(2)}) %copy-start.7) | copy-done | bytes 3145752
  70.2 1.9 %copy-done.9 = f32[3,32,32,256]{3,2,1,0:T(8,128)S(1)} copy-done((f32[3,32,32,256]{3,2,1,0:T(8,128)S(1)}, f32[3,32,32,256]{3,2,1,0:T(8,128)}, u32[]{:S(2)}) %copy-start.9) | copy-done | bytes 3145752
  72.1 1.4 %copy-done.11 = f32[3,16,32,256]{3,2,1,0:T(8,128)S(1)} copy-done((f32[3,16,32,256]{3,2,1,0:T(8,128)S(1)}, f32[3,16,32,256]{3,2,1,0:T(8,128)}, u32[]{:S(2)}) %copy-start.11) | copy-done | bytes 1572888
  73.5 1.4 %copy-done.13 = f32[3,16,32,256]{3,2,1,0:T(8,128)S(1)} copy-done((f32[3,16,32,256]{3,2,1,0:T(8,128)S(1)}, f32[3,16,32,256]{3,2,1,0:T(8,128)}, u32[]{:S(2)}) %copy-start.13) | copy-done | bytes 1572888
  74.9 0.9 copy-done.15
  75.9 6.0 %halo_adj.1.old_ref = f32[3,32,32,256]{3,2,1,0:T(8,128)S(1)} custom-call(f32[3,32,32,256]{3,2,1,0:T(8,128)} %vel_ref.7, f32[3,32,32,256]{3,2,1,0:T(8,128)S(1)} %copy-done.7, f32[3,16,32,256]{3,2,1,0:T(8,128)S(1)} %copy-done.11, f32[3,16,32,256]{3,2,1,0:T(8,128)S(1)} %copy-done.13, bf16[2,256,256]{2,1,0:T(8,128)(2,1)S(1)} %get-tuple-element.57.y_ref.k_ref, ...), custom_call_target="tpu_custom_call" | custom-call | flops 1 | bytes 1 | tf_op jit(solution)/shard_map/halo_adj/pallas_call | solution.py:30
  81.8 0.0 copy-done.3
  81.8 0.0 copy-done.5
  81.8 0.0 copy-done.21
  81.9 7.0 %near.1 = (f32[3,32,32,256]{3,2,1,0:T(8,128)}, f32[2,32,32,256]{3,2,1,0:T(8,128)S(1)}, f32[8,128]{1,0:T(8,128)S(1)}) custom-call(f32[8,128]{1,0:T(8,128)S(1)} %get-tuple-element.50.before_ref, f32[3,32,32,256]{3,2,1,0:T(8,128)S(1)} %copy-done, f32[3,32,32,256]{3,2,1,0:T(8,128)} %vel_ref.7, f32[3,32,32,256]{3,2,1,0:T(8,128)S(1)} %copy-done.3, ...), custom_call_target="tpu_custom_call" | custom-call | flops 1 | bytes 1 | tf_op jit(solution)/shard_map/near/pallas_call | solution.py:30
  88.9 0.0 collective-permute-done.7.far_ref
  88.9 0.0 copy-start.16
  88.9 4.2 %far_vel.1 = (f32[3,32,32,256]{3,2,1,0:T(8,128)}, f32[32,32,256]{2,1,0:T(8,128)S(1)}) custom-call(f32[8,128]{1,0:T(8,128)S(1)} %get-tuple-element.61.token_ref, f32[3,32,32,256]{3,2,1,0:T(8,128)S(1)} %copy-done, f32[3,32,32,256]{3,2,1,0:T(8,128)} %collective-permute-done.7.far_ref, ...), custom_call_target="tpu_custom_call", output_to_operand_aliasing={{0}: (5, {})} | custom-call | flops 1 | bytes 1 | tf_op jit(solution)/shard_map/far_vel/pallas_call | solution.py:30
  93.1 0.0 collective-permute-done.5.up_ref
  93.1 2.9 %collective-permute-done.6.down_ref = f32[3,16,32,256]{3,2,1,0:T(8,128)} collective-permute-done((f32[3,16,32,256]{3,2,1,0:T(8,128)}, f32[3,16,32,256]{3,2,1,0:T(8,128)}, u32[]{:S(2)}, u32[]{:S(2)}) %collective-permute-start.6) | collective-permute-done | bytes 1572896 | tf_op jit(solution)/shard_map/ppermute | solution.py:315
  96.0 0.0 copy-done.16
  96.0 4.1 %z_vel.1 = (f32[3,32,32,256]{3,2,1,0:T(8,128)}, f32[8,128]{1,0:T(8,128)S(1)}) custom-call(f32[3,32,32,256]{3,2,1,0:T(8,128)S(1)} %copy-done, f32[3,16,32,256]{3,2,1,0:T(8,128)} %collective-permute-done.5.up_ref, f32[3,16,32,256]{3,2,1,0:T(8,128)} %collective-permute-done.6.down_ref, ...), custom_call_target="tpu_custom_call", output_to_operand_aliasing={{0}: (5, {})} | custom-call | flops 1 | bytes 1 | tf_op jit(solution)/shard_map/z_vel/pallas_call | solution.py:30
  100.1 0.0 all-to-all-done.terms_ref
  100.1 0.7 share.1
  (16 shorter events, 0.0 us)
Async XLA Ops:
  0.6 2.8 %copy-start = (f32[3,32,32,256]{3,2,1,0:T(8,128)S(1)}, f32[3,32,32,256]{3,2,1,0:T(8,128)}, u32[]{:S(2)}) copy-start(f32[3,32,32,256]{3,2,1,0:T(8,128)} %adj_ref.9) | copy-start | bytes 9437188
  0.6 10.6 %copy-start.24 = (s32[96]{0:T(128)S(1)}, s32[96]{0:T(128)}, u32[]{:S(2)}) copy-start(s32[96]{0:T(128)} %param.15) | copy-start | bytes 1156
  0.7 10.6 %copy-start.23 = (f32[96]{0:T(128)S(1)}, f32[96]{0:T(128)}, u32[]{:S(2)}) copy-start(f32[96]{0:T(128)} %thrust_ref.1) | copy-start | bytes 1156
  0.7 10.6 %copy-start.1 = (f32[96,64,128]{2,1,0:T(8,128)S(1)}, f32[96,64,128]{2,1,0:T(8,128)}, u32[]{:S(2)}) copy-start(f32[96,64,128]{2,1,0:T(8,128)} %weight_ref.1) | copy-start | bytes 9437188
  3.5 14.9 %collective-permute-start = (f32[3,32,32,256]{3,2,1,0:T(8,128)S(1)}, f32[3,32,32,256]{3,2,1,0:T(8,128)S(1)}, u32[]{:S(2)}, u32[]{:S(2)}) collective-permute-start(f32[3,32,32,256]{3,2,1,0:T(8,128)S(1)} %copy-done), channel_id=1, source_target_pairs={{0,1},{1,0},{2,3},{3,2},{4,5},{5,4},{6,7},{7,6},{8,9},{9,8},{10,11... | collective-permute-start | bytes 9437192 | tf_op jit(solution)/shard_map/ppermute | solution.py:320
  3.5 16.6 %collective-permute-start.1 = (f32[3,32,32,256]{3,2,1,0:T(8,128)}, f32[3,32,32,256]{3,2,1,0:T(8,128)S(1)}, u32[]{:S(2)}, u32[]{:S(2)}) collective-permute-start(f32[3,32,32,256]{3,2,1,0:T(8,128)} %vel_ref.7), channel_id=1, source_target_pairs={{0,1},{1,0},{2,3},{3,2},{4,5},{5,4},{6,7},{7,6},{8,9},{9,8},{10,11... | collective-permute-start | bytes 9437192 | tf_op jit(solution)/shard_map/ppermute | solution.py:320
  4.0 46.0 %collective-permute-start.2 = (f32[3,32,32,256]{3,2,1,0:T(8,128)S(1)}, f32[3,32,32,256]{3,2,1,0:T(8,128)S(1)}, u32[]{:S(2)}, u32[]{:S(2)}) collective-permute-start(f32[3,32,32,256]{3,2,1,0:T(8,128)S(1)} %copy-done), channel_id=1, source_target_pairs={{1,2},{2,1},{3,4},{4,3},{5,6},{6,5},{9,10},{10,9},{11,12},{12,11},... | collective-permute-start | bytes 9437192 | tf_op jit(solution)/shard_map/ppermute | solution.py:314
  5.9 38.3 %collective-permute-start.3 = (f32[3,16,32,256]{3,2,1,0:T(8,128)S(1)}, f32[3,16,32,256]{3,2,1,0:T(8,128)S(1)}, u32[]{:S(2)}, u32[]{:S(2)}) collective-permute-start(f32[3,16,32,256]{3,2,1,0:T(8,128)S(1)} %get-tuple-element.44), channel_id=1, source_target_pairs={{0,8},{8,16},{16,24},{24,32},{32,40},{40,48},{48,56},{56,64},{64,7... | collective-permute-start | bytes 4718600 | tf_op jit(solution)/shard_map/ppermute | solution.py:315
  10.0 38.9 %collective-permute-start.4 = (f32[3,16,32,256]{3,2,1,0:T(8,128)S(1)}, f32[3,16,32,256]{3,2,1,0:T(8,128)S(1)}, u32[]{:S(2)}, u32[]{:S(2)}) collective-permute-start(f32[3,16,32,256]{3,2,1,0:T(8,128)S(1)} %get-tuple-element.45), channel_id=1, source_target_pairs={{8,0},{16,8},{24,16},{32,24},{40,32},{48,40},{56,48},{64,56},{72,6... | collective-permute-start | bytes 4718600 | tf_op jit(solution)/shard_map/ppermute | solution.py:315
  11.3 0.8 copy-start.22
  12.1 9.6 %copy-start.17 = (f32[512,512]{1,0:T(8,128)S(1)}, f32[512,512]{1,0:T(8,128)}, u32[]{:S(2)}) copy-start(f32[512,512]{1,0:T(8,128)} %dz_ref.1) | copy-start | bytes 3145732
  12.1 9.6 %copy-start.18 = (f32[256,256]{1,0:T(8,128)S(1)}, f32[256,256]{1,0:T(8,128)}, u32[]{:S(2)}) copy-start(f32[256,256]{1,0:T(8,128)} %dx_ref.1) | copy-start | bytes 786436
  12.1 9.6 %copy-start.19 = (f32[256,256]{1,0:T(8,128)S(1)}, f32[256,256]{1,0:T(8,128)}, u32[]{:S(2)}) copy-start(f32[256,256]{1,0:T(8,128)} %dy_ref) | copy-start | bytes 786436
  18.4 1.7 %copy-start.2 = (f32[3,32,32,256]{3,2,1,0:T(8,128)}, f32[3,32,32,256]{3,2,1,0:T(8,128)S(1)}, u32[]{:S(2)}) copy-start(f32[3,32,32,256]{3,2,1,0:T(8,128)S(1)} %collective-permute-done.adj2_ref) | copy-start | bytes 9437188
  20.0 1.6 %copy-start.4 = (f32[3,32,32,256]{3,2,1,0:T(8,128)}, f32[3,32,32,256]{3,2,1,0:T(8,128)S(1)}, u32[]{:S(2)}) copy-start(f32[3,32,32,256]{3,2,1,0:T(8,128)S(1)} %collective-permute-done.1.vel2_ref) | copy-start | bytes 9437188
  22.7 0.7 copy-start.14
  23.4 0.7 copy-start.20
  32.1 1.7 %copy-start.8 = (f32[3,32,32,256]{3,2,1,0:T(8,128)}, f32[3,32,32,256]{3,2,1,0:T(8,128)S(1)}, u32[]{:S(2)}) copy-start(f32[3,32,32,256]{3,2,1,0:T(8,128)S(1)} %get-tuple-element.58.old_ref) | copy-start | bytes 9437188
  33.8 55.1 %collective-permute-start.7 = (f32[3,32,32,256]{3,2,1,0:T(8,128)}, f32[3,32,32,256]{3,2,1,0:T(8,128)}, u32[]{:S(2)}, u32[]{:S(2)}) collective-permute-start(f32[3,32,32,256]{3,2,1,0:T(8,128)} %vel_ref.7), channel_id=1, source_target_pairs={{1,2},{2,1},{3,4},{4,3},{5,6},{6,5},{9,10},{10,9},{11,12},{12,11},... | collective-permute-start | bytes 9437192 | tf_op jit(solution)/shard_map/ppermute | solution.py:314
  44.2 1.2 %copy-start.10 = (f32[3,16,32,256]{3,2,1,0:T(8,128)}, f32[3,16,32,256]{3,2,1,0:T(8,128)S(1)}, u32[]{:S(2)}) copy-start(f32[3,16,32,256]{3,2,1,0:T(8,128)S(1)} %collective-permute-done.3.up_ref) | copy-start | bytes 4718596
  48.8 1.2 %copy-start.12 = (f32[3,16,32,256]{3,2,1,0:T(8,128)}, f32[3,16,32,256]{3,2,1,0:T(8,128)S(1)}, u32[]{:S(2)}) copy-start(f32[3,16,32,256]{3,2,1,0:T(8,128)S(1)} %collective-permute-done.4.down_ref) | copy-start | bytes 4718596
  50.0 1.7 %copy-start.6 = (f32[3,32,32,256]{3,2,1,0:T(8,128)}, f32[3,32,32,256]{3,2,1,0:T(8,128)S(1)}, u32[]{:S(2)}) copy-start(f32[3,32,32,256]{3,2,1,0:T(8,128)S(1)} %collective-permute-done.2.far_ref) | copy-start | bytes 9437188
  51.7 41.4 %collective-permute-start.5 = (f32[3,16,32,256]{3,2,1,0:T(8,128)}, f32[3,16,32,256]{3,2,1,0:T(8,128)}, u32[]{:S(2)}, u32[]{:S(2)}) collective-permute-start(f32[3,16,32,256]{3,2,1,0:T(8,128)} %get-tuple-element.46), channel_id=1, source_target_pairs={{0,8},{8,16},{16,24},{24,32},{32,40},{40,48},{48,56},{56,64},{64,7... | collective-permute-start | bytes 4718600 | tf_op jit(solution)/shard_map/ppermute | solution.py:315
  56.7 39.3 %collective-permute-start.6 = (f32[3,16,32,256]{3,2,1,0:T(8,128)}, f32[3,16,32,256]{3,2,1,0:T(8,128)}, u32[]{:S(2)}, u32[]{:S(2)}) collective-permute-start(f32[3,16,32,256]{3,2,1,0:T(8,128)} %get-tuple-element.47), channel_id=1, source_target_pairs={{8,0},{16,8},{24,16},{32,24},{40,32},{48,40},{56,48},{64,56},{72,6... | collective-permute-start | bytes 4718600 | tf_op jit(solution)/shard_map/ppermute | solution.py:315
  58.0 42.2 %all-to-all-start = ((f32[128,1,128]{2,1,0:T(1,128)}), f32[128,1,128]{2,1,0:T(1,128)S(1)}, u32[]{:S(2)}, u32[]{:S(2)}) async-start(f32[128,1,128]{2,1,0:T(1,128)} %bitcast.1), calls=%async_computation | async-start | bytes 131072 | tf_op jit(solution)/shard_map/all_to_all | solution.py:326
  68.3 1.9 %copy-start.7 = (f32[3,32,32,256]{3,2,1,0:T(8,128)S(1)}, f32[3,32,32,256]{3,2,1,0:T(8,128)}, u32[]{:S(2)}) copy-start(f32[3,32,32,256]{3,2,1,0:T(8,128)} %copy-done.6) | copy-start | bytes 9437188
  70.2 1.9 %copy-start.9 = (f32[3,32,32,256]{3,2,1,0:T(8,128)S(1)}, f32[3,32,32,256]{3,2,1,0:T(8,128)}, u32[]{:S(2)}) copy-start(f32[3,32,32,256]{3,2,1,0:T(8,128)} %copy-done.8) | copy-start | bytes 9437188
  72.1 1.4 %copy-start.11 = (f32[3,16,32,256]{3,2,1,0:T(8,128)S(1)}, f32[3,16,32,256]{3,2,1,0:T(8,128)}, u32[]{:S(2)}) copy-start(f32[3,16,32,256]{3,2,1,0:T(8,128)} %copy-done.10) | copy-start | bytes 4718596
  73.5 1.4 %copy-start.13 = (f32[3,16,32,256]{3,2,1,0:T(8,128)S(1)}, f32[3,16,32,256]{3,2,1,0:T(8,128)}, u32[]{:S(2)}) copy-start(f32[3,16,32,256]{3,2,1,0:T(8,128)} %copy-done.12) | copy-start | bytes 4718596
  74.9 0.9 copy-start.15
  75.9 6.0 %copy-start.3 = (f32[3,32,32,256]{3,2,1,0:T(8,128)S(1)}, f32[3,32,32,256]{3,2,1,0:T(8,128)}, u32[]{:S(2)}) copy-start(f32[3,32,32,256]{3,2,1,0:T(8,128)} %copy-done.2) | copy-start | bytes 9437188
  75.9 6.0 %copy-start.5 = (f32[3,32,32,256]{3,2,1,0:T(8,128)S(1)}, f32[3,32,32,256]{3,2,1,0:T(8,128)}, u32[]{:S(2)}) copy-start(f32[3,32,32,256]{3,2,1,0:T(8,128)} %copy-done.4) | copy-start | bytes 9437188
  75.9 6.0 %copy-start.21 = (bf16[2,128,256]{2,1,0:T(8,128)(2,1)S(1)}, bf16[2,128,256]{2,1,0:T(8,128)(2,1)}, u32[]{:S(2)}) copy-start(bf16[2,128,256]{2,1,0:T(8,128)(2,1)} %copy-done.20) | copy-start | bytes 393220
  88.9 7.1 %copy-start.16 = (bf16[2,256,256]{2,1,0:T(8,128)(2,1)S(1)}, bf16[2,256,256]{2,1,0:T(8,128)(2,1)}, u32[]{:S(2)}) copy-start(bf16[2,256,256]{2,1,0:T(8,128)(2,1)} %copy-done.14) | copy-start | bytes 786436

commit v4 on v3

--- a/solution.py
+++ b/solution.py
@@ -24,6 +24,10 @@
 
 def resident(v):
     return pltpu.with_memory_space_constraint(v, pltpu.VMEM)
+
+
+def in_hbm(v):
+    return pltpu.with_memory_space_constraint(v, pltpu.HBM)
 
 
 def call(kernel, operands, outs, name, limit=12, **kw):
@@ -204,34 +208,45 @@
     return jnp.concatenate([up_ref[c, :, at, :].reshape(128, 256), down_ref[c, :, at, :].reshape(128, 256)], axis=0)
 
 
-def adj_kernel(vel_ref, far_ref, up_ref, down_ref, y_ref, z_ref, old_ref, out_ref):
-    def planes(g, _):
-        at = pl.ds(pl.multiple_of(g * 8, 8), 8)
+def adj_kernel(vel_ref, far_ref, up_ref, down_ref, y_ref, z_ref, old_ref, out_ref, vel, far, upper, lower, sems):
+    groups = [pl.ds(8 * g, 8) for g in range(SZ // 8)]
+    parts = lambda at: ((far_ref.at[:, at], far.at[:, at]), (old_ref.at[:, at], out_ref.at[:, at]), (vel_ref.at[1, at], vel.at[0, at]))
+    loads = [[copy_of(*ends, sems.at[i, g]) for i, ends in enumerate(parts(at))] for g, at in enumerate(groups)]
+    ends = ((vel_ref.at[2], vel.at[1]), (up_ref, upper), (down_ref, lower))
+    loads.append([copy_of(*pair, sems.at[3, i]) for i, pair in enumerate(ends)])
+    for copies in loads:
+        for copy in copies:
+            copy.start()
+    for at, copies in zip(groups, loads):
+        for copy in copies:
+            copy.wait()
         field = lambda ref, c: ref[c, at, :, :].reshape(256, 256)
         for c in range(3):
-            total = field(vel_ref, 1) * mix(y_ref[0], y_ref[1], field(far_ref, c))
-            out_ref[c, at, :, :] = (field(old_ref, c) + STEP * total).reshape(8, SY, NX)
-        return 0
-
-    def lines(yb, _):
-        at = pl.ds(pl.multiple_of(yb * 8, 8), 8)
+            total = field(vel, 0) * mix(y_ref[0], y_ref[1], field(far, c))
+            out_ref[c, at, :, :] = (field(out_ref, c) + STEP * total).reshape(8, SY, NX)
+    for copy in loads[-1]:
+        copy.wait()
+    for at in groups:
         field = lambda ref, c: ref[c, :, at, :].reshape(256, 256)
         for c in range(3):
-            total = field(vel_ref, 2) * mix(z_ref[0], z_ref[1], side_lines(up_ref, down_ref, c, at))
+            total = field(vel, 1) * mix(z_ref[0], z_ref[1], side_lines(upper, lower, c, at))
             out_ref[c, :, at, :] = (field(out_ref, c) + STEP * total).reshape(SZ, 8, NX)
-        return 0
-
-    lax.fori_loop(0, SZ // 8, planes, 0)
-    lax.fori_loop(0, SY // 8, lines, 0)
-
-
-def near_kernel(before_ref, adj_ref, vel_ref, adj2_ref, vel2_ref, k_ref, old_ref, done_ref, rest_ref, token_ref, stage, sem):
+
+
+def near_kernel(before_ref, adj_ref, vel_ref, adj2_ref, vel2_ref, k_ref, old_ref, done_ref, rest_ref, token_ref, adj2, vel2, stage, sems):
     token_ref[...] = before_ref[...]
-
-    def planes(g, _):
-        at = pl.ds(pl.multiple_of(g * 4, 4), 4)
+    groups = [pl.ds(4 * g, 4) for g in range(SZ // 4)]
+    loads = []
+    for g, at in enumerate(groups):
+        loads.append((copy_of(adj2_ref.at[:, at], adj2.at[:, at], sems.at[0, g]), copy_of(vel2_ref.at[:, at], vel2.at[:, at], sems.at[1, g])))
+        for copy in loads[-1]:
+            copy.start()
+    both = jnp.concatenate([k_ref[0], k_ref[1]], axis=0)
+    stores = []
+    for g, at in enumerate(groups):
+        for copy in loads[g]:
+            copy.wait()
         field = lambda ref, c: ref[c, at, :, :].reshape(128, 256)
-        both = jnp.concatenate([k_ref[0], k_ref[1]], axis=0)
 
         def deriv(one, two, c):
             hi, lo = split(chip_lines(one, two, c, at))
@@ -240,9 +255,9 @@
 
         stretch = jnp.zeros((128, 256), F32)
         for c in range(3):
-            stretch += field(adj_ref, c) * deriv(vel_ref, vel2_ref, c)
-        for c in range(3):
-            total = field(vel_ref, 1) * deriv(adj_ref, adj2_ref, c)
+            stretch += field(adj_ref, c) * deriv(vel_ref, vel2, c)
+        for c in range(3):
+            total = field(vel_ref, 1) * deriv(adj_ref, adj2, c)
             if c == 1:
                 total -= stretch
             total = (field(old_ref, c) + STEP * total).reshape(4, SY, NX)
@@ -250,12 +265,10 @@
                 stage[at, :, :] = total
             else:
                 rest_ref[c - 1, at, :, :] = total
-        return 0
-
-    lax.fori_loop(0, SZ // 4, planes, 0)
-    store = copy_of(stage, done_ref.at[0], sem)
-    store.start()
-    store.wait()
+        stores.append(copy_of(stage.at[at], done_ref.at[0, at], sems.at[2, g]))
+        stores[-1].start()
+    for copy in stores:
+        copy.wait()
 
 
 def far_kernel(token_ref, adj_ref, far_ref, k_ref, rest_ref, done_ref, out_ref, last_ref, stage, sems):
@@ -321,13 +334,13 @@
     adj, vel = resident(adjoint), resident(velocity)
     owner = jnp.broadcast_to(jnp.pad(turbine_owner, (0, 128 - TURB), constant_values=-1)[None], (8, 128))
     force, grad = turbines(rotor_blocks.T, thrust, owner, adj, vel, resident(disk_weight))
-    deriv_y, grad, *near = barrier((deriv_y, grad, *near))
+    deriv_y, grad, vel_upper, vel_lower, *near = barrier((deriv_y, grad, velocity[:, HZ:], velocity[:, :HZ], *near))
     m_x, m_z, m_side, m_far, m_near, token = prep(deriv_x, deriv_y, deriv_z)
     grad = lax.all_to_all(grad.reshape(n_wide * n_narrow, 1, 128), ("wide", "narrow"), split_axis=0, concat_axis=0, tiled=True)
     out, token = call(
         xz_kernel,
         (token, adj, vel, force, m_x, m_z),
-        [shape, small],
+        [pltpu.HBM(adjoint.shape, F32), small],
         "xz",
         16,
         in_specs=[VMEM] * 6,
@@ -337,21 +350,31 @@
     token, gated = barrier((token, velocity))
     vel_far = far(gated)
     out, upper, lower, adj_far, *adj_sides = barrier(
-        (out, velocity[:, HZ:], velocity[:, :HZ], adj_far, *adj_sides)
+        (out, vel_upper, vel_lower, adj_far, *adj_sides)
     )
 
     vel_sides = sides(upper, lower)
     adj, vel = resident(adjoint), resident(velocity)
-    operands = (vel, *[resident(v) for v in (adj_far, *adj_sides)], m_far, m_side, resident(out))
-    out = call(adj_kernel, operands, field, "halo_adj", in_specs=[VMEM] * 7, out_specs=VMEM)
+    two, side = pltpu.VMEM((2, SZ, SY, NX), F32), pltpu.VMEM((3, HZ, SY, NX), F32)
+    out = call(
+        adj_kernel,
+        (*[in_hbm(v) for v in (velocity, adj_far, *adj_sides)], m_far, m_side, in_hbm(out)),
+        field,
+        "halo_adj",
+        16,
+        in_specs=[HBM] * 4 + [VMEM] * 2 + [HBM],
+        out_specs=VMEM,
+        scratch_shapes=[two, field, side, side, dma((4, 4))],
+    )
     out, rest, token = call(
         near_kernel,
-        (token, adj, vel, *[resident(v) for v in near], m_near, out),
+        (token, adj, vel, *[in_hbm(v) for v in near], m_near, out),
         [shape, pltpu.VMEM((2, SZ, SY, NX), F32), small],
         "near",
-        in_specs=[VMEM] * 7,
+        20,
+        in_specs=[VMEM] * 3 + [HBM] * 2 + [VMEM] * 2,
         out_specs=[HBM, VMEM, VMEM],
-        scratch_shapes=[pltpu.VMEM((SZ, SY, NX), F32), dma(())],
+        scratch_shapes=[field, field, pltpu.VMEM((SZ, SY, NX), F32), dma((3, 8))],
     )
     token, vel_far = barrier((token, vel_far))
     plane = pltpu.VMEM((SZ, SY, NX), F32)

time: 101 us -> 98.4 us (0.974)
  local copies, waits for them, and re-layouts: 25.5 us -> 10.5 us
  waiting for transfers between devices: 9.57 us -> 20.9 us
    unnamed x50 -> x36, local copies, waits for them, and re-layouts: 19.2 us -> 4.14 us
    ppermute x2, waiting for transfers between devices: 3.21 us -> 10.9 us  [on_device(): lax.ppermute(upper, 'wide', up)]
    ppermute x2, waiting for transfers between devices: 6.34 us -> 9.89 us  [on_device(): lax.ppermute(lower, 'wide', down)]
  transfers between devices with their start and end apart: 9 -> 9, of which waited for: 3 -> 4; matrix products, arithmetic and copies ran while one was open for 4% -> 4% of each run, Pallas kernels for 36% -> 38%
where the time goes in v4:
time: 98.4 us; the launch traced here: 98 us
  Pallas kernels  38 us (39%)
  starting transfers between devices  27.7 us (28%)
  waiting for transfers between devices  20.9 us (21%)
  local copies, waits for them, and re-layouts  10.5 us (11%)
    pallas_call x8, Pallas kernels, call(): pl.pallas_call(kernel, out_shape=outs, compiler_params=pltpu.CompilerPara...  38 us
    ppermute x2, waiting for transfers between devices, on_device(): lax.ppermute(upper, 'wide', up)  10.9 us
    all_to_all x1, starting transfers between devices, on_device(): lax.all_to_all(grad.reshape(n_wide * n_narrow, 1, 128), ('wide', 'narrow'...  10.4 us
    ppermute x2, waiting for transfers between devices, on_device(): lax.ppermute(lower, 'wide', down)  9.89 us
    ppermute x2, starting transfers between devices, on_device(): lax.ppermute(upper, 'wide', up)  8.96 us
    ppermute x2, starting transfers between devices, on_device(): far = lambda v: lax.ppermute(v, 'narrow', across)  5.26 us
    unnamed x36, local copies, waits for them, and re-layouts  4.14 us
    slice x1, local copies, waits for them, and re-layouts, on_device(): velocity[:, :HZ]  4.05 us
  transfers between devices with their start and end apart: 9, of which 4 were waited for; matrix products, arithmetic and copies ran while one was open for 4% of the time, Pallas kernels for 38%

profile of v4, /device:TPU:2, one launch (start us, length us, event | category | flops | bytes accessed | tf_op | source)
XLA Modules:
  0.0 98.0 jit_solution(8853794430977933629)
XLA Ops:
  0.6 0.0 copy-start
  0.6 0.0 copy-start.17
  0.7 0.0 copy-start.11
  0.7 0.0 copy-start.1
  0.7 2.3 %fusion = (f32[3,16,32,256]{3,2,1,0:T(8,128)S(1)}, f32[3,16,32,256]{3,2,1,0:T(8,128)S(1)}) fusion(f32[3,32,32,256]{3,2,1,0:T(8,128)} %adj_ref.9), kind=kLoop, calls=%fused_computation | loop fusion | bytes 6291456 | tf_op jit(solution)/shard_map/slice | solution.py:330
  3.0 0.5 copy-done
  3.5 0.0 collective-permute-start
  3.5 0.5 collective-permute-start.1
  4.0 2.0 %collective-permute-start.2 = (f32[3,32,32,256]{3,2,1,0:T(8,128)S(1)}, f32[3,32,32,256]{3,2,1,0:T(8,128)S(1)}, u32[]{:S(2)}, u32[]{:S(2)}) collective-permute-start(f32[3,32,32,256]{3,2,1,0:T(8,128)S(1)} %copy-done), channel_id=1, source_target_pairs={{1,2},{2,1},{3,4},{4,3},{5,6},{6,5},{9,10},{10,9},{11,12},{12,11},... | collective-permute-start | bytes 9437192 | tf_op jit(solution)/shard_map/ppermute | solution.py:327
  5.9 4.0 %collective-permute-start.3 = (f32[3,16,32,256]{3,2,1,0:T(8,128)S(1)}, f32[3,16,32,256]{3,2,1,0:T(8,128)S(1)}, u32[]{:S(2)}, u32[]{:S(2)}) collective-permute-start(f32[3,16,32,256]{3,2,1,0:T(8,128)S(1)} %get-tuple-element.48), channel_id=1, source_target_pairs={{0,8},{8,16},{16,24},{24,32},{32,40},{40,48},{48,56},{56,64},{64,7... | collective-permute-start | bytes 4718600 | tf_op jit(solution)/shard_map/ppermute | solution.py:328
  10.0 1.3 %collective-permute-start.4 = (f32[3,16,32,256]{3,2,1,0:T(8,128)S(1)}, f32[3,16,32,256]{3,2,1,0:T(8,128)S(1)}, u32[]{:S(2)}, u32[]{:S(2)}) collective-permute-start(f32[3,16,32,256]{3,2,1,0:T(8,128)S(1)} %get-tuple-element.49), channel_id=1, source_target_pairs={{8,0},{16,8},{24,16},{32,24},{40,32},{48,40},{56,48},{64,56},{72,6... | collective-permute-start | bytes 4718600 | tf_op jit(solution)/shard_map/ppermute | solution.py:328
  11.3 0.0 copy-done.17
  11.3 0.0 copy-done.11
  11.3 0.0 copy-done.1
  11.3 0.0 copy-start.10
  11.3 0.7 copy-done.10
  12.1 6.3 %turbines.1 = (f32[32,32,256]{2,1,0:T(8,128)S(1)}, f32[128,128]{1,0:T(8,128)}) custom-call(s32[64,96]{1,0:T(8,128)S(1)} %bitcast.2, f32[96]{0:T(128)S(1)} %copy-done.11, s32[8,128]{1,0:T(8,128)S(1)} %broadcast_in_dim.2.owner_ref, f32[3,32,32,256]{3,2,1,0:T(8,128)S(1)} %copy-done, f32[3,32,32,256]{3,2,1,0:T(8,128)} %vel_ref.7, f32[96,64,128]{2,1,0:T(8,128)S(1)} %copy-done.1), custom_call_target="tpu_custom_call" | custom-call | flops 1 | bytes 1 | tf_op jit(solution)/shard_map/turbines/pallas_call | solution.py:34
  18.3 0.0 copy-start.5
  18.3 0.0 copy-start.6
  18.3 0.0 copy-start.7
  18.3 4.0 %fusion.1 = (f32[3,16,32,256]{3,2,1,0:T(8,128)}, f32[3,16,32,256]{3,2,1,0:T(8,128)}) fusion(f32[3,32,32,256]{3,2,1,0:T(8,128)} %vel_ref.7), kind=kLoop, calls=%fused_computation.1 | loop fusion | bytes 6291456 | tf_op jit(solution)/shard_map/slice | solution.py:337
  22.4 0.0 collective-permute-done.adj2_ref
  22.4 0.0 copy-start.12
  22.4 0.0 collective-permute-done.1.vel2_ref
  22.4 0.0 copy-start.13
  22.4 0.0 copy-done.5
  22.4 0.0 copy-done.6
  22.4 0.0 copy-done.7
  22.4 1.0 prep.1
  23.4 0.0 copy-start.2
  23.4 1.2 %copy-done.2 = bf16[2,256,256]{2,1,0:T(8,128)(2,1)} copy-done((bf16[2,256,256]{2,1,0:T(8,128)(2,1)}, bf16[2,256,256]{2,1,0:T(8,128)(2,1)S(1)}, u32[]{:S(2)}) %copy-start.2) | copy-done | bytes 262168
  24.6 0.0 copy-start.8
  24.6 0.7 copy-done.8
  25.3 8.1 %xz.1 = (f32[3,32,32,256]{3,2,1,0:T(8,128)}, f32[8,128]{1,0:T(8,128)S(1)}) custom-call(f32[8,128]{1,0:T(8,128)S(1)} %get-tuple-element.41.token_ref, f32[3,32,32,256]{3,2,1,0:T(8,128)S(1)} %copy-done, f32[3,32,32,256]{3,2,1,0:T(8,128)} %vel_ref.7, f32[32,32,256]{2,1,0:T(8,128)S(1)} %get-tuple-element.42.force_ref, ...), custom_call_target="tpu_custom_call" | custom-call | flops 1 | bytes 1 | tf_op jit(solution)/shard_map/xz/pallas_call | solution.py:34
  33.4 3.3 %collective-permute-start.7 = (f32[3,32,32,256]{3,2,1,0:T(8,128)}, f32[3,32,32,256]{3,2,1,0:T(8,128)}, u32[]{:S(2)}, u32[]{:S(2)}) collective-permute-start(f32[3,32,32,256]{3,2,1,0:T(8,128)} %vel_ref.7), channel_id=1, source_target_pairs={{1,2},{2,1},{3,4},{4,3},{5,6},{6,5},{9,10},{10,9},{11,12},{12,11},... | collective-permute-start | bytes 9437192 | tf_op jit(solution)/shard_map/ppermute | solution.py:327
  36.7 7.5 %collective-permute-done.3.up_ref = f32[3,16,32,256]{3,2,1,0:T(8,128)S(1)} collective-permute-done((f32[3,16,32,256]{3,2,1,0:T(8,128)S(1)}, f32[3,16,32,256]{3,2,1,0:T(8,128)S(1)}, u32[]{:S(2)}, u32[]{:S(2)}) %collective-permute-start.3) | collective-permute-done | bytes 1572896 | tf_op jit(solution)/shard_map/ppermute | solution.py:328
  44.2 0.0 copy-start.15
  44.2 4.6 %collective-permute-done.4.down_ref = f32[3,16,32,256]{3,2,1,0:T(8,128)S(1)} collective-permute-done((f32[3,16,32,256]{3,2,1,0:T(8,128)S(1)}, f32[3,16,32,256]{3,2,1,0:T(8,128)S(1)}, u32[]{:S(2)}, u32[]{:S(2)}) %collective-permute-start.4) | collective-permute-done | bytes 1572896 | tf_op jit(solution)/shard_map/ppermute | solution.py:328
  48.8 0.0 copy-start.16
  48.8 0.0 collective-permute-done.2.far_ref
  48.8 0.0 copy-done.12
  48.8 0.0 copy-start.14
  48.8 0.0 copy-done.13
  48.8 5.0 %collective-permute-start.5 = (f32[3,16,32,256]{3,2,1,0:T(8,128)}, f32[3,16,32,256]{3,2,1,0:T(8,128)}, u32[]{:S(2)}, u32[]{:S(2)}) collective-permute-start(f32[3,16,32,256]{3,2,1,0:T(8,128)} %get-tuple-element.50), channel_id=1, source_target_pairs={{0,8},{8,16},{16,24},{24,32},{32,40},{40,48},{48,56},{56,64},{64,7... | collective-permute-start | bytes 4718600 | tf_op jit(solution)/shard_map/ppermute | solution.py:328
  53.8 0.0 copy-done.14
  53.8 1.3 %collective-permute-start.6 = (f32[3,16,32,256]{3,2,1,0:T(8,128)}, f32[3,16,32,256]{3,2,1,0:T(8,128)}, u32[]{:S(2)}, u32[]{:S(2)}) collective-permute-start(f32[3,16,32,256]{3,2,1,0:T(8,128)} %get-tuple-element.51), channel_id=1, source_target_pairs={{8,0},{16,8},{24,16},{32,24},{40,32},{48,40},{56,48},{64,56},{72,6... | collective-permute-start | bytes 4718600 | tf_op jit(solution)/shard_map/ppermute | solution.py:328
  55.1 0.0 copy-done.15
  55.1 0.0 copy-done.16
  55.1 10.4 %all-to-all-start = ((f32[128,1,128]{2,1,0:T(1,128)}), f32[128,1,128]{2,1,0:T(1,128)S(1)}, u32[]{:S(2)}, u32[]{:S(2)}) async-start(f32[128,1,128]{2,1,0:T(1,128)} %bitcast.1), calls=%async_computation | async-start | bytes 131072 | tf_op jit(solution)/shard_map/all_to_all | solution.py:339
  65.5 0.0 copy-start.3
  65.5 0.9 copy-done.3
  66.4 0.0 copy-start.9
  66.4 6.0 %halo_adj.1.old_ref = f32[3,32,32,256]{3,2,1,0:T(8,128)S(1)} custom-call(f32[3,32,32,256]{3,2,1,0:T(8,128)} %vel_ref.7, f32[3,32,32,256]{3,2,1,0:T(8,128)} %copy-done.14, f32[3,16,32,256]{3,2,1,0:T(8,128)} %copy-done.15, f32[3,16,32,256]{3,2,1,0:T(8,128)} %copy-done.16, bf16[2,256,256]{2,1,0:T(8,128)(2,1)S(1)} %get-tuple-element.61.y_ref.k_ref, ...), custom_call_target="tpu_custom_call" | custom-call | flops 1 | bytes 1 | tf_op jit(solution)/shard_map/halo_adj/pallas_call | solution.py:34
  72.4 0.0 copy-done.9
  72.5 7.7 %near.1 = (f32[3,32,32,256]{3,2,1,0:T(8,128)}, f32[2,32,32,256]{3,2,1,0:T(8,128)S(1)}, f32[8,128]{1,0:T(8,128)S(1)}) custom-call(f32[8,128]{1,0:T(8,128)S(1)} %get-tuple-element.54.before_ref, f32[3,32,32,256]{3,2,1,0:T(8,128)S(1)} %copy-done, f32[3,32,32,256]{3,2,1,0:T(8,128)} %vel_ref.7, f32[3,32,32,256]{3,2,1,0:T(8,128)} %copy-done.12, ...), custom_call_target="tpu_custom_call" | custom-call | flops 1 | bytes 1 | tf_op jit(solution)/shard_map/near/pallas_call | solution.py:34
  80.2 0.0 collective-permute-done.7.far_ref
  80.2 0.0 copy-start.4
  80.2 4.2 %far_vel.1 = (f32[3,32,32,256]{3,2,1,0:T(8,128)}, f32[32,32,256]{2,1,0:T(8,128)S(1)}) custom-call(f32[8,128]{1,0:T(8,128)S(1)} %get-tuple-element.65.token_ref, f32[3,32,32,256]{3,2,1,0:T(8,128)S(1)} %copy-done, f32[3,32,32,256]{3,2,1,0:T(8,128)} %collective-permute-done.7.far_ref, ...), custom_call_target="tpu_custom_call", output_to_operand_aliasing={{0}: (5, {})} | custom-call | flops 1 | bytes 1 | tf_op jit(solution)/shard_map/far_vel/pallas_call | solution.py:34
  84.4 3.4 %collective-permute-done.5.up_ref = f32[3,16,32,256]{3,2,1,0:T(8,128)} collective-permute-done((f32[3,16,32,256]{3,2,1,0:T(8,128)}, f32[3,16,32,256]{3,2,1,0:T(8,128)}, u32[]{:S(2)}, u32[]{:S(2)}) %collective-permute-start.5) | collective-permute-done | bytes 1572896 | tf_op jit(solution)/shard_map/ppermute | solution.py:328
  87.9 5.3 %collective-permute-done.6.down_ref = f32[3,16,32,256]{3,2,1,0:T(8,128)} collective-permute-done((f32[3,16,32,256]{3,2,1,0:T(8,128)}, f32[3,16,32,256]{3,2,1,0:T(8,128)}, u32[]{:S(2)}, u32[]{:S(2)}) %collective-permute-start.6) | collective-permute-done | bytes 1572896 | tf_op jit(solution)/shard_map/ppermute | solution.py:328
  93.2 0.0 copy-done.4
  93.2 4.1 %z_vel.1 = (f32[3,32,32,256]{3,2,1,0:T(8,128)}, f32[8,128]{1,0:T(8,128)S(1)}) custom-call(f32[3,32,32,256]{3,2,1,0:T(8,128)S(1)} %copy-done, f32[3,16,32,256]{3,2,1,0:T(8,128)} %collective-permute-done.5.up_ref, f32[3,16,32,256]{3,2,1,0:T(8,128)} %collective-permute-done.6.down_ref, ...), custom_call_target="tpu_custom_call", output_to_operand_aliasing={{0}: (5, {})} | custom-call | flops 1 | bytes 1 | tf_op jit(solution)/shard_map/z_vel/pallas_call | solution.py:34
  97.2 0.0 all-to-all-done.terms_ref
  97.3 0.7 share.1
  (2 shorter events, 0.0 us)
Async XLA Ops:
  0.6 2.8 %copy-start = (f32[3,32,32,256]{3,2,1,0:T(8,128)S(1)}, f32[3,32,32,256]{3,2,1,0:T(8,128)}, u32[]{:S(2)}) copy-start(f32[3,32,32,256]{3,2,1,0:T(8,128)} %adj_ref.9) | copy-start | bytes 9437188
  0.6 10.6 %copy-start.17 = (s32[96]{0:T(128)S(1)}, s32[96]{0:T(128)}, u32[]{:S(2)}) copy-start(s32[96]{0:T(128)} %param.15) | copy-start | bytes 1156
  0.7 10.6 %copy-start.11 = (f32[96]{0:T(128)S(1)}, f32[96]{0:T(128)}, u32[]{:S(2)}) copy-start(f32[96]{0:T(128)} %thrust_ref.1) | copy-start | bytes 1156
  0.7 10.6 %copy-start.1 = (f32[96,64,128]{2,1,0:T(8,128)S(1)}, f32[96,64,128]{2,1,0:T(8,128)}, u32[]{:S(2)}) copy-start(f32[96,64,128]{2,1,0:T(8,128)} %weight_ref.1) | copy-start | bytes 9437188
  3.5 18.9 %collective-permute-start = (f32[3,32,32,256]{3,2,1,0:T(8,128)S(1)}, f32[3,32,32,256]{3,2,1,0:T(8,128)S(1)}, u32[]{:S(2)}, u32[]{:S(2)}) collective-permute-start(f32[3,32,32,256]{3,2,1,0:T(8,128)S(1)} %copy-done), channel_id=1, source_target_pairs={{0,1},{1,0},{2,3},{3,2},{4,5},{5,4},{6,7},{7,6},{8,9},{9,8},{10,11... | collective-permute-start | bytes 9437192 | tf_op jit(solution)/shard_map/ppermute | solution.py:333
  3.5 18.9 %collective-permute-start.1 = (f32[3,32,32,256]{3,2,1,0:T(8,128)}, f32[3,32,32,256]{3,2,1,0:T(8,128)S(1)}, u32[]{:S(2)}, u32[]{:S(2)}) collective-permute-start(f32[3,32,32,256]{3,2,1,0:T(8,128)} %vel_ref.7), channel_id=1, source_target_pairs={{0,1},{1,0},{2,3},{3,2},{4,5},{5,4},{6,7},{7,6},{8,9},{9,8},{10,11... | collective-permute-start | bytes 9437192 | tf_op jit(solution)/shard_map/ppermute | solution.py:333
  4.0 44.8 %collective-permute-start.2 = (f32[3,32,32,256]{3,2,1,0:T(8,128)S(1)}, f32[3,32,32,256]{3,2,1,0:T(8,128)S(1)}, u32[]{:S(2)}, u32[]{:S(2)}) collective-permute-start(f32[3,32,32,256]{3,2,1,0:T(8,128)S(1)} %copy-done), channel_id=1, source_target_pairs={{1,2},{2,1},{3,4},{4,3},{5,6},{6,5},{9,10},{10,9},{11,12},{12,11},... | collective-permute-start | bytes 9437192 | tf_op jit(solution)/shard_map/ppermute | solution.py:327
  5.9 38.3 %collective-permute-start.3 = (f32[3,16,32,256]{3,2,1,0:T(8,128)S(1)}, f32[3,16,32,256]{3,2,1,0:T(8,128)S(1)}, u32[]{:S(2)}, u32[]{:S(2)}) collective-permute-start(f32[3,16,32,256]{3,2,1,0:T(8,128)S(1)} %get-tuple-element.48), channel_id=1, source_target_pairs={{0,8},{8,16},{16,24},{24,32},{32,40},{40,48},{48,56},{56,64},{64,7... | collective-permute-start | bytes 4718600 | tf_op jit(solution)/shard_map/ppermute | solution.py:328
  10.0 38.9 %collective-permute-start.4 = (f32[3,16,32,256]{3,2,1,0:T(8,128)S(1)}, f32[3,16,32,256]{3,2,1,0:T(8,128)S(1)}, u32[]{:S(2)}, u32[]{:S(2)}) collective-permute-start(f32[3,16,32,256]{3,2,1,0:T(8,128)S(1)} %get-tuple-element.49), channel_id=1, source_target_pairs={{8,0},{16,8},{24,16},{32,24},{40,32},{48,40},{56,48},{64,56},{72,6... | collective-permute-start | bytes 4718600 | tf_op jit(solution)/shard_map/ppermute | solution.py:328
  11.3 0.8 copy-start.10
  18.3 4.1 %copy-start.5 = (f32[512,512]{1,0:T(8,128)S(1)}, f32[512,512]{1,0:T(8,128)}, u32[]{:S(2)}) copy-start(f32[512,512]{1,0:T(8,128)} %dz_ref.1) | copy-start | bytes 3145732
  18.3 4.1 %copy-start.6 = (f32[256,256]{1,0:T(8,128)S(1)}, f32[256,256]{1,0:T(8,128)}, u32[]{:S(2)}) copy-start(f32[256,256]{1,0:T(8,128)} %dx_ref.1) | copy-start | bytes 786436
  18.3 4.1 %copy-start.7 = (f32[256,256]{1,0:T(8,128)S(1)}, f32[256,256]{1,0:T(8,128)}, u32[]{:S(2)}) copy-start(f32[256,256]{1,0:T(8,128)} %dy_ref) | copy-start | bytes 786436
  22.4 26.4 %copy-start.12 = (f32[3,32,32,256]{3,2,1,0:T(8,128)}, f32[3,32,32,256]{3,2,1,0:T(8,128)S(1)}, u32[]{:S(2)}) copy-start(f32[3,32,32,256]{3,2,1,0:T(8,128)S(1)} %collective-permute-done.adj2_ref) | copy-start | bytes 9437188
  22.4 26.4 %copy-start.13 = (f32[3,32,32,256]{3,2,1,0:T(8,128)}, f32[3,32,32,256]{3,2,1,0:T(8,128)S(1)}, u32[]{:S(2)}) copy-start(f32[3,32,32,256]{3,2,1,0:T(8,128)S(1)} %collective-permute-done.1.vel2_ref) | copy-start | bytes 9437188
  23.4 1.2 %copy-start.2 = (bf16[2,256,256]{2,1,0:T(8,128)(2,1)}, bf16[2,256,256]{2,1,0:T(8,128)(2,1)S(1)}, u32[]{:S(2)}) copy-start(bf16[2,256,256]{2,1,0:T(8,128)(2,1)S(1)} %get-tuple-element.52.z_ref.k_ref) | copy-start | bytes 786436
  24.6 0.7 copy-start.8
  33.4 46.8 %collective-permute-start.7 = (f32[3,32,32,256]{3,2,1,0:T(8,128)}, f32[3,32,32,256]{3,2,1,0:T(8,128)}, u32[]{:S(2)}, u32[]{:S(2)}) collective-permute-start(f32[3,32,32,256]{3,2,1,0:T(8,128)} %vel_ref.7), channel_id=1, source_target_pairs={{1,2},{2,1},{3,4},{4,3},{5,6},{6,5},{9,10},{10,9},{11,12},{12,11},... | collective-permute-start | bytes 9437192 | tf_op jit(solution)/shard_map/ppermute | solution.py:327
  44.2 10.9 %copy-start.15 = (f32[3,16,32,256]{3,2,1,0:T(8,128)}, f32[3,16,32,256]{3,2,1,0:T(8,128)S(1)}, u32[]{:S(2)}) copy-start(f32[3,16,32,256]{3,2,1,0:T(8,128)S(1)} %collective-permute-done.3.up_ref) | copy-start | bytes 4718596
  48.8 6.3 %copy-start.16 = (f32[3,16,32,256]{3,2,1,0:T(8,128)}, f32[3,16,32,256]{3,2,1,0:T(8,128)S(1)}, u32[]{:S(2)}) copy-start(f32[3,16,32,256]{3,2,1,0:T(8,128)S(1)} %collective-permute-done.4.down_ref) | copy-start | bytes 4718596
  48.8 5.0 %copy-start.14 = (f32[3,32,32,256]{3,2,1,0:T(8,128)}, f32[3,32,32,256]{3,2,1,0:T(8,128)S(1)}, u32[]{:S(2)}) copy-start(f32[3,32,32,256]{3,2,1,0:T(8,128)S(1)} %collective-permute-done.2.far_ref) | copy-start | bytes 9437188
  48.8 39.0 %collective-permute-start.5 = (f32[3,16,32,256]{3,2,1,0:T(8,128)}, f32[3,16,32,256]{3,2,1,0:T(8,128)}, u32[]{:S(2)}, u32[]{:S(2)}) collective-permute-start(f32[3,16,32,256]{3,2,1,0:T(8,128)} %get-tuple-element.50), channel_id=1, source_target_pairs={{0,8},{8,16},{16,24},{24,32},{32,40},{40,48},{48,56},{56,64},{64,7... | collective-permute-start | bytes 4718600 | tf_op jit(solution)/shard_map/ppermute | solution.py:328
  53.8 39.3 %collective-permute-start.6 = (f32[3,16,32,256]{3,2,1,0:T(8,128)}, f32[3,16,32,256]{3,2,1,0:T(8,128)}, u32[]{:S(2)}, u32[]{:S(2)}) collective-permute-start(f32[3,16,32,256]{3,2,1,0:T(8,128)} %get-tuple-element.51), channel_id=1, source_target_pairs={{8,0},{16,8},{24,16},{32,24},{40,32},{48,40},{56,48},{64,56},{72,6... | collective-permute-start | bytes 4718600 | tf_op jit(solution)/shard_map/ppermute | solution.py:328
  55.1 42.1 %all-to-all-start = ((f32[128,1,128]{2,1,0:T(1,128)}), f32[128,1,128]{2,1,0:T(1,128)S(1)}, u32[]{:S(2)}, u32[]{:S(2)}) async-start(f32[128,1,128]{2,1,0:T(1,128)} %bitcast.1), calls=%async_computation | async-start | bytes 131072 | tf_op jit(solution)/shard_map/all_to_all | solution.py:339
  65.5 1.0 copy-start.3
  66.4 6.0 %copy-start.9 = (bf16[2,128,256]{2,1,0:T(8,128)(2,1)S(1)}, bf16[2,128,256]{2,1,0:T(8,128)(2,1)}, u32[]{:S(2)}) copy-start(bf16[2,128,256]{2,1,0:T(8,128)(2,1)} %copy-done.8) | copy-start | bytes 393220
  80.2 13.0 %copy-start.4 = (bf16[2,256,256]{2,1,0:T(8,128)(2,1)S(1)}, bf16[2,256,256]{2,1,0:T(8,128)(2,1)}, u32[]{:S(2)}) copy-start(bf16[2,256,256]{2,1,0:T(8,128)(2,1)} %copy-done.2) | copy-start | bytes 786436

commit v5 on v4

--- a/solution.py
+++ b/solution.py
@@ -288,18 +288,25 @@
         copy.wait()
 
 
-def z_kernel(adj_ref, up_ref, down_ref, k_ref, last_ref, done_ref, out_ref, token_ref, stage, sems):
+def z_kernel(adj_ref, up_ref, down_ref, k_ref, last_ref, done_ref, out_ref, token_ref, upper, lower, stage, sems):
     del done_ref
     token_ref[...] = jnp.zeros_like(token_ref)
+    groups = [pl.ds(8 * g, 8) for g in range(SY // 8)]
+    loads = []
+    for g, at in enumerate(groups):
+        loads.append((copy_of(up_ref.at[:, :, at], upper.at[:, :, at], sems.at[0, g]), copy_of(down_ref.at[:, :, at], lower.at[:, :, at], sems.at[1, g])))
+        for copy in loads[-1]:
+            copy.start()
     stores = []
-    for yb in range(SY // 8):
-        at = pl.ds(8 * yb, 8)
+    for g, at in enumerate(groups):
+        for copy in loads[g]:
+            copy.wait()
         field = lambda ref, c: ref[c, :, at, :].reshape(256, 256)
         stretch = jnp.zeros((256, 256), F32)
         for c in range(3):
-            stretch += field(adj_ref, c) * mix(k_ref[0], k_ref[1], side_lines(up_ref, down_ref, c, at))
+            stretch += field(adj_ref, c) * mix(k_ref[0], k_ref[1], side_lines(upper, lower, c, at))
         stage[:, at, :] = (last_ref[:, at, :].reshape(256, 256) - STEP * stretch).reshape(SZ, 8, NX)
-        stores.append(copy_of(stage.at[:, at], out_ref.at[2, :, at], sems.at[yb]))
+        stores.append(copy_of(stage.at[:, at], out_ref.at[2, :, at], sems.at[2, g]))
         stores[-1].start()
     for copy in stores:
         copy.wait()
@@ -390,13 +397,13 @@
     )
     out, token = call(
         z_kernel,
-        (adj, *[resident(v) for v in vel_sides], m_side, last, out),
+        (adj, *[in_hbm(v) for v in vel_sides], m_side, last, out),
         [shape, small],
         "z_vel",
-        in_specs=[VMEM] * 5 + [HBM],
+        in_specs=[VMEM] + [HBM] * 2 + [VMEM] * 2 + [HBM],
         out_specs=[HBM, VMEM],
         input_output_aliases={5: 0},
-        scratch_shapes=[plane, dma((4,))],
+        scratch_shapes=[side, side, plane, dma((3, 4))],
     )
     share = call(share_kernel, (grad, token), jax.ShapeDtypeStruct((2, 2), F32), "share", in_specs=[VMEM] * 2, out_specs=VMEM)
     return out, share

time: 98.4 us -> 98.7 us (level)
  no operation moved by 1% of the time
where the time goes in v5:
time: 98.7 us; the launch traced here: 98.2 us
  Pallas kernels  38.2 us (39%)
  starting transfers between devices  27.8 us (28%)
  waiting for transfers between devices  20.9 us (21%)
  local copies, waits for them, and re-layouts  10.5 us (11%)
    pallas_call x8, Pallas kernels, call(): pl.pallas_call(kernel, out_shape=outs, compiler_params=pltpu.CompilerPara...  38.2 us
    ppermute x2, waiting for transfers between devices, on_device(): lax.ppermute(upper, 'wide', up)  10.9 us
    all_to_all x1, starting transfers between devices, on_device(): lax.all_to_all(grad.reshape(n_wide * n_narrow, 1, 128), ('wide', 'narrow'...  10.4 us
    ppermute x2, waiting for transfers between devices, on_device(): lax.ppermute(lower, 'wide', down)  9.89 us
    ppermute x2, starting transfers between devices, on_device(): lax.ppermute(upper, 'wide', up)  8.96 us
    ppermute x2, starting transfers between devices, on_device(): far = lambda v: lax.ppermute(v, 'narrow', across)  5.34 us
    unnamed x36, local copies, waits for them, and re-layouts  4.15 us
    slice x1, local copies, waits for them, and re-layouts, on_device(): velocity[:, :HZ]  4.05 us
  transfers between devices with their start and end apart: 9, of which 4 were waited for; matrix products, arithmetic and copies ran while one was open for 4% of the time, Pallas kernels for 38%

profile of v5, /device:TPU:2, one launch (start us, length us, event | category | flops | bytes accessed | tf_op | source)
XLA Modules:
  0.0 98.2 jit_solution(8943556761955649257)
XLA Ops:
  0.6 0.0 copy-start
  0.6 0.0 copy-start.17
  0.7 0.0 copy-start.11
  0.7 0.0 copy-start.1
  0.7 2.3 %fusion = (f32[3,16,32,256]{3,2,1,0:T(8,128)S(1)}, f32[3,16,32,256]{3,2,1,0:T(8,128)S(1)}) fusion(f32[3,32,32,256]{3,2,1,0:T(8,128)} %adj_ref.9), kind=kLoop, calls=%fused_computation | loop fusion | bytes 6291456 | tf_op jit(solution)/shard_map/slice | solution.py:337
  3.0 0.5 copy-done
  3.5 0.0 collective-permute-start
  3.5 0.5 collective-permute-start.1
  4.0 2.0 %collective-permute-start.2 = (f32[3,32,32,256]{3,2,1,0:T(8,128)S(1)}, f32[3,32,32,256]{3,2,1,0:T(8,128)S(1)}, u32[]{:S(2)}, u32[]{:S(2)}) collective-permute-start(f32[3,32,32,256]{3,2,1,0:T(8,128)S(1)} %copy-done), channel_id=1, source_target_pairs={{1,2},{2,1},{3,4},{4,3},{5,6},{6,5},{9,10},{10,9},{11,12},{12,11},... | collective-permute-start | bytes 9437192 | tf_op jit(solution)/shard_map/ppermute | solution.py:334
  5.9 4.0 %collective-permute-start.3 = (f32[3,16,32,256]{3,2,1,0:T(8,128)S(1)}, f32[3,16,32,256]{3,2,1,0:T(8,128)S(1)}, u32[]{:S(2)}, u32[]{:S(2)}) collective-permute-start(f32[3,16,32,256]{3,2,1,0:T(8,128)S(1)} %get-tuple-element.48), channel_id=1, source_target_pairs={{0,8},{8,16},{16,24},{24,32},{32,40},{40,48},{48,56},{56,64},{64,7... | collective-permute-start | bytes 4718600 | tf_op jit(solution)/shard_map/ppermute | solution.py:335
  10.0 1.3 %collective-permute-start.4 = (f32[3,16,32,256]{3,2,1,0:T(8,128)S(1)}, f32[3,16,32,256]{3,2,1,0:T(8,128)S(1)}, u32[]{:S(2)}, u32[]{:S(2)}) collective-permute-start(f32[3,16,32,256]{3,2,1,0:T(8,128)S(1)} %get-tuple-element.49), channel_id=1, source_target_pairs={{8,0},{16,8},{24,16},{32,24},{40,32},{48,40},{56,48},{64,56},{72,6... | collective-permute-start | bytes 4718600 | tf_op jit(solution)/shard_map/ppermute | solution.py:335
  11.3 0.0 copy-done.17
  11.3 0.0 copy-done.11
  11.3 0.0 copy-done.1
  11.3 0.0 copy-start.10
  11.3 0.7 copy-done.10
  12.1 6.2 %turbines.1 = (f32[32,32,256]{2,1,0:T(8,128)S(1)}, f32[128,128]{1,0:T(8,128)}) custom-call(s32[64,96]{1,0:T(8,128)S(1)} %bitcast.2, f32[96]{0:T(128)S(1)} %copy-done.11, s32[8,128]{1,0:T(8,128)S(1)} %broadcast_in_dim.2.owner_ref, f32[3,32,32,256]{3,2,1,0:T(8,128)S(1)} %copy-done, f32[3,32,32,256]{3,2,1,0:T(8,128)} %vel_ref.7, f32[96,64,128]{2,1,0:T(8,128)S(1)} %copy-done.1), custom_call_target="tpu_custom_call" | custom-call | flops 1 | bytes 1 | tf_op jit(solution)/shard_map/turbines/pallas_call | solution.py:34
  18.2 0.0 copy-start.5
  18.2 0.0 copy-start.6
  18.3 0.0 copy-start.7
  18.3 4.0 %fusion.1 = (f32[3,16,32,256]{3,2,1,0:T(8,128)}, f32[3,16,32,256]{3,2,1,0:T(8,128)}) fusion(f32[3,32,32,256]{3,2,1,0:T(8,128)} %vel_ref.7), kind=kLoop, calls=%fused_computation.1 | loop fusion | bytes 6291456 | tf_op jit(solution)/shard_map/slice | solution.py:344
  22.3 0.0 collective-permute-done.adj2_ref
  22.3 0.0 copy-start.12
  22.3 0.0 collective-permute-done.1.vel2_ref
  22.3 0.0 copy-start.13
  22.3 0.0 copy-done.5
  22.3 0.0 copy-done.6
  22.3 0.0 copy-done.7
  22.4 1.0 prep.1
  23.3 0.0 copy-start.2
  23.3 1.2 %copy-done.2 = bf16[2,256,256]{2,1,0:T(8,128)(2,1)} copy-done((bf16[2,256,256]{2,1,0:T(8,128)(2,1)}, bf16[2,256,256]{2,1,0:T(8,128)(2,1)S(1)}, u32[]{:S(2)}) %copy-start.2) | copy-done | bytes 262168
  24.6 0.0 copy-start.8
  24.6 0.7 copy-done.8
  25.2 8.1 %xz.1 = (f32[3,32,32,256]{3,2,1,0:T(8,128)}, f32[8,128]{1,0:T(8,128)S(1)}) custom-call(f32[8,128]{1,0:T(8,128)S(1)} %get-tuple-element.41.token_ref, f32[3,32,32,256]{3,2,1,0:T(8,128)S(1)} %copy-done, f32[3,32,32,256]{3,2,1,0:T(8,128)} %vel_ref.7, f32[32,32,256]{2,1,0:T(8,128)S(1)} %get-tuple-element.42.force_ref, ...), custom_call_target="tpu_custom_call" | custom-call | flops 1 | bytes 1 | tf_op jit(solution)/shard_map/xz/pallas_call | solution.py:34
  33.3 3.4 %collective-permute-start.7 = (f32[3,32,32,256]{3,2,1,0:T(8,128)}, f32[3,32,32,256]{3,2,1,0:T(8,128)}, u32[]{:S(2)}, u32[]{:S(2)}) collective-permute-start(f32[3,32,32,256]{3,2,1,0:T(8,128)} %vel_ref.7), channel_id=1, source_target_pairs={{1,2},{2,1},{3,4},{4,3},{5,6},{6,5},{9,10},{10,9},{11,12},{12,11},... | collective-permute-start | bytes 9437192 | tf_op jit(solution)/shard_map/ppermute | solution.py:334
  36.7 7.5 %collective-permute-done.3.up_ref = f32[3,16,32,256]{3,2,1,0:T(8,128)S(1)} collective-permute-done((f32[3,16,32,256]{3,2,1,0:T(8,128)S(1)}, f32[3,16,32,256]{3,2,1,0:T(8,128)S(1)}, u32[]{:S(2)}, u32[]{:S(2)}) %collective-permute-start.3) | collective-permute-done | bytes 1572896 | tf_op jit(solution)/shard_map/ppermute | solution.py:335
  44.2 0.0 copy-start.15
  44.2 4.6 %collective-permute-done.4.down_ref = f32[3,16,32,256]{3,2,1,0:T(8,128)S(1)} collective-permute-done((f32[3,16,32,256]{3,2,1,0:T(8,128)S(1)}, f32[3,16,32,256]{3,2,1,0:T(8,128)S(1)}, u32[]{:S(2)}, u32[]{:S(2)}) %collective-permute-start.4) | collective-permute-done | bytes 1572896 | tf_op jit(solution)/shard_map/ppermute | solution.py:335
  48.8 0.0 copy-start.16
  48.8 0.0 collective-permute-done.2.far_ref
  48.8 0.0 copy-done.12
  48.8 0.0 copy-start.14
  48.8 0.0 copy-done.13
  48.8 5.0 %collective-permute-start.5 = (f32[3,16,32,256]{3,2,1,0:T(8,128)}, f32[3,16,32,256]{3,2,1,0:T(8,128)}, u32[]{:S(2)}, u32[]{:S(2)}) collective-permute-start(f32[3,16,32,256]{3,2,1,0:T(8,128)} %get-tuple-element.50), channel_id=1, source_target_pairs={{0,8},{8,16},{16,24},{24,32},{32,40},{40,48},{48,56},{56,64},{64,7... | collective-permute-start | bytes 4718600 | tf_op jit(solution)/shard_map/ppermute | solution.py:335
  53.8 0.0 copy-done.14
  53.8 1.3 %collective-permute-start.6 = (f32[3,16,32,256]{3,2,1,0:T(8,128)}, f32[3,16,32,256]{3,2,1,0:T(8,128)}, u32[]{:S(2)}, u32[]{:S(2)}) collective-permute-start(f32[3,16,32,256]{3,2,1,0:T(8,128)} %get-tuple-element.51), channel_id=1, source_target_pairs={{8,0},{16,8},{24,16},{32,24},{40,32},{48,40},{56,48},{64,56},{72,6... | collective-permute-start | bytes 4718600 | tf_op jit(solution)/shard_map/ppermute | solution.py:335
  55.1 0.0 copy-done.15
  55.1 0.0 copy-done.16
  55.1 10.4 %all-to-all-start = ((f32[128,1,128]{2,1,0:T(1,128)}), f32[128,1,128]{2,1,0:T(1,128)S(1)}, u32[]{:S(2)}, u32[]{:S(2)}) async-start(f32[128,1,128]{2,1,0:T(1,128)} %bitcast.1), calls=%async_computation | async-start | bytes 131072 | tf_op jit(solution)/shard_map/all_to_all | solution.py:346
  65.5 0.0 copy-start.3
  65.5 0.9 copy-done.3
  66.4 0.0 copy-start.9
  66.4 6.0 %halo_adj.1.old_ref = f32[3,32,32,256]{3,2,1,0:T(8,128)S(1)} custom-call(f32[3,32,32,256]{3,2,1,0:T(8,128)} %vel_ref.7, f32[3,32,32,256]{3,2,1,0:T(8,128)} %copy-done.14, f32[3,16,32,256]{3,2,1,0:T(8,128)} %copy-done.15, f32[3,16,32,256]{3,2,1,0:T(8,128)} %copy-done.16, bf16[2,256,256]{2,1,0:T(8,128)(2,1)S(1)} %get-tuple-element.61.y_ref.k_ref, ...), custom_call_target="tpu_custom_call" | custom-call | flops 1 | bytes 1 | tf_op jit(solution)/shard_map/halo_adj/pallas_call | solution.py:34
  72.4 0.0 copy-done.9
  72.5 7.7 %near.1 = (f32[3,32,32,256]{3,2,1,0:T(8,128)}, f32[2,32,32,256]{3,2,1,0:T(8,128)S(1)}, f32[8,128]{1,0:T(8,128)S(1)}) custom-call(f32[8,128]{1,0:T(8,128)S(1)} %get-tuple-element.54.before_ref, f32[3,32,32,256]{3,2,1,0:T(8,128)S(1)} %copy-done, f32[3,32,32,256]{3,2,1,0:T(8,128)} %vel_ref.7, f32[3,32,32,256]{3,2,1,0:T(8,128)} %copy-done.12, ...), custom_call_target="tpu_custom_call" | custom-call | flops 1 | bytes 1 | tf_op jit(solution)/shard_map/near/pallas_call | solution.py:34
  80.2 0.0 collective-permute-done.7.far_ref
  80.2 0.0 copy-start.4
  80.2 4.2 %far_vel.1 = (f32[3,32,32,256]{3,2,1,0:T(8,128)}, f32[32,32,256]{2,1,0:T(8,128)S(1)}) custom-call(f32[8,128]{1,0:T(8,128)S(1)} %get-tuple-element.65.token_ref, f32[3,32,32,256]{3,2,1,0:T(8,128)S(1)} %copy-done, f32[3,32,32,256]{3,2,1,0:T(8,128)} %collective-permute-done.7.far_ref, ...), custom_call_target="tpu_custom_call", output_to_operand_aliasing={{0}: (5, {})} | custom-call | flops 1 | bytes 1 | tf_op jit(solution)/shard_map/far_vel/pallas_call | solution.py:34
  84.4 3.4 %collective-permute-done.5.up_ref = f32[3,16,32,256]{3,2,1,0:T(8,128)} collective-permute-done((f32[3,16,32,256]{3,2,1,0:T(8,128)}, f32[3,16,32,256]{3,2,1,0:T(8,128)}, u32[]{:S(2)}, u32[]{:S(2)}) %collective-permute-start.5) | collective-permute-done | bytes 1572896 | tf_op jit(solution)/shard_map/ppermute | solution.py:335
  87.9 5.3 %collective-permute-done.6.down_ref = f32[3,16,32,256]{3,2,1,0:T(8,128)} collective-permute-done((f32[3,16,32,256]{3,2,1,0:T(8,128)}, f32[3,16,32,256]{3,2,1,0:T(8,128)}, u32[]{:S(2)}, u32[]{:S(2)}) %collective-permute-start.6) | collective-permute-done | bytes 1572896 | tf_op jit(solution)/shard_map/ppermute | solution.py:335
  93.2 0.0 copy-done.4
  93.2 4.3 %z_vel.1 = (f32[3,32,32,256]{3,2,1,0:T(8,128)}, f32[8,128]{1,0:T(8,128)S(1)}) custom-call(f32[3,32,32,256]{3,2,1,0:T(8,128)S(1)} %copy-done, f32[3,16,32,256]{3,2,1,0:T(8,128)} %collective-permute-done.5.up_ref, f32[3,16,32,256]{3,2,1,0:T(8,128)} %collective-permute-done.6.down_ref, ...), custom_call_target="tpu_custom_call", output_to_operand_aliasing={{0}: (5, {})} | custom-call | flops 1 | bytes 1 | tf_op jit(solution)/shard_map/z_vel/pallas_call | solution.py:34
  97.5 0.0 all-to-all-done.terms_ref
  97.5 0.7 share.1
  (2 shorter events, 0.0 us)
Async XLA Ops:
  0.6 2.8 %copy-start = (f32[3,32,32,256]{3,2,1,0:T(8,128)S(1)}, f32[3,32,32,256]{3,2,1,0:T(8,128)}, u32[]{:S(2)}) copy-start(f32[3,32,32,256]{3,2,1,0:T(8,128)} %adj_ref.9) | copy-start | bytes 9437188
  0.6 10.6 %copy-start.17 = (s32[96]{0:T(128)S(1)}, s32[96]{0:T(128)}, u32[]{:S(2)}) copy-start(s32[96]{0:T(128)} %param.15) | copy-start | bytes 1156
  0.7 10.6 %copy-start.11 = (f32[96]{0:T(128)S(1)}, f32[96]{0:T(128)}, u32[]{:S(2)}) copy-start(f32[96]{0:T(128)} %thrust_ref.1) | copy-start | bytes 1156
  0.7 10.6 %copy-start.1 = (f32[96,64,128]{2,1,0:T(8,128)S(1)}, f32[96,64,128]{2,1,0:T(8,128)}, u32[]{:S(2)}) copy-start(f32[96,64,128]{2,1,0:T(8,128)} %weight_ref.1) | copy-start | bytes 9437188
  3.5 18.8 %collective-permute-start = (f32[3,32,32,256]{3,2,1,0:T(8,128)S(1)}, f32[3,32,32,256]{3,2,1,0:T(8,128)S(1)}, u32[]{:S(2)}, u32[]{:S(2)}) collective-permute-start(f32[3,32,32,256]{3,2,1,0:T(8,128)S(1)} %copy-done), channel_id=1, source_target_pairs={{0,1},{1,0},{2,3},{3,2},{4,5},{5,4},{6,7},{7,6},{8,9},{9,8},{10,11... | collective-permute-start | bytes 9437192 | tf_op jit(solution)/shard_map/ppermute | solution.py:340
  3.5 18.8 %collective-permute-start.1 = (f32[3,32,32,256]{3,2,1,0:T(8,128)}, f32[3,32,32,256]{3,2,1,0:T(8,128)S(1)}, u32[]{:S(2)}, u32[]{:S(2)}) collective-permute-start(f32[3,32,32,256]{3,2,1,0:T(8,128)} %vel_ref.7), channel_id=1, source_target_pairs={{0,1},{1,0},{2,3},{3,2},{4,5},{5,4},{6,7},{7,6},{8,9},{9,8},{10,11... | collective-permute-start | bytes 9437192 | tf_op jit(solution)/shard_map/ppermute | solution.py:340
  4.0 44.8 %collective-permute-start.2 = (f32[3,32,32,256]{3,2,1,0:T(8,128)S(1)}, f32[3,32,32,256]{3,2,1,0:T(8,128)S(1)}, u32[]{:S(2)}, u32[]{:S(2)}) collective-permute-start(f32[3,32,32,256]{3,2,1,0:T(8,128)S(1)} %copy-done), channel_id=1, source_target_pairs={{1,2},{2,1},{3,4},{4,3},{5,6},{6,5},{9,10},{10,9},{11,12},{12,11},... | collective-permute-start | bytes 9437192 | tf_op jit(solution)/shard_map/ppermute | solution.py:334
  5.9 38.3 %collective-permute-start.3 = (f32[3,16,32,256]{3,2,1,0:T(8,128)S(1)}, f32[3,16,32,256]{3,2,1,0:T(8,128)S(1)}, u32[]{:S(2)}, u32[]{:S(2)}) collective-permute-start(f32[3,16,32,256]{3,2,1,0:T(8,128)S(1)} %get-tuple-element.48), channel_id=1, source_target_pairs={{0,8},{8,16},{16,24},{24,32},{32,40},{40,48},{48,56},{56,64},{64,7... | collective-permute-start | bytes 4718600 | tf_op jit(solution)/shard_map/ppermute | solution.py:335
  10.0 38.9 %collective-permute-start.4 = (f32[3,16,32,256]{3,2,1,0:T(8,128)S(1)}, f32[3,16,32,256]{3,2,1,0:T(8,128)S(1)}, u32[]{:S(2)}, u32[]{:S(2)}) collective-permute-start(f32[3,16,32,256]{3,2,1,0:T(8,128)S(1)} %get-tuple-element.49), channel_id=1, source_target_pairs={{8,0},{16,8},{24,16},{32,24},{40,32},{48,40},{56,48},{64,56},{72,6... | collective-permute-start | bytes 4718600 | tf_op jit(solution)/shard_map/ppermute | solution.py:335
  11.3 0.8 copy-start.10
  18.2 4.1 %copy-start.5 = (f32[512,512]{1,0:T(8,128)S(1)}, f32[512,512]{1,0:T(8,128)}, u32[]{:S(2)}) copy-start(f32[512,512]{1,0:T(8,128)} %dz_ref.1) | copy-start | bytes 3145732
  18.2 4.1 %copy-start.6 = (f32[256,256]{1,0:T(8,128)S(1)}, f32[256,256]{1,0:T(8,128)}, u32[]{:S(2)}) copy-start(f32[256,256]{1,0:T(8,128)} %dx_ref.1) | copy-start | bytes 786436
  18.3 4.1 %copy-start.7 = (f32[256,256]{1,0:T(8,128)S(1)}, f32[256,256]{1,0:T(8,128)}, u32[]{:S(2)}) copy-start(f32[256,256]{1,0:T(8,128)} %dy_ref) | copy-start | bytes 786436
  22.3 26.5 %copy-start.12 = (f32[3,32,32,256]{3,2,1,0:T(8,128)}, f32[3,32,32,256]{3,2,1,0:T(8,128)S(1)}, u32[]{:S(2)}) copy-start(f32[3,32,32,256]{3,2,1,0:T(8,128)S(1)} %collective-permute-done.adj2_ref) | copy-start | bytes 9437188
  22.3 26.5 %copy-start.13 = (f32[3,32,32,256]{3,2,1,0:T(8,128)}, f32[3,32,32,256]{3,2,1,0:T(8,128)S(1)}, u32[]{:S(2)}) copy-start(f32[3,32,32,256]{3,2,1,0:T(8,128)S(1)} %collective-permute-done.1.vel2_ref) | copy-start | bytes 9437188
  23.3 1.2 %copy-start.2 = (bf16[2,256,256]{2,1,0:T(8,128)(2,1)}, bf16[2,256,256]{2,1,0:T(8,128)(2,1)S(1)}, u32[]{:S(2)}) copy-start(bf16[2,256,256]{2,1,0:T(8,128)(2,1)S(1)} %get-tuple-element.52.z_ref.k_ref) | copy-start | bytes 786436
  24.6 0.7 copy-start.8
  33.3 46.9 %collective-permute-start.7 = (f32[3,32,32,256]{3,2,1,0:T(8,128)}, f32[3,32,32,256]{3,2,1,0:T(8,128)}, u32[]{:S(2)}, u32[]{:S(2)}) collective-permute-start(f32[3,32,32,256]{3,2,1,0:T(8,128)} %vel_ref.7), channel_id=1, source_target_pairs={{1,2},{2,1},{3,4},{4,3},{5,6},{6,5},{9,10},{10,9},{11,12},{12,11},... | collective-permute-start | bytes 9437192 | tf_op jit(solution)/shard_map/ppermute | solution.py:334
  44.2 10.9 %copy-start.15 = (f32[3,16,32,256]{3,2,1,0:T(8,128)}, f32[3,16,32,256]{3,2,1,0:T(8,128)S(1)}, u32[]{:S(2)}) copy-start(f32[3,16,32,256]{3,2,1,0:T(8,128)S(1)} %collective-permute-done.3.up_ref) | copy-start | bytes 4718596
  48.8 6.3 %copy-start.16 = (f32[3,16,32,256]{3,2,1,0:T(8,128)}, f32[3,16,32,256]{3,2,1,0:T(8,128)S(1)}, u32[]{:S(2)}) copy-start(f32[3,16,32,256]{3,2,1,0:T(8,128)S(1)} %collective-permute-done.4.down_ref) | copy-start | bytes 4718596
  48.8 5.0 %copy-start.14 = (f32[3,32,32,256]{3,2,1,0:T(8,128)}, f32[3,32,32,256]{3,2,1,0:T(8,128)S(1)}, u32[]{:S(2)}) copy-start(f32[3,32,32,256]{3,2,1,0:T(8,128)S(1)} %collective-permute-done.2.far_ref) | copy-start | bytes 9437188
  48.8 39.0 %collective-permute-start.5 = (f32[3,16,32,256]{3,2,1,0:T(8,128)}, f32[3,16,32,256]{3,2,1,0:T(8,128)}, u32[]{:S(2)}, u32[]{:S(2)}) collective-permute-start(f32[3,16,32,256]{3,2,1,0:T(8,128)} %get-tuple-element.50), channel_id=1, source_target_pairs={{0,8},{8,16},{16,24},{24,32},{32,40},{40,48},{48,56},{56,64},{64,7... | collective-permute-start | bytes 4718600 | tf_op jit(solution)/shard_map/ppermute | solution.py:335
  53.8 39.3 %collective-permute-start.6 = (f32[3,16,32,256]{3,2,1,0:T(8,128)}, f32[3,16,32,256]{3,2,1,0:T(8,128)}, u32[]{:S(2)}, u32[]{:S(2)}) collective-permute-start(f32[3,16,32,256]{3,2,1,0:T(8,128)} %get-tuple-element.51), channel_id=1, source_target_pairs={{8,0},{16,8},{24,16},{32,24},{40,32},{48,40},{56,48},{64,56},{72,6... | collective-permute-start | bytes 4718600 | tf_op jit(solution)/shard_map/ppermute | solution.py:335
  55.1 42.4 %all-to-all-start = ((f32[128,1,128]{2,1,0:T(1,128)}), f32[128,1,128]{2,1,0:T(1,128)S(1)}, u32[]{:S(2)}, u32[]{:S(2)}) async-start(f32[128,1,128]{2,1,0:T(1,128)} %bitcast.1), calls=%async_computation | async-start | bytes 131072 | tf_op jit(solution)/shard_map/all_to_all | solution.py:346
  65.5 1.0 copy-start.3
  66.4 6.0 %copy-start.9 = (bf16[2,128,256]{2,1,0:T(8,128)(2,1)S(1)}, bf16[2,128,256]{2,1,0:T(8,128)(2,1)}, u32[]{:S(2)}) copy-start(bf16[2,128,256]{2,1,0:T(8,128)(2,1)} %copy-done.8) | copy-start | bytes 393220
  80.2 13.0 %copy-start.4 = (bf16[2,256,256]{2,1,0:T(8,128)(2,1)S(1)}, bf16[2,256,256]{2,1,0:T(8,128)(2,1)}, u32[]{:S(2)}) copy-start(bf16[2,256,256]{2,1,0:T(8,128)(2,1)} %copy-done.2) | copy-start | bytes 786436
